TPU v7x, 128 devices: a whole 4x4x4 slice. The times are simulated.
128 devices in a mesh: grp: 4 (over x), dev: 32 (over y, z, core).
Axes of the slice: x: 4, y: 4, z: 4, core: 2. Of those that a mesh axis runs over, the one named last changes fastest.
Arguments:
- canvas: bfloat16 [256, 4096, 256], P('grp', 'dev'), may hold values from -6 to 6
- conv_weight: bfloat16 [2304, 256], replicated, may hold values from -0.125 to 0.125
- conv_bias: float32 [256], replicated, may hold values from -3 to 3
- score_weight: float32 [256], replicated, may hold values from -0.75 to 0.75
- tile_tokens: bfloat16 [4096, 24, 3200], P(('grp', 'dev')), may hold values from -6 to 6
- tile_cell: int32 [4, 1024], P('grp', 'dev'), may hold values from 0 to 8191
- tile_count: int32 [4, 32], P('grp'), may hold values from 1 to 32, 256 in all within a row
- holder_order: int32 [4, 32], P('grp'), may hold values from 0 to 31, each once within a row
- tile_image: int32 [4, 256], P('grp'), may hold values from 0 to 127, never falling along the last dimension, each value on 1 to 9 neighbouring positions
- ln_gain: float32 [3200], replicated, may hold values from 0.25 to 1.75
- qkv_weight: bfloat16 [3200, 4992], P(('grp', 'dev')), may hold values from -2 to 2
Outputs:
- score_map: float32 [256, 4096], P('grp', 'dev')
- attended: bfloat16 [24576, 1664], P(('grp', 'dev'))
Inputs may be any that keep to these rules, and one draw needn't show every extreme that they name: `tile_count`: the counts of one group add up to 256; in each group one device holds exactly 32. `tile_image`: ids never fall along a group's held tiles; each image has 1 to 9 tiles and one has exactly 9.
All inputs are finite; a program needn't handle non-finite values.
Results may differ from a plain program's by a relative error of at most 0.012.
Values may be sent and summed in bfloat16 or wider, within the bound.
No kernel may reach another device: no remote copies, remote signals or barrier semaphores. Data moves between devices by JAX's collectives and lax.ppermute only.
A program may use at most 192 MiB of HBM per device.

v0:
```python
import math

import jax
import jax.numpy as jnp
from jax import lax
from jax.sharding import PartitionSpec as P

HD = 128
HEADS = 13
MT = 8


def with_halo(value, sides, width):
    for axis, dim in sides:
        size, length = (lax.axis_size(axis), value.shape[dim])
        up = [(i, (i + 1) % size) for i in range(size - 1)]
        down = [(j, i) for i, j in up]
        last = lax.slice_in_dim(value, length - width, length, axis=dim)
        initial = lax.slice_in_dim(value, 0, width, axis=dim)
        before = lax.ppermute(last, axis, up)
        after = lax.ppermute(initial, axis, down)
        value = jnp.concatenate([before, value, after], axis=dim)
    return value


def layer_norm(rows, gain):
    values = rows.astype(jnp.float32)
    center = jnp.mean(values, axis=1, keepdims=True)
    spread = jnp.mean(jnp.square(values - center), axis=1, keepdims=True)
    return ((values - center) * lax.rsqrt(spread + 1e-06) * gain).astype(jnp.bfloat16)


def conv_scores(padded, conv_weight, conv_bias, score_weight, height, breadth):
    channels = padded.shape[2]
    summed = jnp.zeros((height * breadth, conv_weight.shape[1]), jnp.float32)
    for row_off in range(3):
        for col_off in range(3):
            window = padded[row_off : row_off + height, col_off : col_off + breadth].reshape(
                height * breadth, channels
            )
            offset = (row_off * 3 + col_off) * channels
            summed = summed + jnp.dot(
                window, conv_weight[offset : offset + channels], preferred_element_type=jnp.float32
            )
    hidden = jax.nn.gelu(summed + conv_bias)
    return jnp.dot(hidden, score_weight, precision=lax.Precision.HIGHEST)


def attend(queries, keys, values, query_ids, key_ids):
    rows = queries.shape[0]
    query_heads = queries.reshape(rows, HEADS, HD)
    key_heads = keys.reshape(keys.shape[0], HEADS, HD)
    value_heads = values.reshape(values.shape[0], HEADS, HD)
    logits = jnp.einsum(
        "qhd,khd->hqk", query_heads, key_heads, preferred_element_type=jnp.float32
    ) * (1.0 / math.sqrt(HD))
    same = query_ids[:, None] == key_ids[None, :]
    logits = jnp.where(same[None], logits, -1e30)
    peak = jnp.max(logits, axis=2, keepdims=True)
    weights = jnp.exp(logits - peak)
    probs = (weights / jnp.sum(weights, axis=2, keepdims=True)).astype(jnp.bfloat16)
    result = jnp.einsum("hqk,khd->qhd", probs, value_heads, preferred_element_type=jnp.float32)
    return result.astype(jnp.bfloat16).reshape(rows, HEADS * HD)


def key_scale(sharp, col_count, head_width):
    columns = jnp.arange(col_count, dtype=jnp.int32)
    is_key = (columns >= head_width) & (columns < 2 * head_width)
    return jnp.where(is_key[None, :], sharp[:, None], 1.0)


def shards(
    canvas,
    conv_weight,
    conv_bias,
    score_weight,
    tile_tokens,
    tile_cell,
    tile_count,
    holder_order,
    tile_image,
    ln_gain,
    qkv_weight,
):
    height, breadth = (canvas.shape[0], canvas.shape[1])
    padded = with_halo(canvas, (("grp", 0), ("dev", 1)), 1)
    score_flat = conv_scores(padded, conv_weight, conv_bias, score_weight, height, breadth)
    score_map = score_flat.reshape(height, breadth)
    holders = lax.axis_size("dev")
    own_index = lax.axis_index("dev")
    slot_count = tile_tokens.shape[0]
    tile_len = tile_tokens.shape[1]
    model_width = tile_tokens.shape[2]
    per_peer = max(1, slot_count // holders)
    counts = tile_count[0]
    order = holder_order[0]
    prefix = jnp.cumsum(counts) - counts
    slot_range = jnp.arange(slot_count, dtype=jnp.int32)
    round_range = jnp.arange(per_peer, dtype=jnp.int32)
    holder_range = jnp.arange(holders, dtype=jnp.int32)
    position = jnp.take(prefix, own_index) + slot_range
    is_live = slot_range < jnp.take(counts, own_index)
    target = jnp.take(order, position % holders)
    same_holder = target[None, None, :] == holder_range[:, None, None]
    same_round = (slot_range // holders)[None, None, :] == round_range[None, :, None]
    send_mask = (same_holder & same_round & is_live[None, None, :]).astype(jnp.bfloat16)
    send_tiles = jnp.einsum(
        "kcs,std->kctd", send_mask, tile_tokens, preferred_element_type=jnp.float32
    ).astype(jnp.bfloat16)
    tile_score = jnp.take(score_flat, tile_cell[0]).astype(jnp.bfloat16)
    send_score = jnp.einsum(
        "kcs,s->kc", send_mask, tile_score, preferred_element_type=jnp.float32
    ).astype(jnp.bfloat16)
    recv_tiles, recv_score = (
        lax.all_to_all(send_tiles, "dev", split_axis=0, concat_axis=0, tiled=True),
        lax.all_to_all(send_score, "dev", split_axis=0, concat_axis=0, tiled=True),
    )
    place = jnp.sum(jnp.where(order == own_index, holder_range, 0))
    wanted = jnp.arange(MT, dtype=jnp.int32) * holders + place
    from_source = (prefix[None, :] <= wanted[:, None]) & (
        wanted[:, None] < (prefix + counts)[None, :]
    )
    round_of = (wanted[:, None] - prefix[None, :]) // holders
    take_mask = (
        from_source[:, :, None] & (round_of[:, :, None] == round_range[None, None, :])
    ).astype(jnp.bfloat16)
    held = jnp.einsum(
        "mjc,jctd->mtd", take_mask, recv_tiles, preferred_element_type=jnp.float32
    ).astype(jnp.bfloat16)
    held_rows = MT * tile_len
    held = held.reshape(held_rows, model_width)
    held_score = jnp.einsum(
        "mjc,jc->m", take_mask, recv_score, preferred_element_type=jnp.float32
    ).astype(jnp.bfloat16)
    sharpness = jnp.repeat(0.5 + jax.nn.softplus(held_score.astype(jnp.float32)), tile_len)
    normed = layer_norm(held, ln_gain)
    width_all = qkv_weight.shape[1]
    head_width = width_all // 3
    mixed = jnp.dot(
        normed,
        lax.all_gather(qkv_weight, ("grp", "dev"), axis=0, tiled=True),
        preferred_element_type=jnp.float32,
    )
    projected = (mixed * key_scale(sharpness, width_all, head_width)).astype(jnp.bfloat16)
    queries = projected[:, :head_width]
    near = with_halo(projected[:, head_width:], (("dev", 0),), held_rows)
    all_ids = tile_image[0]
    tile_total = all_ids.shape[0]
    near_tiles = own_index * MT - MT + jnp.arange(3 * MT, dtype=jnp.int32)
    inside = (near_tiles >= 0) & (near_tiles < tile_total)
    near_ids = jnp.where(inside, jnp.take(all_ids, jnp.clip(near_tiles, 0, tile_total - 1)), -1)
    key_ids = jnp.repeat(near_ids, tile_len)
    own_ids = jnp.repeat(
        jnp.take(all_ids, own_index * MT + jnp.arange(MT, dtype=jnp.int32)), tile_len
    )
    attended = attend(queries, near[:, :head_width], near[:, head_width:], own_ids, key_ids)
    return (score_map, attended)


def solution(mesh):
    placed = (
        P("grp", "dev", None),
        P(),
        P(),
        P(),
        P(("grp", "dev"), None, None),
        P("grp", "dev"),
        P("grp", None),
        P("grp", None),
        P("grp", None),
        P(),
        P(("grp", "dev"), None),
    )
    return jax.shard_map(
        shards,
        mesh=mesh,
        in_specs=placed,
        out_specs=(P("grp", "dev"), P(("grp", "dev"), None)),
        check_vma=False,
    )
```

profile of v0, /device:TPU:97, one launch (start us, length us, event | category | flops | bytes accessed | tf_op | source)
XLA Modules:
  0.0 299.1 jit_solution(9895497213868560094)
XLA Ops:
  7.2 0.7 all-gather.3.cloned.1.call-update
  7.9 0.9 fusion.100
  8.8 3.1 %collective-permute-start = (bf16[1,128,256]{2,1,0:T(8,128)(2,1)S(1)}, bf16[1,128,256]{2,1,0:T(8,128)(2,1)S(1)}, u32[]{:S(2)}, u32[]{:S(2)}) collective-permute-start(bf16[1,128,256]{2,1,0:T(8,128)(2,1)S(1)} %get-tuple-element.39), channel_id=1, source_target_pairs={{0,32},{32,64},{64,96},{1,33},{33,65},{65,97},{2,34},{34,66},{66,9... | collective-permute-start | bytes 196616 | tf_op jit(solution)/shard_map/ppermute | solution.py:20
  11.9 1.3 collective-permute-start.1
  13.2 1.3 constant_dynamic-slice_fusion
  14.5 0.7 copy.56
  15.3 0.1 reduce.2
  15.4 0.7 bitcast_subtract_fusion.2
  16.1 0.6 dynamic-slice.4
  18.0 0.7 fusion.79
  18.7 1.4 gather_fusion
  20.1 6.3 %fusion.12 = bf16[32,1,24,3200]{3,0,2,1:T(8,128)(2,1)} fusion(bf16[32,24,3200]{2,1,0:T(8,128)(2,1)} %param.15, s32[32]{0:T(128)S(1)} %and_select_fusion.6, pred[32]{0:T(512)(128)(4,1)S(1)} %get-tuple-element.51, pred[32]{0:T(512)(128)(4,1)S(1)} %get-tuple-element.50), kind=kOutput, calls=%fused_computation.32 | convolution fusion | flops 159747072 | bytes 9830592 | tf_op jit(solution)/shard_map/kcs,std->kctd/dot_general | solution.py:107
  26.4 1.8 pad_maximum_fusion.3
  28.2 0.1 fusion.99
  28.3 2.6 collective-permute-start.2
  31.0 2.2 collective-permute-start.3
  33.2 2.2 fusion.47
  35.4 2.2 fusion.40
  37.6 1.1 collective-permute-done.3
  38.7 12.9 %pad_maximum_fusion.2 = (bf16[64,128,256]{2,1,0:T(8,128)(2,1)}, bf16[64,128,256]{2,1,0:T(8,128)(2,1)}, bf16[64,128,256]{2,1,0:T(8,128)(2,1)}, bf16[64,128,256]{2...) fusion(bf16[66,128,256]{2,1,0:T(8,128)(2,1)S(1)} %constant_dynamic-update-slice_fusion, ...), kind=kLoop, calls=%fused_computation.45 | loop fusion | flops 50331648 | bytes 29558784 | tf_op jit(solution)/shard_map/concatenate | solution.py:22
  51.6 4.5 %fusion.38 = f32[8192,256]{1,0:T(8,128)} fusion(bf16[8192,256]{1,0:T(8,128)(2,1)S(1)} %bitcast.141, bf16[2304,256]{1,0:T(8,128)(2,1)S(1)} %copy-done.9), kind=kOutput, calls=%fused_computation.71 | convolution fusion | flops 1073741824 | bytes 12713984 | tf_op jit(solution)/shard_map/dot_general | solution.py:42
  56.1 1.3 convolution_add_fusion.5
  57.4 3.7 %convolution_add_fusion.4 = f32[8192,256]{1,0:T(8,128)S(1)} fusion(f32[8192,256]{1,0:T(8,128)S(1)} %convolution_add_fusion.5, bf16[8192,256]{1,0:T(8,128)(2,1)} %bitcast.137, bf16[2304,256]{1,0:T(8,128)(2,1)S(1)} %copy-done.9), kind=kOutput, calls=%fused_computation.11 | convolution fusion | flops 1075838976 | bytes 21102592 | tf_op jit(solution)/shard_map/dot_general | solution.py:42
  61.1 3.7 %convolution_add_fusion.3 = f32[8192,256]{1,0:T(8,128)S(1)} fusion(f32[8192,256]{1,0:T(8,128)S(1)} %convolution_add_fusion.4, bf16[8192,256]{1,0:T(8,128)(2,1)} %bitcast.136, bf16[2304,256]{1,0:T(8,128)(2,1)S(1)} %copy-done.9), kind=kOutput, calls=%fused_computation.10 | convolution fusion | flops 1075838976 | bytes 21102592 | tf_op jit(solution)/shard_map/dot_general | solution.py:42
  64.8 1.3 convolution_add_fusion.2
  66.1 3.6 %convolution_add_fusion.1 = f32[8192,256]{1,0:T(8,128)S(1)} fusion(f32[8192,256]{1,0:T(8,128)S(1)} %convolution_add_fusion.2, bf16[8192,256]{1,0:T(8,128)(2,1)} %bitcast.135, bf16[2304,256]{1,0:T(8,128)(2,1)S(1)} %copy-done.9), kind=kOutput, calls=%fused_computation.8 | convolution fusion | flops 1075838976 | bytes 21102592 | tf_op jit(solution)/shard_map/dot_general | solution.py:42
  69.7 11.1 %fusion.10 = f32[8192,256]{1,0:T(8,128)} fusion(f32[8192,256]{1,0:T(8,128)} %fusion.38, f32[8192,256]{1,0:T(8,128)S(1)} %fusion.40, f32[8192,256]{1,0:T(8,128)S(1)} %convolution_add_fusion.1, bf16[8192,256]{1,0:T(8,128)(2,1)} %bitcast.142, f32[256]{0:T(256)S(1)} %copy-done.11, bf16[2304,256]{1,0:T(8,128)(2,1)} %param.12), kind=kOutput, calls=%fused_computation.21 | convolution fusion | flops 1098907648 | bytes 37880832 | tf_op jit(solution)/shard_map/dot_general | solution.py:42
  80.9 11.1 %fusion.104 = f32[1,8192]{1,0:T(1,128)S(1)} fusion(f32[8192,256]{1,0:T(8,128)} %fusion.10, f32[256,1]{0,1:T(1,128)S(1)} %bitcast.130), kind=kOutput, calls=%fused_computation.182 | convolution fusion | flops 25165824 | bytes 8422400 | tf_op jit(solution)/shard_map/dot_general | solution.py:46
  92.0 0.7 gather_fusion.1
  92.7 0.1 fusion.32
  92.9 0.7 copy.64
  93.6 7.1 %all-to-all-start.1 = ((bf16[32,1,1]{2,1,0:T(2,128)(2,1)}), bf16[32,1,1]{2,1,0:T(2,128)(2,1)S(1)}, u32[]{:S(2)}, u32[]{:S(2)}) async-start(bf16[32,1,1]{2,1,0:T(2,128)(2,1)} %copy.64), calls=%async_computation.1 | async-start | bytes 32768 | tf_op jit(solution)/shard_map/all_to_all | solution.py:116
  100.7 6.3 %copy.58 = bf16[32,1,24,3200]{3,2,1,0:T(8,128)(2,1)} copy(bf16[32,1,24,3200]{3,0,2,1:T(8,128)(2,1)} %fusion.12) | data formatting | bytes 9830400 | tf_op jit(solution)/shard_map/convert_element_type | solution.py:109
  107.0 7.9 %all-to-all-start = ((bf16[32,1,24,3200]{3,2,1,0:T(8,128)(2,1)}), bf16[32,1,24,3200]{3,2,1,0:T(8,128)(2,1)}, u32[]{:S(2)}, u32[]{:S(2)}) async-start(bf16[32,1,24,3200]{3,2,1,0:T(8,128)(2,1)} %copy.58), calls=%async_computation | async-start | bytes 9830400 | tf_op jit(solution)/shard_map/all_to_all | solution.py:115
  115.0 0.6 fusion.75
  115.6 0.6 multiply_add_fusion
  116.3 0.3 reduce.4
  116.6 0.2 fusion.80
  116.9 0.1 broadcast_in_dim.101
  117.0 66.4 %all-to-all-done = bf16[32,1,24,3200]{3,2,1,0:T(8,128)(2,1)} async-done(((bf16[32,1,24,3200]{3,2,1,0:T(8,128)(2,1)}), bf16[32,1,24,3200]{3,2,1,0:T(8,128)(2,1)}, u32[]{:S(2)}, u32[]{:S(2)}) %all-to-all-start) | async-done | bytes 4915232 | tf_op jit(solution)/shard_map/all_to_all | solution.py:115
  183.4 3.5 %fusion.102 = (f32[8,24]{0,1:T(8,128)S(1)}, f32[8,24,3200]{2,0,1:T(8,128)S(1)}) fusion(bf16[32,1,24,3200]{3,2,1,0:T(8,128)(2,1)} %all-to-all-done, s32[32]{0:T(128)S(1)} %reduce.2, s32[8]{0:T(128)S(1)} %multiply_add_fusion, s32[32]{0:T(128)S(1)} %fusion.83), kind=kOutput, calls=%fused_computation.180 | convolution fusion | flops 41169984 | bytes 7373856 | tf_op jit(solution)/shard_map/mjc,jctd->mtd/dot_general | solution.py:127
  187.1 1.9 copy.60
  189.0 0.4 multiply_reduce_fusion
  189.6 2.1 fusion.28
  191.7 31.8 %reshape.836 = bf16[3200,4992]{1,0:T(8,128)(2,1)} reshape(bf16[128,25,4992]{2,1,0:T(8,128)(2,1)} %all-gather.3.cloned.1.call-done) | data formatting | bytes 63897600
  223.5 13.7 %fusion.11 = bf16[192,4992]{1,0:T(8,128)(2,1)S(1)} fusion(bf16[192,3200]{1,0:T(8,128)(2,1)S(1)} %fusion.28, bf16[3200,4992]{1,0:T(8,128)(2,1)} %reshape.836, f32[192]{0:T(256)S(1)} %broadcast_in_dim.101, pred[4992]{0:T(1024)(128)(4,1)S(1)} %fusion.50), kind=kOutput, calls=%fused_computation.31 | convolution fusion | flops 6137044992 | bytes 35100288 | tf_op jit(solution)/shard_map/dot_general | solution.py:139
  237.2 0.1 slice.136
  237.3 1.2 copy-done.8
  238.5 7.1 %collective-permute-start.4 = (bf16[192,3328]{1,0:T(8,128)(2,1)S(1)}, bf16[192,3328]{1,0:T(8,128)(2,1)S(1)}, u32[]{:S(2)}, u32[]{:S(2)}) collective-permute-start(bf16[192,3328]{1,0:T(8,128)(2,1)S(1)} %slice.136), channel_id=1, source_target_pairs={{0,1},{1,2},{2,3},{3,4},{4,5},{5,6},{6,7},{7,8},{8,9},{9,10},{10,1... | collective-permute-start | bytes 3833864 | tf_op jit(solution)/shard_map/ppermute | solution.py:20
  245.6 1.9 collective-permute-start.5
  247.5 0.7 gather_fusion.3
  248.3 0.1 eq.113
  248.4 0.6 gather_fusion.2
  249.2 0.1 broadcast_compare_fusion
  249.4 10.3 %collective-permute-done.4 = bf16[192,3328]{1,0:T(8,128)(2,1)S(1)} collective-permute-done((bf16[192,3328]{1,0:T(8,128)(2,1)S(1)}, bf16[192,3328]{1,0:T(8,128)(2,1)S(1)}, u32[]{:S(2)}, u32[]{:S(2)}) %collective-permute-start.4) | collective-permute-done | bytes 1277984 | tf_op jit(solution)/shard_map/ppermute | solution.py:20
  259.7 6.6 %collective-permute-done.5 = bf16[192,3328]{1,0:T(8,128)(2,1)} collective-permute-done((bf16[192,3328]{1,0:T(8,128)(2,1)S(1)}, bf16[192,3328]{1,0:T(8,128)(2,1)}, u32[]{:S(2)}, u32[]{:S(2)}) %collective-permute-start.5) | collective-permute-done | bytes 1277984 | tf_op jit(solution)/shard_map/ppermute | solution.py:21
  266.3 1.7 pad_maximum_fusion.4
  268.0 2.2 fusion.101
  270.2 3.4 %copy.66 = bf16[576,1664]{0,1:T(8,128)(2,1)S(1)} copy(bf16[576,1664]{1,0:T(8,128)(2,1)} %get-tuple-element.40) | data formatting | bytes 3833856 | tf_op jit(solution)/shard_map/slice | solution.py:156
  273.6 4.8 %fusion.35 = f32[13,192,576]{2,1,0:T(8,128)} fusion(bf16[576,13,128]{0,2,1:T(8,128)(2,1)S(1)} %bitcast.145, bf16[192,4992]{1,0:T(8,128)(2,1)} %copy-done.8), kind=kOutput, calls=%fused_computation.66 | convolution fusion | flops 368050176 | bytes 8306688 | tf_op jit(solution)/shard_map/qhd,khd->hqk/dot_general | solution.py:54
  278.3 3.4 %copy.65 = bf16[576,1664]{0,1:T(8,128)(2,1)S(1)} copy(bf16[576,1664]{1,0:T(8,128)(2,1)} %get-tuple-element.41) | data formatting | bytes 3833856 | tf_op jit(solution)/shard_map/slice | solution.py:156
  281.7 8.0 %fusion.103 = (f32[13,192]{1,0:T(8,128)S(1)}, f32[13,192,576]{2,1,0:T(8,128)S(1)}) fusion(f32[13,192,576]{2,1,0:T(8,128)} %fusion.35, pred[192,576]{1,0:T(8,128)(4,1)S(1)} %broadcast_compare_fusion), kind=kOutput, calls=%fused_computation.181 | output fusion | flops 8626751 | bytes 11622144 | tf_op jit(solution)/shard_map/sub | solution.py:60
  289.7 1.3 fusion.30
  291.0 0.9 copy.88
  (58 shorter events, 1.0 us)
Async XLA Ops:
  7.2 73.7 %copy-start = (f32[256]{0:T(256)S(1)}, f32[256]{0:T(256)}, u32[]{:S(2)}) copy-start(f32[256]{0:T(256)} %param.14) | copy-start | bytes 3076
  7.2 184.5 %all-gather.3.cloned.1.call-start = ((), (), s32[]{:S(2)}) async-start(), calls=%async_computation.2 | async-start | bytes 41213952 | tf_op jit(solution)/shard_map/all_gather | solution.py:141
  8.8 17.6 %collective-permute-start = (bf16[1,128,256]{2,1,0:T(8,128)(2,1)S(1)}, bf16[1,128,256]{2,1,0:T(8,128)(2,1)S(1)}, u32[]{:S(2)}, u32[]{:S(2)}) collective-permute-start(bf16[1,128,256]{2,1,0:T(8,128)(2,1)S(1)} %get-tuple-element.39), channel_id=1, source_target_pairs={{0,32},{32,64},{64,96},{1,33},{33,65},{65,97},{2,34},{34,66},{66,9... | collective-permute-start | bytes 196616 | tf_op jit(solution)/shard_map/ppermute | solution.py:20
  11.9 14.5 %collective-permute-start.1 = (bf16[1,128,256]{2,1,0:T(8,128)(2,1)S(1)}, bf16[1,128,256]{2,1,0:T(8,128)(2,1)S(1)}, u32[]{:S(2)}, u32[]{:S(2)}) collective-permute-start(bf16[1,128,256]{2,1,0:T(8,128)(2,1)S(1)} %get-tuple-element.38), channel_id=1, source_target_pairs={{32,0},{64,32},{96,64},{33,1},{65,33},{97,65},{34,2},{66,34},{98,6... | collective-permute-start | bytes 196616 | tf_op jit(solution)/shard_map/ppermute | solution.py:21
  20.1 6.3 %copy-start.4 = (bf16[64,128,256]{2,1,0:T(8,128)(2,1)S(1)}, bf16[64,128,256]{2,1,0:T(8,128)(2,1)}, u32[]{:S(2)}) copy-start(bf16[64,128,256]{2,1,0:T(8,128)(2,1)} %param.11) | copy-start | bytes 12582916
  28.3 9.2 %collective-permute-start.2 = (bf16[66,1,256]{2,1,0:T(2,128)(2,1)S(1)}, bf16[66,1,256]{2,1,0:T(2,128)(2,1)S(1)}, u32[]{:S(2)}, u32[]{:S(2)}) collective-permute-start(bf16[66,1,256]{2,1,0:T(2,128)(2,1)S(1)} %get-tuple-element.33), channel_id=1, source_target_pairs={{0,1},{1,2},{2,3},{3,4},{4,5},{5,6},{6,7},{7,8},{8,9},{9,10},{10,1... | collective-permute-start | bytes 101384 | tf_op jit(solution)/shard_map/ppermute | solution.py:20
  31.0 7.7 %collective-permute-start.3 = (bf16[66,1,256]{2,1,0:T(2,128)(2,1)S(1)}, bf16[66,1,256]{2,1,0:T(2,128)(2,1)S(1)}, u32[]{:S(2)}, u32[]{:S(2)}) collective-permute-start(bf16[66,1,256]{2,1,0:T(2,128)(2,1)S(1)} %get-tuple-element.34), channel_id=1, source_target_pairs={{1,0},{2,1},{3,2},{4,3},{5,4},{6,5},{7,6},{8,7},{9,8},{10,9},{11,1... | collective-permute-start | bytes 101384 | tf_op jit(solution)/shard_map/ppermute | solution.py:21
  37.5 14.1 %copy-start.9 = (bf16[2304,256]{1,0:T(8,128)(2,1)S(1)}, bf16[2304,256]{1,0:T(8,128)(2,1)}, u32[]{:S(2)}) copy-start(bf16[2304,256]{1,0:T(8,128)(2,1)} %param.12) | copy-start | bytes 3538948
  51.6 4.5 %copy-start.6 = (bf16[64,128,256]{2,1,0:T(8,128)(2,1)S(1)}, bf16[64,128,256]{2,1,0:T(8,128)(2,1)}, u32[]{:S(2)}) copy-start(bf16[64,128,256]{2,1,0:T(8,128)(2,1)} %get-tuple-element.25) | copy-start | bytes 12582916
  61.1 3.8 %copy-start.5 = (bf16[64,128,256]{2,1,0:T(8,128)(2,1)S(1)}, bf16[64,128,256]{2,1,0:T(8,128)(2,1)}, u32[]{:S(2)}) copy-start(bf16[64,128,256]{2,1,0:T(8,128)(2,1)} %param.11) | copy-start | bytes 12582916
  66.1 3.6 %copy-start.11 = (f32[256]{0:T(256)S(1)}, f32[256]{0:T(256)}, u32[]{:S(2)}) copy-start(f32[256]{0:T(256)} %param.13) | copy-start | bytes 3076
  80.9 11.8 %copy-start.13 = (s32[1,32]{1,0:T(1,128)S(1)}, s32[1,32]{1,0:T(1,128)}, u32[]{:S(2)}) copy-start(s32[1,32]{1,0:T(1,128)} %param.16) | copy-start | bytes 388
  92.0 15.0 %copy-start.7 = (f32[1,8192]{1,0:T(1,128)}, f32[1,8192]{1,0:T(1,128)S(1)}, u32[]{:S(2)}) copy-start(f32[1,8192]{1,0:T(1,128)S(1)} %fusion.104) | copy-start | bytes 98308
  93.6 13.5 %all-to-all-start.1 = ((bf16[32,1,1]{2,1,0:T(2,128)(2,1)}), bf16[32,1,1]{2,1,0:T(2,128)(2,1)S(1)}, u32[]{:S(2)}, u32[]{:S(2)}) async-start(bf16[32,1,1]{2,1,0:T(2,128)(2,1)} %copy.64), calls=%async_computation.1 | async-start | bytes 32768 | tf_op jit(solution)/shard_map/all_to_all | solution.py:116
  107.0 7.9 %copy-start.3 = (s32[1,32]{1,0:T(1,128)S(1)}, s32[1,32]{1,0:T(1,128)}, u32[]{:S(2)}) copy-start(s32[1,32]{1,0:T(1,128)} %param.18) | copy-start | bytes 388
  107.0 9.2 %copy-start.12 = (s32[1,32]{1,0:T(1,128)S(1)}, s32[1,32]{1,0:T(1,128)}, u32[]{:S(2)}) copy-start(s32[1,32]{1,0:T(1,128)} %param.17) | copy-start | bytes 388
  107.0 76.4 %all-to-all-start = ((bf16[32,1,24,3200]{3,2,1,0:T(8,128)(2,1)}), bf16[32,1,24,3200]{3,2,1,0:T(8,128)(2,1)}, u32[]{:S(2)}, u32[]{:S(2)}) async-start(bf16[32,1,24,3200]{3,2,1,0:T(8,128)(2,1)} %copy.58), calls=%async_computation | async-start | bytes 9830400 | tf_op jit(solution)/shard_map/all_to_all | solution.py:115
  186.9 2.7 copy-start.10
  223.5 24.0 %copy-start.2 = (s32[1,256]{1,0:T(1,128)S(1)}, s32[1,256]{1,0:T(1,128)}, u32[]{:S(2)}) copy-start(s32[1,256]{1,0:T(1,128)} %param.19) | copy-start | bytes 3076
  237.2 1.3 copy-start.8
  238.5 21.3 %collective-permute-start.4 = (bf16[192,3328]{1,0:T(8,128)(2,1)S(1)}, bf16[192,3328]{1,0:T(8,128)(2,1)S(1)}, u32[]{:S(2)}, u32[]{:S(2)}) collective-permute-start(bf16[192,3328]{1,0:T(8,128)(2,1)S(1)} %slice.136), channel_id=1, source_target_pairs={{0,1},{1,2},{2,3},{3,4},{4,5},{5,6},{6,7},{7,8},{8,9},{9,10},{10,1... | collective-permute-start | bytes 3833864 | tf_op jit(solution)/shard_map/ppermute | solution.py:20
  245.6 20.8 %collective-permute-start.5 = (bf16[192,3328]{1,0:T(8,128)(2,1)S(1)}, bf16[192,3328]{1,0:T(8,128)(2,1)}, u32[]{:S(2)}, u32[]{:S(2)}) collective-permute-start(bf16[192,3328]{1,0:T(8,128)(2,1)S(1)} %slice.136), channel_id=1, source_target_pairs={{1,0},{2,1},{3,2},{4,3},{5,4},{6,5},{7,6},{8,7},{9,8},{10,9},{11,1... | collective-permute-start | bytes 3833864 | tf_op jit(solution)/shard_map/ppermute | solution.py:21
  289.7 2.2 copy-start.1
Sparse Core Ops, SparseCore 0:
  11.0 164.7 all-gather.2
where the time goes:
time: 304 us; the launch traced here: 299 us
  waiting for transfers between devices  85.2 us (28%)
  matrix products  74.4 us (24%)
  local copies, waits for them, and re-layouts  59.8 us (20%)
  starting transfers between devices  33.3 us (11%)
  other arithmetic  30.2 us (10%)
  between operations  16.1 us (5%)
    all_to_all x1, waiting for transfers between devices, shards(): lax.all_to_all(send_tiles, 'dev', split_axis=0, concat_axis=0, tiled=True)  66.4 us
    dot_general x9, matrix products, conv_scores(): jnp.dot(window, conv_weight[offset:offset + channels], preferred_element_...  33.5 us
    unnamed x30, local copies, waits for them, and re-layouts  33 us
    concatenate x3, other arithmetic, with_halo(): value = jnp.concatenate([before, value, after], axis=dim)  16.3 us
    dot_general x1, matrix products, shards(): jnp.dot(normed, lax.all_gather(qkv_weight, ('grp', 'dev'), axis=0, tiled=...  13.7 us
    ppermute x3, starting transfers between devices, with_halo(): before = lax.ppermute(last, axis, up)  12.8 us
    dot_general x1, matrix products, conv_scores(): return jnp.dot(hidden, score_weight, precision=lax.Precision.HIGHEST)  11.1 us
    ppermute x3, waiting for transfers between devices, with_halo(): before = lax.ppermute(last, axis, up)  10.3 us
  transfers between devices with their start and end apart: 9, of which 4 were waited for; matrix products, arithmetic and copies ran while one was open for 31% of the time, Pallas kernels for 0%

commit v1 on v0

v1 whole, which is shorter than its diff:
```python
import math

import jax
import jax.numpy as jnp
import numpy as np
from jax import lax
from jax.experimental import pallas as pl
from jax.experimental.pallas import tpu as pltpu
from jax.sharding import PartitionSpec as P


HD = 128
HEADS = 13
HW = HEADS * HD
MT = 8
BF = jnp.bfloat16
F32 = jnp.float32
ANY = pl.BlockSpec(memory_space=pl.ANY)
SMEM = pl.BlockSpec(memory_space=pltpu.SMEM)
VMEM = pl.BlockSpec(memory_space=pltpu.VMEM)


def ring_pairs(axis):
    size = lax.axis_size(axis)
    up = [(i, i + 1) for i in range(size - 1)]
    return up, [(j, i) for i, j in up]


def send_order(counts, order, own, tokens):
    holders = order.shape[0]

    def body(counts_ref, order_ref, own_ref, tok_ref, out_ref, tiles, in_sems, out_sems):
        fetch = [pltpu.make_async_copy(tok_ref.at[s], tiles.at[s], in_sems.at[s]) for s in range(holders)]
        for c in fetch:
            c.start()
        first = lax.fori_loop(0, own_ref[0], lambda j, acc: acc + counts_ref[j], jnp.int32(0))

        def copy(s):
            holder = order_ref[(first + s) & (holders - 1)]
            return pltpu.make_async_copy(tiles.at[s], out_ref.at[holder], out_sems.at[s])

        for s in range(holders):
            fetch[s].wait()
            copy(s).start()
        for s in range(holders):
            copy(s).wait()

    return pl.pallas_call(
        body,
        out_shape=jax.ShapeDtypeStruct(tokens.shape, tokens.dtype),
        in_specs=[SMEM, SMEM, SMEM, ANY],
        out_specs=ANY,
        scratch_shapes=[
            pltpu.VMEM(tokens.shape, tokens.dtype),
            pltpu.SemaphoreType.DMA((holders,)),
            pltpu.SemaphoreType.DMA((holders,)),
        ],
        name="send_order",
    )(counts, order, own, tokens)


def spread_index(parts, rows):
    part, row = np.arange(parts)[:, None], np.arange(8)[None, :]
    main = [(rows * part + 8 * b + row).reshape(-1) for b in range(rows // 8)]
    return np.concatenate(main + [rows * np.arange(parts) + rows - 1]).astype(np.int32)


def hold_and_norm(source, recv, gain, parts):
    tile_len, width = recv.shape[1], recv.shape[2]
    rows = MT * tile_len
    index = spread_index(parts, width // parts)
    blocks = width // 128
    table = jnp.asarray(index.reshape(blocks, 128))

    def body(src_ref, recv_ref, gain_ref, table_ref, out_ref, tiles, normed, sems):
        copies = [
            pltpu.make_async_copy(recv_ref.at[src_ref[m]], tiles.at[m], sems.at[m]) for m in range(MT)
        ]
        for c in copies:
            c.start()
        for m in range(MT):
            copies[m].wait()
            values = tiles[m].astype(F32)
            center = jnp.mean(values, axis=1, keepdims=True)
            values = values - center
            spread = jnp.mean(values * values, axis=1, keepdims=True)
            scaled = values * lax.rsqrt(spread + 1e-06) * gain_ref[...]
            normed[m * tile_len : (m + 1) * tile_len, :] = scaled.astype(BF)
        for n in range(blocks):
            part = index[n * 128 : (n + 1) * 128]
            low = int(part.min()) // 128 * 128
            high = int(part.max()) // 128 * 128 + 128
            place = lax.broadcasted_iota(jnp.int32, (high - low, 128), 0) + low
            pick = jnp.where(place == table_ref[n : n + 1, :], 1.0, 0.0).astype(BF)
            out_ref[:, n * 128 : (n + 1) * 128] = jnp.dot(
                normed[:, low:high], pick, preferred_element_type=F32
            ).astype(BF)

    return pl.pallas_call(
        body,
        out_shape=jax.ShapeDtypeStruct((rows, width), BF),
        in_specs=[SMEM, ANY, VMEM, VMEM],
        out_specs=VMEM,
        scratch_shapes=[
            pltpu.VMEM((MT, tile_len, width), BF),
            pltpu.VMEM((rows, width), BF),
            pltpu.SemaphoreType.DMA((MT,)),
        ],
        name="hold_and_norm",
    )(source, recv, gain.reshape(1, width), table)


def conv_scores(canvas, top, bottom, left, right, weight, bias, readout):
    height, breadth, channels = canvas.shape
    hidden = weight.shape[1]
    step = 8
    pixels = step * breadth

    def side(edge):
        return jnp.concatenate([edge[0:height], edge[1 : height + 1], edge[2 : height + 2]], axis=1)

    def body(canvas_ref, top_ref, bottom_ref, left_ref, right_ref, w_ref, bias_ref, read_ref, out_ref,
             padded, lside, rside, sem):
        i = pl.program_id(0)

        def w_of(col):
            return jnp.concatenate(
                [w_ref[(row * 3 + col) * channels : (row * 3 + col + 1) * channels, :] for row in range(3)],
                axis=0,
            )

        @pl.when(i == 0)
        def _():
            fetch = pltpu.make_async_copy(canvas_ref, padded.at[pl.ds(1, height)], sem)
            fetch.start()
            padded[0:1] = top_ref[...]
            padded[height + 1 : height + 2] = bottom_ref[...]
            sides = (height // step, step, hidden)
            lside[...] = jnp.dot(left_ref[...], w_of(0), preferred_element_type=F32).reshape(sides)
            rside[...] = jnp.dot(right_ref[...], w_of(2), preferred_element_type=F32).reshape(sides)
            fetch.wait()

        window = jnp.concatenate(
            [padded[pl.ds(i * step + row, step)].reshape(pixels, channels) for row in range(3)], axis=1
        )
        before = jnp.dot(window, w_of(0), preferred_element_type=F32)
        at = jnp.dot(window, w_of(1), preferred_element_type=F32)
        after = jnp.dot(window, w_of(2), preferred_element_type=F32)
        before = pltpu.roll(before, 1, 0).reshape(step, breadth, hidden)
        after = pltpu.roll(after, pixels - 1, 0).reshape(step, breadth, hidden)
        col = lax.broadcasted_iota(jnp.int32, (step, breadth, hidden), 1)
        lrow = lside[i]
        rrow = rside[i]
        before = jnp.where(col == 0, lrow[:, None, :], before)
        after = jnp.where(col == breadth - 1, rrow[:, None, :], after)
        x = (before + after).reshape(pixels, hidden) + at + bias_ref[...]
        inner = math.sqrt(2.0 / math.pi) * (x + 0.044715 * (x * x * x))
        h = x * (0.5 * (1.0 + jnp.tanh(inner)))
        h = h * read_ref[...]
        half = h[:, 0:128]
        for k in range(1, hidden // 128):
            half = half + h[:, k * 128 : (k + 1) * 128]
        ones = jnp.ones((8, 128), F32)
        score = lax.dot_general(
            ones, half, (((1,), (1,)), ((), ())), precision=lax.Precision.HIGHEST, preferred_element_type=F32
        )
        for r in range(step):
            out_ref[0, r : r + 1, :] = score[0:1, r * breadth : (r + 1) * breadth]

    out = pl.pallas_call(
        body,
        grid=(height // step,),
        out_shape=jax.ShapeDtypeStruct((height // step, step, breadth), F32),
        in_specs=[ANY] + [pl.BlockSpec(memory_space=pltpu.VMEM)] * 7,
        out_specs=pl.BlockSpec((1, step, breadth), lambda i: (i, 0, 0)),
        scratch_shapes=[
            pltpu.VMEM((height + 2, breadth, channels), BF),
            pltpu.VMEM((height // step, step, hidden), F32),
            pltpu.VMEM((height // step, step, hidden), F32),
            pltpu.SemaphoreType.DMA,
        ],
        compiler_params=pltpu.CompilerParams(vmem_limit_bytes=32 << 20),
        name="conv_scores",
    )(canvas, top, bottom, side(left), side(right), weight, bias.reshape(1, hidden), readout.reshape(1, hidden))
    return out.reshape(height, breadth)


def pack_rows(weight):
    eights = weight.shape[0] // 8
    tiles = weight.shape[1] // 128
    last = weight[8 * eights :].reshape(tiles, 128)
    last = jnp.pad(last, ((0, -tiles % 8), (0, 0))).reshape(-1, 8, 128)
    pieces = []
    for b in range(eights):
        pieces += [weight[8 * b : 8 * b + 8], last[b]]
    return jnp.concatenate(pieces + [last[j] for j in range(eights, last.shape[0])], axis=1)


def project(normed, packed, sharp, head_width):
    rows, width = normed.shape
    deep = packed.shape[0]
    eights = width // deep
    parts = deep // 8
    pairs = 20
    block = 256

    def body(x_ref, w0, w1, w2, last_ref, sharp_ref, out_ref):
        n = pl.program_id(0)
        acc = jnp.dot(x_ref[:, 0:deep], w0[...], preferred_element_type=F32)
        acc = acc + jnp.dot(x_ref[:, deep : 2 * deep], w1[...], preferred_element_type=F32)
        acc = acc + jnp.dot(x_ref[:, 2 * deep : 3 * deep], w2[...], preferred_element_type=F32)
        part = lax.broadcasted_iota(jnp.int32, (parts, deep), 0)
        place = lax.broadcasted_iota(jnp.int32, (parts, deep), 1)
        lasts = []
        for k in range(2):
            pick = jnp.where(place == 8 * part + (2 * n + k) % 8, 1.0, 0.0).astype(BF)
            lasts.append(jnp.dot(pick, last_ref[...], preferred_element_type=F32).astype(BF))
        acc = acc + jnp.dot(x_ref[:, 3 * deep :], jnp.concatenate(lasts, axis=1), preferred_element_type=F32)
        col = lax.broadcasted_iota(jnp.int32, (1, block), 1) + n * block
        is_key = (col >= head_width) & (col < 2 * head_width)
        out_ref[...] = (acc * jnp.where(is_key, sharp_ref[...], 1.0)).astype(BF)

    def last_tile(n):
        j = n // 4
        return (0, jnp.where(j < eights, 40 * j + 39, 117 + j))

    return pl.pallas_call(
        body,
        grid=(pairs,),
        out_shape=jax.ShapeDtypeStruct((rows, pairs * block), BF),
        in_specs=[
            VMEM,
            pl.BlockSpec((deep, block), lambda n: (0, n)),
            pl.BlockSpec((deep, block), lambda n: (0, n + 20)),
            pl.BlockSpec((deep, block), lambda n: (0, n + 40)),
            pl.BlockSpec((deep, 128), last_tile),
            VMEM,
        ],
        out_specs=pl.BlockSpec((rows, block), lambda n: (0, n)),
        compiler_params=pltpu.CompilerParams(vmem_limit_bytes=32 << 20),
        name="project",
    )(normed, packed, packed, packed, packed, sharp)


def attend(before, here, after, own_ids, key_ids):
    rows = here.shape[0]
    scale = 1.0 / math.sqrt(HD)

    def body(q_ref, kb, kh, ka, vb, vh, va, own_ref, key_ref, out_ref, bias):
        @pl.when(pl.program_id(0) == 0)
        def _():
            bias[...] = jnp.where(own_ref[...] == key_ref[...], 0.0, -1e30)

        q = q_ref[...]
        parts = [
            lax.dot_general(q, k[...], (((1,), (1,)), ((), ())), preferred_element_type=F32)
            for k in (kb, kh, ka)
        ]
        logits = jnp.concatenate(parts, axis=1) * scale + bias[...]
        peak = jnp.max(logits, axis=1, keepdims=True)
        weights = jnp.exp(logits - peak)
        total = jnp.sum(weights, axis=1, keepdims=True)
        probs = weights.astype(BF)
        value = jnp.concatenate([vb[...], vh[...], va[...]], axis=0)
        out = jnp.dot(probs, value, preferred_element_type=F32)
        out_ref[...] = (out / total).astype(BF)

    q_spec = pl.BlockSpec((rows, HD), lambda h: (0, h))
    k_here = pl.BlockSpec((rows, HD), lambda h: (0, h + HEADS))
    v_here = pl.BlockSpec((rows, HD), lambda h: (0, h + 2 * HEADS))
    k_near = pl.BlockSpec((rows, HD), lambda h: (0, h))
    v_near = pl.BlockSpec((rows, HD), lambda h: (0, h + HEADS))
    return pl.pallas_call(
        body,
        grid=(HEADS,),
        out_shape=jax.ShapeDtypeStruct((rows, HW), BF),
        in_specs=[q_spec, k_near, k_here, k_near, v_near, v_here, v_near, VMEM, VMEM],
        out_specs=q_spec,
        scratch_shapes=[pltpu.VMEM((rows, 3 * rows), F32)],
        name="attend",
    )(here, before, here, after, before, here, after, own_ids, key_ids)


def shards(
    canvas,
    conv_weight,
    conv_bias,
    score_weight,
    tile_tokens,
    tile_cell,
    tile_count,
    holder_order,
    tile_image,
    ln_gain,
    qkv_weight,
):
    axes = ("grp", "dev")
    holders = lax.axis_size("dev")
    parts = holders * lax.axis_size("grp")
    own = lax.axis_index("dev")
    counts, order = tile_count[0], holder_order[0]
    tile_len = tile_tokens.shape[1]
    held_rows = MT * tile_len

    sent = send_order(counts, order, own.reshape(1), tile_tokens)
    recv = lax.all_to_all(sent, "dev", split_axis=0, concat_axis=0, tiled=True)

    packed = lax.all_gather(pack_rows(qkv_weight), axes, axis=0, tiled=True)

    up, down = ring_pairs("grp")
    top = lax.ppermute(canvas[-1:], "grp", up)
    bottom = lax.ppermute(canvas[:1], "grp", down)
    up, down = ring_pairs("dev")

    def edge(col):
        return jnp.concatenate([top[:, col], canvas[:, col], bottom[:, col]], axis=0)

    left = lax.ppermute(edge(-1), "dev", up)
    right = lax.ppermute(edge(0), "dev", down)
    score_map = conv_scores(canvas, top, bottom, left, right, conv_weight, conv_bias, score_weight)

    ranks = jnp.arange(holders, dtype=jnp.int32)
    first = jnp.sum(jnp.where(ranks < own, counts, 0))
    place_of = jnp.sum(jnp.where(order[None, :] == ranks[:, None], ranks[None, :], 0), axis=1)
    slot_for = (place_of - first) & (holders - 1)
    cells = jnp.take(tile_cell[0], slot_for)
    send_score = jnp.take(score_map.reshape(-1), cells).astype(BF)
    recv, send_score = lax.optimization_barrier((recv, send_score))
    recv_score = lax.all_to_all(
        send_score.reshape(holders, 1, 1), "dev", split_axis=0, concat_axis=0, tiled=True
    ).reshape(holders)

    place = jnp.sum(jnp.where(order == own, ranks, 0))
    wanted = jnp.arange(MT, dtype=jnp.int32) * holders + place
    ends = jnp.sum(jnp.where(ranks[None, :] <= ranks[:, None], counts[None, :], 0), axis=1)
    source = jnp.sum((ends[None, :] <= wanted[:, None]).astype(jnp.int32), axis=1)
    held_score = jnp.take(recv_score, source).astype(F32)
    sharp = jnp.repeat(0.5 + jax.nn.softplus(held_score), tile_len)[:, None]

    normed = hold_and_norm(source, recv, ln_gain, parts)
    here = project(normed, packed, sharp, HW)
    near = here[:, HW : 3 * HW]
    before = lax.ppermute(near, "dev", up)
    after = lax.ppermute(near, "dev", down)

    all_ids = tile_image[0]
    places = own * MT - MT + jnp.arange(3 * MT, dtype=jnp.int32)
    inside = (places >= 0) & (places < all_ids.shape[0])
    near_ids = jnp.where(inside, jnp.take(all_ids, jnp.clip(places, 0, all_ids.shape[0] - 1)), -1)
    key_ids = jnp.repeat(near_ids, tile_len)
    own_ids = key_ids[held_rows : 2 * held_rows]
    attended = attend(before, here, after, own_ids[:, None], key_ids[None, :])
    return (score_map, attended)


def solution(mesh):
    placed = (
        P("grp", "dev", None),
        P(),
        P(),
        P(),
        P(("grp", "dev"), None, None),
        P("grp", "dev"),
        P("grp", None),
        P("grp", None),
        P("grp", None),
        P(),
        P(("grp", "dev"), None),
    )
    return jax.shard_map(
        shards,
        mesh=mesh,
        in_specs=placed,
        out_specs=(P("grp", "dev"), P(("grp", "dev"), None)),
        check_vma=False,
    )
```

time: 304 us -> 228 us (0.75)
  matrix products: 74.4 us -> 0 us
  Pallas kernels: 0 us -> 70.9 us
  local copies, waits for them, and re-layouts: 59.8 us -> 18.7 us
  other arithmetic: 30.2 us -> 4.58 us
    dot_general x17 -> x0, matrix products: 74.4 us -> none  [the longest x9 33.5 us: conv_scores(): jnp.dot(window, conv_weight[offset:offset + channels], preferred_element_...]
    pallas_call x0 -> x5, Pallas kernels: none -> 70.9 us  [the longest x1 23.6 us: project(): pl.pallas_call(body, grid=(pairs,), out_shape=jax.ShapeDtypeStruct((rows,...]
    all_to_all x2, waiting for transfers between devices: 66.4 us -> 0.01 us  [the longest x1 0.01 us: shards(): recv = lax.all_to_all(sent, 'dev', split_axis=0, concat_axis=0, tiled=True)]
    ppermute x6, waiting for transfers between devices: 18.1 us -> 69.9 us  [the longest x1 53.2 us: shards(): right = lax.ppermute(edge(0), 'dev', down)]
    unnamed x30 -> x37, local copies, waits for them, and re-layouts: 33 us -> 6.96 us
    concatenate x3, other arithmetic: 16.3 us -> 0.05 us  [the longest x2 0.03 us: edge(): jnp.concatenate([top[:, col], canvas[:, col], bottom[:, col]], axis=0)]
    all_gather x1, waiting for transfers between devices: 0.02 us -> 15.8 us  [shards(): packed = lax.all_gather(pack_rows(qkv_weight), axes, axis=0, tiled=True)]
    sub x3 -> x0, other arithmetic: 8.68 us -> none  [the longest x1 8.01 us: attend(): weights = jnp.exp(logits - peak)]
  transfers between devices with their start and end apart: 9 -> 9, of which waited for: 4 -> 4; matrix products, arithmetic and copies ran while one was open for 31% -> 6% of each run, Pallas kernels for 0% -> 16%
where the time goes in v1:
time: 228 us; the launch traced here: 226 us
  waiting for transfers between devices  85.7 us (38%)
  Pallas kernels  70.9 us (31%)
  starting transfers between devices  31.3 us (14%)
  local copies, waits for them, and re-layouts  18.7 us (8%)
  between operations  14.5 us (6%)
  other arithmetic  4.58 us (2%)
    ppermute x1, waiting for transfers between devices, shards(): right = lax.ppermute(edge(0), 'dev', down)  53.2 us
    pallas_call x1, Pallas kernels, project(): pl.pallas_call(body, grid=(pairs,), out_shape=jax.ShapeDtypeStruct((rows,...  23.6 us
    pallas_call x1, Pallas kernels, conv_scores(): pl.pallas_call(body, grid=(height // step,), out_shape=jax.ShapeDtypeStru...  22.9 us
    all_gather x1, waiting for transfers between devices, shards(): packed = lax.all_gather(pack_rows(qkv_weight), axes, axis=0, tiled=True)  15.8 us
    pallas_call x1, Pallas kernels, attend(): pl.pallas_call(body, grid=(HEADS,), out_shape=jax.ShapeDtypeStruct((rows,...  12.1 us
    ppermute x1, waiting for transfers between devices, shards(): before = lax.ppermute(near, 'dev', up)  10.2 us
    all_to_all x1, starting transfers between devices, shards(): recv = lax.all_to_all(sent, 'dev', split_axis=0, concat_axis=0, tiled=True)  7.77 us
    unnamed x37, local copies, waits for them, and re-layouts  6.96 us
  transfers between devices with their start and end apart: 9, of which 4 were waited for; matrix products, arithmetic and copies ran while one was open for 6% of the time, Pallas kernels for 16%

profile of v1, /device:TPU:97, one launch (start us, length us, event | category | flops | bytes accessed | tf_op | source)
XLA Modules:
  0.0 225.6 jit_solution(10102444675749096205)
XLA Ops:
  7.2 0.0 copy-start
  7.2 0.0 all-gather.2.cloned.1.call-start
  7.2 0.8 slice_reduce_fusion.1
  8.0 0.9 slice_dynamic-update-slice_fusion.2
  8.9 0.9 slice_reduce_fusion
  9.9 0.9 slice_dynamic-update-slice_fusion.1
  10.8 0.9 slice_dynamic-update-slice_fusion
  11.7 0.0 copy-start.9
  11.7 0.7 copy-done.9
  12.4 0.0 all-gather.2.cloned.1.call-update
  12.5 5.7 %send_order.1 = bf16[32,24,3200]{2,1,0:T(8,128)(2,1)} custom-call(s32[32]{0:T(128)} %bitcast.67, s32[32]{0:T(128)} %bitcast.65, s32[1]{0:T(128)} %bitcast.11.own_ref, bf16[32,24,3200]{2,1,0:T(8,128)(2,1)} %tok_ref.1), custom_call_target="tpu_custom_call" | custom-call | tf_op jit(solution)/shard_map/send_order/pallas_call | solution.py:48
  18.2 0.0 copy-start.10
  18.2 0.0 copy-start.11
  18.2 0.0 copy-start.12
  18.2 0.0 copy-start.7
  18.2 0.0 copy-start.4
  18.2 0.0 copy-start.5
  18.2 0.0 copy-start.6
  18.3 7.8 %all-to-all-start = ((bf16[32,24,3200]{2,1,0:T(8,128)(2,1)}), bf16[32,24,3200]{2,1,0:T(8,128)(2,1)}, u32[]{:S(2)}, u32[]{:S(2)}) async-start(bf16[32,24,3200]{2,1,0:T(8,128)(2,1)} %send_order.1), calls=%async_computation | async-start | bytes 9830400 | tf_op jit(solution)/shard_map/all_to_all | solution.py:306
  26.0 0.9 fusion.9
  26.9 3.1 %collective-permute-start = (bf16[1,128,256]{2,1,0:T(8,128)(2,1)S(1)}, bf16[1,128,256]{2,1,0:T(8,128)(2,1)S(1)}, u32[]{:S(2)}, u32[]{:S(2)}) collective-permute-start(bf16[1,128,256]{2,1,0:T(8,128)(2,1)S(1)} %get-tuple-element.13), channel_id=1, source_target_pairs={{0,32},{32,64},{64,96},{1,33},{33,65},{65,97},{2,34},{34,66},{66,9... | collective-permute-start | bytes 196616 | tf_op jit(solution)/shard_map/ppermute | solution.py:311
  30.0 1.3 collective-permute-start.1
  31.3 1.1 fusion.8
  32.5 0.6 reshape.161.gain_ref
  33.1 0.6 fusion
  33.8 0.1 select_reduce_fusion
  33.9 0.6 fusion.7
  34.5 0.7 gather_fusion
  35.2 0.7 multiply_add_fusion
  35.9 0.6 fusion.2
  36.5 0.1 select_reduce_fusion.1
  36.6 0.2 convert_reduce_fusion.src_ref
  36.8 0.0 collective-permute-done.1.bottom_ref
  36.9 2.6 %collective-permute-start.3 = (bf16[66,256]{1,0:T(8,128)(2,1)S(1)}, bf16[66,256]{1,0:T(8,128)(2,1)S(1)}, u32[]{:S(2)}, u32[]{:S(2)}) collective-permute-start(bf16[66,256]{1,0:T(8,128)(2,1)S(1)} %pad_maximum_fusion.3), channel_id=1, source_target_pairs={{1,0},{2,1},{3,2},{4,3},{5,4},{6,5},{7,6},{8,7},{9,8},{10,9},{11,1... | collective-permute-start | bytes 101384 | tf_op jit(solution)/shard_map/ppermute | solution.py:319
  39.5 5.1 %collective-permute-start.2 = (bf16[66,256]{1,0:T(8,128)(2,1)S(1)}, bf16[66,256]{1,0:T(8,128)(2,1)S(1)}, u32[]{:S(2)}, u32[]{:S(2)}) collective-permute-start(bf16[66,256]{1,0:T(8,128)(2,1)S(1)} %pad_maximum_fusion.2), channel_id=1, source_target_pairs={{0,1},{1,2},{2,3},{3,4},{4,5},{5,6},{6,7},{7,8},{8,9},{9,10},{10,1... | collective-permute-start | bytes 101384 | tf_op jit(solution)/shard_map/ppermute | solution.py:318
  44.6 53.2 %collective-permute-done.3 = bf16[66,256]{1,0:T(8,128)(2,1)S(1)} collective-permute-done((bf16[66,256]{1,0:T(8,128)(2,1)S(1)}, bf16[66,256]{1,0:T(8,128)(2,1)S(1)}, u32[]{:S(2)}, u32[]{:S(2)}) %collective-permute-start.3) | collective-permute-done | bytes 33824 | tf_op jit(solution)/shard_map/ppermute | solution.py:319
  97.9 0.0 copy-start.3
  97.9 2.2 copy-done.3
  100.1 22.9 %conv_scores.1 = f32[8,8,128]{2,1,0:T(8,128)} custom-call(bf16[64,128,256]{2,1,0:T(8,128)(2,1)S(1)} %copy-done.3, bf16[1,128,256]{2,1,0:T(8,128)(2,1)S(1)} %collective-permute-done.top_ref, bf16[1,128,256]{2,1,0:T(8,128)(2,1)S(1)} %collective-permute-done.1.bottom_ref, bf16[64,768]{1,0:T(8,128)(2,1)S(1)} %get-tuple-element.24.left_ref, ...), custom_call_target="tpu_custom_call" | custom-call | tf_op jit(solution)/shard_map/conv_scores/pallas_call | solution.py:170
  123.0 1.5 gather_fusion.1
  124.4 0.6 fusion.6
  125.0 0.7 copy.32
  125.7 5.1 %all-to-all-start.1 = ((bf16[32,1,1]{2,1,0:T(2,128)(2,1)}), bf16[32,1,1]{2,1,0:T(2,128)(2,1)S(1)}, u32[]{:S(2)}, u32[]{:S(2)}) async-start(bf16[32,1,1]{2,1,0:T(2,128)(2,1)} %copy.32), calls=%async_computation.1 | async-start | bytes 32768 | tf_op jit(solution)/shard_map/all_to_all | solution.py:329
  130.8 6.5 %hold_and_norm.1.x_ref = bf16[192,3200]{1,0:T(8,128)(2,1)} custom-call(s32[8]{0:T(128)} %copy-done.13, bf16[32,24,3200]{2,1,0:T(8,128)(2,1)} %all-to-all-done.recv_ref, f32[1,3200]{1,0:T(1,128)} %reshape.161.gain_ref, s32[25,128]{1,0:T(8,128)} %constant.83.clone.table_ref), custom_call_target="tpu_custom_call" | custom-call | tf_op jit(solution)/shard_map/hold_and_norm/pallas_call | solution.py:99
  137.4 0.3 reduce.5
  137.7 0.6 gather_fusion.2
  138.4 0.7 fusion.4
  139.1 0.1 broadcast_in_dim.72
  139.1 0.1 broadcast_in_dim_reshape.8.sharp_ref
  139.2 15.8 %all-gather.2.cloned.1.call-done.w0.w1.w2.last_ref = bf16[1024,15616]{1,0:T(8,128)(2,1)} async-done(((bf16[8,15616]{1,0:T(8,128)(2,1)}), bf16[1024,15616]{1,0:T(8,128)(2,1)}) %all-gather.2.cloned.1.call-update) | async-done | bytes 31981584 | tf_op jit(solution)/shard_map/all_gather | solution.py:308
  155.0 1.3 copy-done.2
  156.3 23.6 %project.1.q_ref.kh.vh = bf16[192,5120]{1,0:T(8,128)(2,1)S(1)} custom-call(bf16[192,3200]{1,0:T(8,128)(2,1)S(1)} %copy-done.2, bf16[1024,15616]{1,0:T(8,128)(2,1)} %all-gather.2.cloned.1.call-done.w0.w1.w2.last_ref, bf16[1024,15616]{1,0:T(8,128)(2,1)} %all-gather.2.cloned.1.call-done.w0.w1.w2.last_ref, ...), custom_call_target="tpu_custom_call" | custom-call | tf_op jit(solution)/shard_map/project/pallas_call | solution.py:227
  180.0 1.2 slice.149
  181.2 4.4 %collective-permute-start.4 = (bf16[192,3328]{1,0:T(8,128)(2,1)}, bf16[192,3328]{1,0:T(8,128)(2,1)S(1)}, u32[]{:S(2)}, u32[]{:S(2)}) collective-permute-start(bf16[192,3328]{1,0:T(8,128)(2,1)} %slice.149), channel_id=1, source_target_pairs={{0,1},{1,2},{2,3},{3,4},{4,5},{5,6},{6,7},{7,8},{8,9},{9,10},{10,1... | collective-permute-start | bytes 3833864 | tf_op jit(solution)/shard_map/ppermute | solution.py:343
  185.6 1.9 collective-permute-start.5
  187.5 0.7 gather_fusion.3
  188.3 0.1 slice.130
  188.3 0.1 broadcast_in_dim.74
  188.4 0.7 broadcast_in_dim.77.own_ref
  189.1 0.1 broadcast_in_dim.76
  189.2 0.7 broadcast_in_dim_reshape.7.key_ref
  189.9 10.2 %collective-permute-done.4.kb.vb = bf16[192,3328]{1,0:T(8,128)(2,1)S(1)} collective-permute-done((bf16[192,3328]{1,0:T(8,128)(2,1)}, bf16[192,3328]{1,0:T(8,128)(2,1)S(1)}, u32[]{:S(2)}, u32[]{:S(2)}) %collective-permute-start.4) | collective-permute-done | bytes 1277984 | tf_op jit(solution)/shard_map/ppermute | solution.py:343
  200.1 6.5 %collective-permute-done.5.ka.va = bf16[192,3328]{1,0:T(8,128)(2,1)} collective-permute-done((bf16[192,3328]{1,0:T(8,128)(2,1)}, bf16[192,3328]{1,0:T(8,128)(2,1)}, u32[]{:S(2)}, u32[]{:S(2)}) %collective-permute-start.5) | collective-permute-done | bytes 1277984 | tf_op jit(solution)/shard_map/ppermute | solution.py:344
  206.6 12.1 %attend.1 = bf16[192,1664]{1,0:T(8,128)(2,1)} custom-call(bf16[192,5120]{1,0:T(8,128)(2,1)} %copy-done.1, bf16[192,3328]{1,0:T(8,128)(2,1)} %copy-done.8, bf16[192,5120]{1,0:T(8,128)(2,1)} %copy-done.1, bf16[192,3328]{1,0:T(8,128)(2,1)} %collective-permute-done.5.ka.va, bf16[192,3328]{1,0:T(8,128)(2,1)} %copy-done.8, bf16[192,5120]{1,0:T(8,128)(2,1)} %copy-done.1, ...), custom_call_target="tpu_custom_call" | custom-call | tf_op jit(solution)/shard_map/attend/pallas_call | solution.py:273
  (40 shorter events, 0.2 us)
Async XLA Ops:
  7.2 180.4 %copy-start = (s32[1,256]{1,0:T(1,128)S(1)}, s32[1,256]{1,0:T(1,128)}, u32[]{:S(2)}) copy-start(s32[1,256]{1,0:T(1,128)} %param.20) | copy-start | bytes 3076
  7.2 147.8 %all-gather.2.cloned.1.call-start = ((), (), s32[]{:S(2)}) async-start(), calls=%async_computation.2 | async-start | bytes 32231424 | tf_op jit(solution)/shard_map/all_gather | solution.py:308
  11.7 0.7 copy-start.9
  18.2 14.3 %copy-start.10 = (f32[3200]{0:T(1024)S(1)}, f32[3200]{0:T(1024)}, u32[]{:S(2)}) copy-start(f32[3200]{0:T(1024)} %param.21) | copy-start | bytes 38404
  18.2 15.0 %copy-start.11 = (s32[1,32]{1,0:T(1,128)S(1)}, s32[1,32]{1,0:T(1,128)}, u32[]{:S(2)}) copy-start(s32[1,32]{1,0:T(1,128)} %param.19) | copy-start | bytes 388
  18.2 14.9 %copy-start.12 = (s32[1,32]{1,0:T(1,128)S(1)}, s32[1,32]{1,0:T(1,128)}, u32[]{:S(2)}) copy-start(s32[1,32]{1,0:T(1,128)} %param.18) | copy-start | bytes 388
  18.2 16.3 %copy-start.7 = (s32[1,32]{1,0:T(1,128)S(1)}, s32[1,32]{1,0:T(1,128)}, u32[]{:S(2)}) copy-start(s32[1,32]{1,0:T(1,128)} %param.17) | copy-start | bytes 388
  18.2 79.6 %copy-start.4 = (bf16[2304,256]{1,0:T(8,128)(2,1)S(1)}, bf16[2304,256]{1,0:T(8,128)(2,1)}, u32[]{:S(2)}) copy-start(bf16[2304,256]{1,0:T(8,128)(2,1)} %w_ref.1) | copy-start | bytes 3538948
  18.2 79.6 %copy-start.5 = (f32[256]{0:T(256)S(1)}, f32[256]{0:T(256)}, u32[]{:S(2)}) copy-start(f32[256]{0:T(256)} %param.14) | copy-start | bytes 3076
  18.2 79.6 %copy-start.6 = (f32[256]{0:T(256)S(1)}, f32[256]{0:T(256)}, u32[]{:S(2)}) copy-start(f32[256]{0:T(256)} %param.15) | copy-start | bytes 3076
  18.3 106.8 %all-to-all-start = ((bf16[32,24,3200]{2,1,0:T(8,128)(2,1)}), bf16[32,24,3200]{2,1,0:T(8,128)(2,1)}, u32[]{:S(2)}, u32[]{:S(2)}) async-start(bf16[32,24,3200]{2,1,0:T(8,128)(2,1)} %send_order.1), calls=%async_computation | async-start | bytes 9830400 | tf_op jit(solution)/shard_map/all_to_all | solution.py:306
  26.9 9.9 %collective-permute-start = (bf16[1,128,256]{2,1,0:T(8,128)(2,1)S(1)}, bf16[1,128,256]{2,1,0:T(8,128)(2,1)S(1)}, u32[]{:S(2)}, u32[]{:S(2)}) collective-permute-start(bf16[1,128,256]{2,1,0:T(8,128)(2,1)S(1)} %get-tuple-element.13), channel_id=1, source_target_pairs={{0,32},{32,64},{64,96},{1,33},{33,65},{65,97},{2,34},{34,66},{66,9... | collective-permute-start | bytes 196616 | tf_op jit(solution)/shard_map/ppermute | solution.py:311
  30.0 6.8 %collective-permute-start.1 = (bf16[1,128,256]{2,1,0:T(8,128)(2,1)S(1)}, bf16[1,128,256]{2,1,0:T(8,128)(2,1)S(1)}, u32[]{:S(2)}, u32[]{:S(2)}) collective-permute-start(bf16[1,128,256]{2,1,0:T(8,128)(2,1)S(1)} %get-tuple-element.12), channel_id=1, source_target_pairs={{32,0},{64,32},{96,64},{33,1},{65,33},{97,65},{34,2},{66,34},{98,6... | collective-permute-start | bytes 196616 | tf_op jit(solution)/shard_map/ppermute | solution.py:312
  36.8 94.1 %copy-start.13 = (s32[8]{0:T(128)}, s32[8]{0:T(128)S(1)}, u32[]{:S(2)}) copy-start(s32[8]{0:T(128)S(1)} %convert_reduce_fusion.src_ref) | copy-start | bytes 100
  36.9 60.9 %collective-permute-start.3 = (bf16[66,256]{1,0:T(8,128)(2,1)S(1)}, bf16[66,256]{1,0:T(8,128)(2,1)S(1)}, u32[]{:S(2)}, u32[]{:S(2)}) collective-permute-start(bf16[66,256]{1,0:T(8,128)(2,1)S(1)} %pad_maximum_fusion.3), channel_id=1, source_target_pairs={{1,0},{2,1},{3,2},{4,3},{5,4},{6,5},{7,6},{8,7},{9,8},{10,9},{11,1... | collective-permute-start | bytes 101384 | tf_op jit(solution)/shard_map/ppermute | solution.py:319
  39.5 58.3 %collective-permute-start.2 = (bf16[66,256]{1,0:T(8,128)(2,1)S(1)}, bf16[66,256]{1,0:T(8,128)(2,1)S(1)}, u32[]{:S(2)}, u32[]{:S(2)}) collective-permute-start(bf16[66,256]{1,0:T(8,128)(2,1)S(1)} %pad_maximum_fusion.2), channel_id=1, source_target_pairs={{0,1},{1,2},{2,3},{3,4},{4,5},{5,6},{6,7},{7,8},{8,9},{9,10},{10,1... | collective-permute-start | bytes 101384 | tf_op jit(solution)/shard_map/ppermute | solution.py:318
  97.9 2.2 copy-start.3
  125.7 11.7 %all-to-all-start.1 = ((bf16[32,1,1]{2,1,0:T(2,128)(2,1)}), bf16[32,1,1]{2,1,0:T(2,128)(2,1)S(1)}, u32[]{:S(2)}, u32[]{:S(2)}) async-start(bf16[32,1,1]{2,1,0:T(2,128)(2,1)} %copy.32), calls=%async_computation.1 | async-start | bytes 32768 | tf_op jit(solution)/shard_map/all_to_all | solution.py:329
  155.0 1.3 copy-start.2
  180.0 26.6 %copy-start.1 = (bf16[192,5120]{1,0:T(8,128)(2,1)}, bf16[192,5120]{1,0:T(8,128)(2,1)S(1)}, u32[]{:S(2)}) copy-start(bf16[192,5120]{1,0:T(8,128)(2,1)S(1)} %project.1.q_ref.kh.vh) | copy-start | bytes 5898244
  181.2 18.9 %collective-permute-start.4 = (bf16[192,3328]{1,0:T(8,128)(2,1)}, bf16[192,3328]{1,0:T(8,128)(2,1)S(1)}, u32[]{:S(2)}, u32[]{:S(2)}) collective-permute-start(bf16[192,3328]{1,0:T(8,128)(2,1)} %slice.149), channel_id=1, source_target_pairs={{0,1},{1,2},{2,3},{3,4},{4,5},{5,6},{6,7},{7,8},{8,9},{9,10},{10,1... | collective-permute-start | bytes 3833864 | tf_op jit(solution)/shard_map/ppermute | solution.py:343
  185.6 21.0 %collective-permute-start.5 = (bf16[192,3328]{1,0:T(8,128)(2,1)}, bf16[192,3328]{1,0:T(8,128)(2,1)}, u32[]{:S(2)}, u32[]{:S(2)}) collective-permute-start(bf16[192,3328]{1,0:T(8,128)(2,1)} %slice.149), channel_id=1, source_target_pairs={{1,0},{2,1},{3,2},{4,3},{5,4},{6,5},{7,6},{8,7},{9,8},{10,9},{11,1... | collective-permute-start | bytes 3833864 | tf_op jit(solution)/shard_map/ppermute | solution.py:344
  200.1 6.5 %copy-start.8 = (bf16[192,3328]{1,0:T(8,128)(2,1)}, bf16[192,3328]{1,0:T(8,128)(2,1)S(1)}, u32[]{:S(2)}) copy-start(bf16[192,3328]{1,0:T(8,128)(2,1)S(1)} %collective-permute-done.4.kb.vb) | copy-start | bytes 3833860
Sparse Core Ops, SparseCore 0:
  12.6 142.4 all-gather.1

commit v2 on v1

--- a/solution.py
+++ b/solution.py
@@ -186,99 +186,112 @@
 
 
 def pack_rows(weight):
-    eights = weight.shape[0] // 8
-    tiles = weight.shape[1] // 128
-    last = weight[8 * eights :].reshape(tiles, 128)
-    last = jnp.pad(last, ((0, -tiles % 8), (0, 0))).reshape(-1, 8, 128)
-    pieces = []
-    for b in range(eights):
-        pieces += [weight[8 * b : 8 * b + 8], last[b]]
-    return jnp.concatenate(pieces + [last[j] for j in range(eights, last.shape[0])], axis=1)
-
-
-def project(normed, packed, sharp, head_width):
-    rows, width = normed.shape
+    rows, cols = weight.shape
+    eights, tiles = rows // 8, cols // 128
+    spare = -(-tiles // 8)
+
+    def body(w_ref, out_ref):
+        w = w_ref[...].astype(F32)
+        zero = jnp.zeros((1, 128), F32)
+        for j in range(spare):
+            pieces = [
+                w[rows - 1 : rows, t * 128 : (t + 1) * 128] if t < tiles else zero
+                for t in range(8 * j, 8 * j + 8)
+            ]
+            out_ref[:, j * 128 : (j + 1) * 128] = jnp.concatenate(pieces, axis=0).astype(BF)
+        for b in range(eights):
+            at = spare * 128 + b * cols
+            out_ref[:, at : at + cols] = w[8 * b : 8 * b + 8].astype(BF)
+
+    return pl.pallas_call(
+        body,
+        out_shape=jax.ShapeDtypeStruct((8, spare * 128 + eights * cols), BF),
+        in_specs=[VMEM],
+        out_specs=VMEM,
+        name="pack_rows",
+    )(weight)
+
+
+def project_and_attend(before, here, after, packed, sharp, own_ids, key_ids):
+    rows, width = here.shape
     deep = packed.shape[0]
-    eights = width // deep
-    parts = deep // 8
-    pairs = 20
-    block = 256
-
-    def body(x_ref, w0, w1, w2, last_ref, sharp_ref, out_ref):
+    eights, parts = width // deep, deep // 8
+    near = 3 * rows
+    spare = -(-3 * HEADS // 8)
+    scale = 1.0 / math.sqrt(HD)
+
+    def body(xb, xh, xa, ext, *refs):
+        w_refs = refs[:9]
+        sharp_ref, own_ref, key_ref, out_ref, x, bias, wide, lasts, q_buf, k_buf, v_buf = refs[9:]
         n = pl.program_id(0)
-        acc = jnp.dot(x_ref[:, 0:deep], w0[...], preferred_element_type=F32)
-        acc = acc + jnp.dot(x_ref[:, deep : 2 * deep], w1[...], preferred_element_type=F32)
-        acc = acc + jnp.dot(x_ref[:, 2 * deep : 3 * deep], w2[...], preferred_element_type=F32)
-        part = lax.broadcasted_iota(jnp.int32, (parts, deep), 0)
-        place = lax.broadcasted_iota(jnp.int32, (parts, deep), 1)
-        lasts = []
-        for k in range(2):
-            pick = jnp.where(place == 8 * part + (2 * n + k) % 8, 1.0, 0.0).astype(BF)
-            lasts.append(jnp.dot(pick, last_ref[...], preferred_element_type=F32).astype(BF))
-        acc = acc + jnp.dot(x_ref[:, 3 * deep :], jnp.concatenate(lasts, axis=1), preferred_element_type=F32)
-        col = lax.broadcasted_iota(jnp.int32, (1, block), 1) + n * block
-        is_key = (col >= head_width) & (col < 2 * head_width)
-        out_ref[...] = (acc * jnp.where(is_key, sharp_ref[...], 1.0)).astype(BF)
-
-    def last_tile(n):
-        j = n // 4
-        return (0, jnp.where(j < eights, 40 * j + 39, 117 + j))
-
-    return pl.pallas_call(
-        body,
-        grid=(pairs,),
-        out_shape=jax.ShapeDtypeStruct((rows, pairs * block), BF),
-        in_specs=[
-            VMEM,
-            pl.BlockSpec((deep, block), lambda n: (0, n)),
-            pl.BlockSpec((deep, block), lambda n: (0, n + 20)),
-            pl.BlockSpec((deep, block), lambda n: (0, n + 40)),
-            pl.BlockSpec((deep, 128), last_tile),
-            VMEM,
-        ],
-        out_specs=pl.BlockSpec((rows, block), lambda n: (0, n)),
-        compiler_params=pltpu.CompilerParams(vmem_limit_bytes=32 << 20),
-        name="project",
-    )(normed, packed, packed, packed, packed, sharp)
-
-
-def attend(before, here, after, own_ids, key_ids):
-    rows = here.shape[0]
-    scale = 1.0 / math.sqrt(HD)
-
-    def body(q_ref, kb, kh, ka, vb, vh, va, own_ref, key_ref, out_ref, bias):
-        @pl.when(pl.program_id(0) == 0)
+        head = jnp.minimum(n, HEADS - 1)
+
+        @pl.when(n == 0)
         def _():
+            x[0:rows] = xb[...]
+            x[rows : 2 * rows] = xh[...]
+            x[2 * rows :] = xa[...]
             bias[...] = jnp.where(own_ref[...] == key_ref[...], 0.0, -1e30)
-
-        q = q_ref[...]
-        parts = [
-            lax.dot_general(q, k[...], (((1,), (1,)), ((), ())), preferred_element_type=F32)
-            for k in (kb, kh, ka)
-        ]
-        logits = jnp.concatenate(parts, axis=1) * scale + bias[...]
+            for j in range(spare):
+                wide[j] = ext[:, j * 128 : (j + 1) * 128].astype(F32)
+            for j in range(spare):
+                for s in range(8):
+                    lasts[8 * j + s] = wide[j, pl.ds(s, parts, stride=8), :].astype(BF)
+            q_buf[1] = jnp.zeros((rows, HD), BF)
+            k_buf[1] = jnp.zeros((near, HD), BF)
+            v_buf[1] = jnp.zeros((near, HD), BF)
+
+        done = (n + 1) % 2
+        logits = lax.dot_general(
+            q_buf[done], k_buf[done], (((1,), (1,)), ((), ())), preferred_element_type=F32
+        )
+        logits = logits * scale + bias[...]
         peak = jnp.max(logits, axis=1, keepdims=True)
         weights = jnp.exp(logits - peak)
         total = jnp.sum(weights, axis=1, keepdims=True)
-        probs = weights.astype(BF)
-        value = jnp.concatenate([vb[...], vh[...], va[...]], axis=0)
-        out = jnp.dot(probs, value, preferred_element_type=F32)
-        out_ref[...] = (out / total).astype(BF)
-
-    q_spec = pl.BlockSpec((rows, HD), lambda h: (0, h))
-    k_here = pl.BlockSpec((rows, HD), lambda h: (0, h + HEADS))
-    v_here = pl.BlockSpec((rows, HD), lambda h: (0, h + 2 * HEADS))
-    k_near = pl.BlockSpec((rows, HD), lambda h: (0, h))
-    v_near = pl.BlockSpec((rows, HD), lambda h: (0, h + HEADS))
+        result = jnp.dot(weights.astype(BF), v_buf[done], preferred_element_type=F32)
+        out_ref[...] = (result / total).astype(BF)
+
+        q = jnp.zeros((rows, HD), F32)
+        kv = jnp.zeros((near, 2 * HD), F32)
+        for b in range(eights):
+            at = b * deep
+            q = q + jnp.dot(xh[:, at : at + deep], w_refs[b][...], preferred_element_type=F32)
+            both = jnp.concatenate([w_refs[3 + b][...], w_refs[6 + b][...]], axis=1)
+            kv = kv + jnp.dot(x[:, at : at + deep], both, preferred_element_type=F32)
+        at = eights * deep
+        q = q + jnp.dot(xh[:, at:], lasts[head], preferred_element_type=F32)
+        both = jnp.concatenate([lasts[head + HEADS], lasts[head + 2 * HEADS]], axis=1)
+        kv = kv + jnp.dot(x[:, at:], both, preferred_element_type=F32)
+        new = n % 2
+        q_buf[new] = q.astype(BF)
+        k_buf[new] = (kv[:, :HD] * sharp_ref[...]).astype(BF)
+        v_buf[new] = kv[:, HD:].astype(BF)
+
+    def w_spec(b, kind):
+        first = spare + b * 3 * HEADS + kind * HEADS
+        return pl.BlockSpec((deep, HD), lambda n: (0, first + jnp.minimum(n, HEADS - 1)))
+
     return pl.pallas_call(
         body,
-        grid=(HEADS,),
+        grid=(HEADS + 1,),
         out_shape=jax.ShapeDtypeStruct((rows, HW), BF),
-        in_specs=[q_spec, k_near, k_here, k_near, v_near, v_here, v_near, VMEM, VMEM],
-        out_specs=q_spec,
-        scratch_shapes=[pltpu.VMEM((rows, 3 * rows), F32)],
-        name="attend",
-    )(here, before, here, after, before, here, after, own_ids, key_ids)
+        in_specs=[VMEM, VMEM, VMEM, pl.BlockSpec((deep, spare * 128), lambda n: (0, 0))]
+        + [w_spec(b, kind) for kind in range(3) for b in range(3)]
+        + [VMEM, VMEM, VMEM],
+        out_specs=pl.BlockSpec((rows, HD), lambda n: (0, jnp.maximum(n - 1, 0))),
+        scratch_shapes=[
+            pltpu.VMEM((near, width), BF),
+            pltpu.VMEM((rows, near), F32),
+            pltpu.VMEM((spare, deep, 128), F32),
+            pltpu.VMEM((8 * spare, parts, HD), BF),
+            pltpu.VMEM((2, rows, HD), BF),
+            pltpu.VMEM((2, near, HD), BF),
+            pltpu.VMEM((2, near, HD), BF),
+        ],
+        compiler_params=pltpu.CompilerParams(vmem_limit_bytes=48 << 20),
+        name="project_and_attend",
+    )(before, here, after, *([packed] * 10), sharp, own_ids, key_ids)
 
 
 def shards(
@@ -334,14 +347,15 @@
     wanted = jnp.arange(MT, dtype=jnp.int32) * holders + place
     ends = jnp.sum(jnp.where(ranks[None, :] <= ranks[:, None], counts[None, :], 0), axis=1)
     source = jnp.sum((ends[None, :] <= wanted[:, None]).astype(jnp.int32), axis=1)
-    held_score = jnp.take(recv_score, source).astype(F32)
-    sharp = jnp.repeat(0.5 + jax.nn.softplus(held_score), tile_len)[:, None]
-
-    normed = hold_and_norm(source, recv, ln_gain, parts)
-    here = project(normed, packed, sharp, HW)
-    near = here[:, HW : 3 * HW]
-    before = lax.ppermute(near, "dev", up)
-    after = lax.ppermute(near, "dev", down)
+    held_score = jnp.take(recv_score, source).reshape(1, MT)
+    near_score = jnp.concatenate(
+        [lax.ppermute(held_score, "dev", up), held_score, lax.ppermute(held_score, "dev", down)], axis=1
+    )
+    sharp = jnp.repeat(0.5 + jax.nn.softplus(near_score[0].astype(F32)), tile_len)[:, None]
+
+    here = hold_and_norm(source, recv, ln_gain, parts)
+    before = lax.ppermute(here, "dev", up)
+    after = lax.ppermute(here, "dev", down)
 
     all_ids = tile_image[0]
     places = own * MT - MT + jnp.arange(3 * MT, dtype=jnp.int32)
@@ -349,7 +363,7 @@
     near_ids = jnp.where(inside, jnp.take(all_ids, jnp.clip(places, 0, all_ids.shape[0] - 1)), -1)
     key_ids = jnp.repeat(near_ids, tile_len)
     own_ids = key_ids[held_rows : 2 * held_rows]
-    attended = attend(before, here, after, own_ids[:, None], key_ids[None, :])
+    attended = project_and_attend(before, here, after, packed, sharp, own_ids[:, None], key_ids[None, :])
     return (score_map, attended)
 
 

time: 228 us -> 220 us (0.965)
  local copies, waits for them, and re-layouts: 18.7 us -> 11.2 us
  starting transfers between devices: 31.3 us -> 35.7 us
  waiting for transfers between devices: 85.7 us -> 82.1 us
    all_to_all x1, waiting for transfers between devices: 0.01 us -> 30.4 us  [shards(): lax.all_to_all(send_score.reshape(holders, 1, 1), 'dev', split_axis=0, co...]
    all_gather x1, waiting for transfers between devices: 15.8 us -> 0.02 us  [shards(): packed = lax.all_gather(pack_rows(qkv_weight), axes, axis=0, tiled=True)]
    ppermute x2 -> x4, waiting for transfers between devices: 16.7 us -> 5.07 us  [the longest x1 5.06 us: shards(): lax.ppermute(held_score, 'dev', down)]
    ppermute x1, waiting for transfers between devices: 53.2 us -> 46.7 us  [shards(): right = lax.ppermute(edge(0), 'dev', down)]
    unnamed x37 -> x24, local copies, waits for them, and re-layouts: 6.96 us -> 3.65 us
    ppermute x2 -> x4, starting transfers between devices: 6.28 us -> 9.58 us  [the longest x1 3.34 us: shards(): lax.ppermute(held_score, 'dev', up)]
    slice x3 -> x0, local copies, waits for them, and re-layouts: 2.97 us -> none  [the longest x1 1.21 us: shards(): near = here[:, HW:3 * HW]]
  transfers between devices with their start and end apart: 9 -> 11, of which waited for: 4 -> 3; matrix products, arithmetic and copies ran while one was open for 6% -> 6% of each run, Pallas kernels for 16% -> 16%
where the time goes in v2:
time: 220 us; the launch traced here: 217 us
  waiting for transfers between devices  82.1 us (37%)
  Pallas kernels  69 us (31%)
  starting transfers between devices  35.7 us (16%)
  between operations  14.5 us (7%)
  local copies, waits for them, and re-layouts  11.2 us (5%)
  other arithmetic  4.76 us (2%)
    ppermute x1, waiting for transfers between devices, shards(): right = lax.ppermute(edge(0), 'dev', down)  46.7 us
    pallas_call x1, Pallas kernels, project_and_attend(): pl.pallas_call(body, grid=(HEADS + 1,), out_shape=jax.ShapeDtypeStruct((r...  32.2 us
    all_to_all x1, waiting for transfers between devices, shards(): lax.all_to_all(send_score.reshape(holders, 1, 1), 'dev', split_axis=0, co...  30.4 us
    pallas_call x1, Pallas kernels, conv_scores(): pl.pallas_call(body, grid=(height // step,), out_shape=jax.ShapeDtypeStru...  22.9 us
    all_to_all x1, starting transfers between devices, shards(): recv = lax.all_to_all(sent, 'dev', split_axis=0, concat_axis=0, tiled=True)  7.76 us
    pallas_call x1, Pallas kernels, hold_and_norm(): pl.pallas_call(body, out_shape=jax.ShapeDtypeStruct((rows, width), BF), i...  6.56 us
    all_to_all x1, starting transfers between devices, shards(): lax.all_to_all(send_score.reshape(holders, 1, 1), 'dev', split_axis=0, co...  6.26 us
    pallas_call x1, Pallas kernels, send_order(): pl.pallas_call(body, out_shape=jax.ShapeDtypeStruct(tokens.shape, tokens....  5.7 us
  transfers between devices with their start and end apart: 11, of which 3 were waited for; matrix products, arithmetic and copies ran while one was open for 6% of the time, Pallas kernels for 16%

profile of v2, /device:TPU:97, one launch (start us, length us, event | category | flops | bytes accessed | tf_op | source)
XLA Modules:
  0.0 217.4 jit_solution(3444266404625263566)
XLA Ops:
  7.2 0.0 copy-start
  7.2 0.0 all-gather.2.cloned.1.call-start
  7.2 1.7 pack_rows.1
  8.9 0.0 all-gather.2.cloned.1.call-update
  8.9 5.7 %send_order.1 = bf16[32,24,3200]{2,1,0:T(8,128)(2,1)} custom-call(s32[32]{0:T(128)} %bitcast.68, s32[32]{0:T(128)} %bitcast.66, s32[1]{0:T(128)} %bitcast.11.own_ref, bf16[32,24,3200]{2,1,0:T(8,128)(2,1)} %tok_ref.1), custom_call_target="tpu_custom_call" | custom-call | tf_op jit(solution)/shard_map/send_order/pallas_call | solution.py:48
  14.7 0.0 copy-start.7
  14.7 0.0 copy-start.8
  14.7 0.0 copy-start.9
  14.7 0.0 copy-start.6
  14.7 0.0 copy-start.3
  14.7 0.0 copy-start.4
  14.7 0.0 copy-start.5
  14.7 7.8 %all-to-all-start = ((bf16[32,24,3200]{2,1,0:T(8,128)(2,1)}), bf16[32,24,3200]{2,1,0:T(8,128)(2,1)}, u32[]{:S(2)}, u32[]{:S(2)}) async-start(bf16[32,24,3200]{2,1,0:T(8,128)(2,1)} %send_order.1), calls=%async_computation | async-start | bytes 9830400 | tf_op jit(solution)/shard_map/all_to_all | solution.py:319
  22.5 0.9 fusion.10
  23.4 3.1 %collective-permute-start = (bf16[1,128,256]{2,1,0:T(8,128)(2,1)S(1)}, bf16[1,128,256]{2,1,0:T(8,128)(2,1)S(1)}, u32[]{:S(2)}, u32[]{:S(2)}) collective-permute-start(bf16[1,128,256]{2,1,0:T(8,128)(2,1)S(1)} %get-tuple-element.9), channel_id=1, source_target_pairs={{0,32},{32,64},{64,96},{1,33},{33,65},{65,97},{2,34},{34,66},{66,9... | collective-permute-start | bytes 196616 | tf_op jit(solution)/shard_map/ppermute | solution.py:324
  26.5 1.3 collective-permute-start.1
  27.8 1.1 fusion.9
  29.0 0.6 reshape.175.gain_ref
  29.6 0.7 fusion
  30.3 0.1 select_reduce_fusion
  30.4 0.6 fusion.8
  31.1 0.7 gather_fusion
  31.8 0.7 multiply_add_fusion
  32.5 0.1 select_reduce_fusion.1
  32.6 0.7 convert_reduce_fusion.src_ref
  33.3 0.6 fusion.2
  34.0 0.0 collective-permute-done.top_ref
  34.0 0.0 collective-permute-done.1.bottom_ref
  34.1 2.6 %collective-permute-start.3 = (bf16[66,256]{1,0:T(8,128)(2,1)S(1)}, bf16[66,256]{1,0:T(8,128)(2,1)S(1)}, u32[]{:S(2)}, u32[]{:S(2)}) collective-permute-start(bf16[66,256]{1,0:T(8,128)(2,1)S(1)} %pad_maximum_fusion.3), channel_id=1, source_target_pairs={{1,0},{2,1},{3,2},{4,3},{5,4},{6,5},{7,6},{8,7},{9,8},{10,9},{11,1... | collective-permute-start | bytes 101384 | tf_op jit(solution)/shard_map/ppermute | solution.py:332
  36.7 5.1 %collective-permute-start.2 = (bf16[66,256]{1,0:T(8,128)(2,1)S(1)}, bf16[66,256]{1,0:T(8,128)(2,1)S(1)}, u32[]{:S(2)}, u32[]{:S(2)}) collective-permute-start(bf16[66,256]{1,0:T(8,128)(2,1)S(1)} %pad_maximum_fusion.2), channel_id=1, source_target_pairs={{0,1},{1,2},{2,3},{3,4},{4,5},{5,6},{6,7},{7,8},{8,9},{9,10},{10,1... | collective-permute-start | bytes 101384 | tf_op jit(solution)/shard_map/ppermute | solution.py:331
  41.8 46.7 %collective-permute-done.3 = bf16[66,256]{1,0:T(8,128)(2,1)S(1)} collective-permute-done((bf16[66,256]{1,0:T(8,128)(2,1)S(1)}, bf16[66,256]{1,0:T(8,128)(2,1)S(1)}, u32[]{:S(2)}, u32[]{:S(2)}) %collective-permute-start.3) | collective-permute-done | bytes 33824 | tf_op jit(solution)/shard_map/ppermute | solution.py:332
  88.4 0.0 collective-permute-done.2
  88.5 0.0 copy-start.2
  88.5 2.3 %copy-done.2 = bf16[64,128,256]{2,1,0:T(8,128)(2,1)S(1)} copy-done((bf16[64,128,256]{2,1,0:T(8,128)(2,1)S(1)}, bf16[64,128,256]{2,1,0:T(8,128)(2,1)}, u32[]{:S(2)}) %copy-start.2) | copy-done | bytes 4194328
  90.8 22.9 %conv_scores.1 = f32[8,8,128]{2,1,0:T(8,128)} custom-call(bf16[64,128,256]{2,1,0:T(8,128)(2,1)S(1)} %copy-done.2, bf16[1,128,256]{2,1,0:T(8,128)(2,1)S(1)} %collective-permute-done.top_ref, bf16[1,128,256]{2,1,0:T(8,128)(2,1)S(1)} %collective-permute-done.1.bottom_ref, bf16[64,768]{1,0:T(8,128)(2,1)S(1)} %get-tuple-element.20.left_ref, ...), custom_call_target="tpu_custom_call" | custom-call | tf_op jit(solution)/shard_map/conv_scores/pallas_call | solution.py:170
  113.7 1.5 gather_fusion.1
  115.2 0.6 fusion.7
  115.9 0.0 all-to-all-done.recv_ref
  115.9 6.6 %hold_and_norm.1.xh = bf16[192,3200]{1,0:T(8,128)(2,1)} custom-call(s32[8]{0:T(128)} %convert_reduce_fusion.src_ref, bf16[32,24,3200]{2,1,0:T(8,128)(2,1)} %all-to-all-done.recv_ref, f32[1,3200]{1,0:T(1,128)} %reshape.175.gain_ref, s32[25,128]{1,0:T(8,128)} %constant.81.clone.table_ref), custom_call_target="tpu_custom_call" | custom-call | tf_op jit(solution)/shard_map/hold_and_norm/pallas_call | solution.py:99
  122.4 2.0 collective-permute-start.4
  124.5 2.3 %collective-permute-start.5 = (bf16[192,3200]{1,0:T(8,128)(2,1)}, bf16[192,3200]{1,0:T(8,128)(2,1)S(1)}, u32[]{:S(2)}, u32[]{:S(2)}) collective-permute-start(bf16[192,3200]{1,0:T(8,128)(2,1)} %hold_and_norm.1.xh), channel_id=1, source_target_pairs={{1,0},{2,1},{3,2},{4,3},{5,4},{6,5},{7,6},{8,7},{9,8},{10,9},{11,1... | collective-permute-start | bytes 3686408 | tf_op jit(solution)/shard_map/ppermute | solution.py:358
  126.8 0.7 gather_fusion.3
  127.6 0.1 slice.61
  127.6 0.1 broadcast_in_dim.74
  127.7 0.1 broadcast_in_dim.77.refs_10_
  127.8 0.7 copy.32
  128.5 6.3 %all-to-all-start.1 = ((bf16[32,1,1]{2,1,0:T(2,128)(2,1)}), bf16[32,1,1]{2,1,0:T(2,128)(2,1)S(1)}, u32[]{:S(2)}, u32[]{:S(2)}) async-start(bf16[32,1,1]{2,1,0:T(2,128)(2,1)} %copy.32), calls=%async_computation.1 | async-start | bytes 32768 | tf_op jit(solution)/shard_map/all_to_all | solution.py:342
  134.8 0.1 broadcast_in_dim.76
  134.9 0.1 broadcast_in_dim_reshape.7.refs_11_
  135.0 30.4 %all-to-all-done.1 = bf16[32,1,1]{2,1,0:T(2,128)(2,1)S(1)} async-done(((bf16[32,1,1]{2,1,0:T(2,128)(2,1)}), bf16[32,1,1]{2,1,0:T(2,128)(2,1)S(1)}, u32[]{:S(2)}, u32[]{:S(2)}) %all-to-all-start.1) | async-done | bytes 96 | tf_op jit(solution)/shard_map/all_to_all | solution.py:342
  165.3 0.3 reduce
  165.7 0.6 gather_fusion.2
  166.3 3.3 %collective-permute-start.6 = (bf16[1,8]{1,0:T(2,128)(2,1)S(1)}, bf16[1,8]{1,0:T(2,128)(2,1)S(1)}, u32[]{:S(2)}, u32[]{:S(2)}) collective-permute-start(bf16[1,8]{1,0:T(2,128)(2,1)S(1)} %and_select_fusion.2), channel_id=1, source_target_pairs={{0,1},{1,2},{2,3},{3,4},{4,5},{5,6},{6,7},{7,8},{8,9},{9,10},{10,1... | collective-permute-start | bytes 56 | tf_op jit(solution)/shard_map/ppermute | solution.py:352
  169.7 1.9 collective-permute-start.7
  171.6 0.0 collective-permute-done.6
  171.6 5.1 %collective-permute-done.7 = bf16[1,8]{1,0:T(2,128)(2,1)S(1)} collective-permute-done((bf16[1,8]{1,0:T(2,128)(2,1)S(1)}, bf16[1,8]{1,0:T(2,128)(2,1)S(1)}, u32[]{:S(2)}, u32[]{:S(2)}) %collective-permute-start.7) | collective-permute-done | bytes 48 | tf_op jit(solution)/shard_map/ppermute | solution.py:352
  176.7 0.1 fusion.4
  176.8 0.1 broadcast_in_dim.72
  176.8 0.2 broadcast_in_dim_reshape.8.refs_9_
  177.0 0.0 collective-permute-done.4.xb
  177.0 0.0 collective-permute-done.5.xa
  177.0 0.0 all-gather.2.cloned.1.call-done.ext.refs_0_.refs_1_.refs_2_.refs_3_.refs_4_.refs_5_.refs_6_.refs_7_.refs_8_
  177.1 1.3 copy-done.1
  178.3 32.2 %project_and_attend.1 = bf16[192,1664]{1,0:T(8,128)(2,1)} custom-call(bf16[192,3200]{1,0:T(8,128)(2,1)S(1)} %collective-permute-done.4.xb, bf16[192,3200]{1,0:T(8,128)(2,1)S(1)} %copy-done.1, bf16[192,3200]{1,0:T(8,128)(2,1)S(1)} %collective-permute-done.5.xa, ...), custom_call_target="tpu_custom_call" | custom-call | tf_op jit(solution)/shard_map/project_and_attend/pallas_call | solution.py:275
  (28 shorter events, 0.2 us)
Async XLA Ops:
  7.2 119.7 %copy-start = (s32[1,256]{1,0:T(1,128)S(1)}, s32[1,256]{1,0:T(1,128)}, u32[]{:S(2)}) copy-start(s32[1,256]{1,0:T(1,128)} %param.20) | copy-start | bytes 3076
  7.2 169.9 %all-gather.2.cloned.1.call-start = ((), (), s32[]{:S(2)}) async-start(), calls=%async_computation.2 | async-start | bytes 32231424 | tf_op jit(solution)/shard_map/all_gather | solution.py:321
  14.7 14.4 %copy-start.7 = (f32[3200]{0:T(1024)S(1)}, f32[3200]{0:T(1024)}, u32[]{:S(2)}) copy-start(f32[3200]{0:T(1024)} %param.21) | copy-start | bytes 38404
  14.7 15.0 %copy-start.8 = (s32[1,32]{1,0:T(1,128)S(1)}, s32[1,32]{1,0:T(1,128)}, u32[]{:S(2)}) copy-start(s32[1,32]{1,0:T(1,128)} %param.19) | copy-start | bytes 388
  14.7 15.0 %copy-start.9 = (s32[1,32]{1,0:T(1,128)S(1)}, s32[1,32]{1,0:T(1,128)}, u32[]{:S(2)}) copy-start(s32[1,32]{1,0:T(1,128)} %param.18) | copy-start | bytes 388
  14.7 16.4 %copy-start.6 = (s32[1,32]{1,0:T(1,128)S(1)}, s32[1,32]{1,0:T(1,128)}, u32[]{:S(2)}) copy-start(s32[1,32]{1,0:T(1,128)} %param.17) | copy-start | bytes 388
  14.7 73.8 %copy-start.3 = (bf16[2304,256]{1,0:T(8,128)(2,1)S(1)}, bf16[2304,256]{1,0:T(8,128)(2,1)}, u32[]{:S(2)}) copy-start(bf16[2304,256]{1,0:T(8,128)(2,1)} %w_ref.2) | copy-start | bytes 3538948
  14.7 73.8 %copy-start.4 = (f32[256]{0:T(256)S(1)}, f32[256]{0:T(256)}, u32[]{:S(2)}) copy-start(f32[256]{0:T(256)} %param.14) | copy-start | bytes 3076
  14.7 73.8 %copy-start.5 = (f32[256]{0:T(256)S(1)}, f32[256]{0:T(256)}, u32[]{:S(2)}) copy-start(f32[256]{0:T(256)} %param.15) | copy-start | bytes 3076
  14.7 101.1 %all-to-all-start = ((bf16[32,24,3200]{2,1,0:T(8,128)(2,1)}), bf16[32,24,3200]{2,1,0:T(8,128)(2,1)}, u32[]{:S(2)}, u32[]{:S(2)}) async-start(bf16[32,24,3200]{2,1,0:T(8,128)(2,1)} %send_order.1), calls=%async_computation | async-start | bytes 9830400 | tf_op jit(solution)/shard_map/all_to_all | solution.py:319
  23.4 10.6 %collective-permute-start = (bf16[1,128,256]{2,1,0:T(8,128)(2,1)S(1)}, bf16[1,128,256]{2,1,0:T(8,128)(2,1)S(1)}, u32[]{:S(2)}, u32[]{:S(2)}) collective-permute-start(bf16[1,128,256]{2,1,0:T(8,128)(2,1)S(1)} %get-tuple-element.9), channel_id=1, source_target_pairs={{0,32},{32,64},{64,96},{1,33},{33,65},{65,97},{2,34},{34,66},{66,9... | collective-permute-start | bytes 196616 | tf_op jit(solution)/shard_map/ppermute | solution.py:324
  26.5 7.5 %collective-permute-start.1 = (bf16[1,128,256]{2,1,0:T(8,128)(2,1)S(1)}, bf16[1,128,256]{2,1,0:T(8,128)(2,1)S(1)}, u32[]{:S(2)}, u32[]{:S(2)}) collective-permute-start(bf16[1,128,256]{2,1,0:T(8,128)(2,1)S(1)} %get-tuple-element.8), channel_id=1, source_target_pairs={{32,0},{64,32},{96,64},{33,1},{65,33},{97,65},{34,2},{66,34},{98,6... | collective-permute-start | bytes 196616 | tf_op jit(solution)/shard_map/ppermute | solution.py:325
  34.1 54.4 %collective-permute-start.3 = (bf16[66,256]{1,0:T(8,128)(2,1)S(1)}, bf16[66,256]{1,0:T(8,128)(2,1)S(1)}, u32[]{:S(2)}, u32[]{:S(2)}) collective-permute-start(bf16[66,256]{1,0:T(8,128)(2,1)S(1)} %pad_maximum_fusion.3), channel_id=1, source_target_pairs={{1,0},{2,1},{3,2},{4,3},{5,4},{6,5},{7,6},{8,7},{9,8},{10,9},{11,1... | collective-permute-start | bytes 101384 | tf_op jit(solution)/shard_map/ppermute | solution.py:332
  36.7 51.8 %collective-permute-start.2 = (bf16[66,256]{1,0:T(8,128)(2,1)S(1)}, bf16[66,256]{1,0:T(8,128)(2,1)S(1)}, u32[]{:S(2)}, u32[]{:S(2)}) collective-permute-start(bf16[66,256]{1,0:T(8,128)(2,1)S(1)} %pad_maximum_fusion.2), channel_id=1, source_target_pairs={{0,1},{1,2},{2,3},{3,4},{4,5},{5,6},{6,7},{7,8},{8,9},{9,10},{10,1... | collective-permute-start | bytes 101384 | tf_op jit(solution)/shard_map/ppermute | solution.py:331
  88.5 2.3 %copy-start.2 = (bf16[64,128,256]{2,1,0:T(8,128)(2,1)S(1)}, bf16[64,128,256]{2,1,0:T(8,128)(2,1)}, u32[]{:S(2)}) copy-start(bf16[64,128,256]{2,1,0:T(8,128)(2,1)} %canvas_ref.1) | copy-start | bytes 12582916
  113.7 14.1 %copy-start.10 = (s32[8]{0:T(128)S(1)}, s32[8]{0:T(128)}, u32[]{:S(2)}) copy-start(s32[8]{0:T(128)} %convert_reduce_fusion.src_ref) | copy-start | bytes 100
  122.4 54.5 %collective-permute-start.4 = (bf16[192,3200]{1,0:T(8,128)(2,1)}, bf16[192,3200]{1,0:T(8,128)(2,1)S(1)}, u32[]{:S(2)}, u32[]{:S(2)}) collective-permute-start(bf16[192,3200]{1,0:T(8,128)(2,1)} %hold_and_norm.1.xh), channel_id=1, source_target_pairs={{0,1},{1,2},{2,3},{3,4},{4,5},{5,6},{6,7},{7,8},{8,9},{9,10},{10,1... | collective-permute-start | bytes 3686408 | tf_op jit(solution)/shard_map/ppermute | solution.py:357
  124.5 52.5 %collective-permute-start.5 = (bf16[192,3200]{1,0:T(8,128)(2,1)}, bf16[192,3200]{1,0:T(8,128)(2,1)S(1)}, u32[]{:S(2)}, u32[]{:S(2)}) collective-permute-start(bf16[192,3200]{1,0:T(8,128)(2,1)} %hold_and_norm.1.xh), channel_id=1, source_target_pairs={{1,0},{2,1},{3,2},{4,3},{5,4},{6,5},{7,6},{8,7},{9,8},{10,9},{11,1... | collective-permute-start | bytes 3686408 | tf_op jit(solution)/shard_map/ppermute | solution.py:358
  128.5 36.8 %all-to-all-start.1 = ((bf16[32,1,1]{2,1,0:T(2,128)(2,1)}), bf16[32,1,1]{2,1,0:T(2,128)(2,1)S(1)}, u32[]{:S(2)}, u32[]{:S(2)}) async-start(bf16[32,1,1]{2,1,0:T(2,128)(2,1)} %copy.32), calls=%async_computation.1 | async-start | bytes 32768 | tf_op jit(solution)/shard_map/all_to_all | solution.py:342
  166.3 5.3 %collective-permute-start.6 = (bf16[1,8]{1,0:T(2,128)(2,1)S(1)}, bf16[1,8]{1,0:T(2,128)(2,1)S(1)}, u32[]{:S(2)}, u32[]{:S(2)}) collective-permute-start(bf16[1,8]{1,0:T(2,128)(2,1)S(1)} %and_select_fusion.2), channel_id=1, source_target_pairs={{0,1},{1,2},{2,3},{3,4},{4,5},{5,6},{6,7},{7,8},{8,9},{9,10},{10,1... | collective-permute-start | bytes 56 | tf_op jit(solution)/shard_map/ppermute | solution.py:352
  169.7 7.0 %collective-permute-start.7 = (bf16[1,8]{1,0:T(2,128)(2,1)S(1)}, bf16[1,8]{1,0:T(2,128)(2,1)S(1)}, u32[]{:S(2)}, u32[]{:S(2)}) collective-permute-start(bf16[1,8]{1,0:T(2,128)(2,1)S(1)} %and_select_fusion.2), channel_id=1, source_target_pairs={{1,0},{2,1},{3,2},{4,3},{5,4},{6,5},{7,6},{8,7},{9,8},{10,9},{11,1... | collective-permute-start | bytes 56 | tf_op jit(solution)/shard_map/ppermute | solution.py:352
  177.0 1.3 copy-start.1
Sparse Core Ops, SparseCore 0:
  11.5 155.3 all-gather.1

commit v3 on v2

--- a/solution.py
+++ b/solution.py
@@ -338,22 +338,20 @@
     slot_for = (place_of - first) & (holders - 1)
     cells = jnp.take(tile_cell[0], slot_for)
     send_score = jnp.take(score_map.reshape(-1), cells).astype(BF)
+    send_score = jnp.stack([jnp.roll(send_score, 1), send_score, jnp.roll(send_score, -1)], axis=1)
     recv, send_score = lax.optimization_barrier((recv, send_score))
-    recv_score = lax.all_to_all(
-        send_score.reshape(holders, 1, 1), "dev", split_axis=0, concat_axis=0, tiled=True
-    ).reshape(holders)
-
-    place = jnp.sum(jnp.where(order == own, ranks, 0))
-    wanted = jnp.arange(MT, dtype=jnp.int32) * holders + place
+    recv_score = lax.all_to_all(send_score, "dev", split_axis=0, concat_axis=0, tiled=True)
+
+    near_holders = jnp.clip(own + jnp.arange(-1, 2, dtype=jnp.int32), 0, holders - 1)
+    places = jnp.sum(jnp.where(order[None, :] == near_holders[:, None], ranks[None, :], 0), axis=1)
+    wanted = jnp.arange(MT, dtype=jnp.int32)[None, :] * holders + places[:, None]
     ends = jnp.sum(jnp.where(ranks[None, :] <= ranks[:, None], counts[None, :], 0), axis=1)
-    source = jnp.sum((ends[None, :] <= wanted[:, None]).astype(jnp.int32), axis=1)
-    held_score = jnp.take(recv_score, source).reshape(1, MT)
-    near_score = jnp.concatenate(
-        [lax.ppermute(held_score, "dev", up), held_score, lax.ppermute(held_score, "dev", down)], axis=1
-    )
-    sharp = jnp.repeat(0.5 + jax.nn.softplus(near_score[0].astype(F32)), tile_len)[:, None]
-
-    here = hold_and_norm(source, recv, ln_gain, parts)
+    source = jnp.sum((ends <= wanted[:, :, None]).astype(jnp.int32), axis=2)
+    picked = source[:, :, None] == ranks
+    near_score = jnp.sum(jnp.where(picked, recv_score.astype(F32).T[:, None, :], 0.0), axis=2)
+    sharp = jnp.repeat(0.5 + jax.nn.softplus(near_score.reshape(-1)), tile_len)[:, None]
+
+    here = hold_and_norm(source[1], recv, ln_gain, parts)
     before = lax.ppermute(here, "dev", up)
     after = lax.ppermute(here, "dev", down)
 

time: 220 us -> 211 us (0.959)
  starting transfers between devices: 35.7 us -> 30.5 us
  waiting for transfers between devices: 82.1 us -> 77.9 us
    ppermute x2 -> x0, starting transfers between devices: 5.26 us -> none  [the longest x1 3.34 us: shards(): lax.ppermute(held_score, 'dev', up)]
    ppermute x2 -> x0, waiting for transfers between devices: 5.06 us -> none  [the longest x1 5.06 us: shards(): lax.ppermute(held_score, 'dev', down)]
  transfers between devices with their start and end apart: 11 -> 9, of which waited for: 3 -> 3; matrix products, arithmetic and copies ran while one was open for 6% -> 6% of each run, Pallas kernels for 16% -> 17%
where the time goes in v3:
time: 211 us; the launch traced here: 207 us
  waiting for transfers between devices  77.9 us (37%)
  Pallas kernels  69 us (33%)
  starting transfers between devices  30.5 us (14%)
  between operations  14.4 us (7%)
  local copies, waits for them, and re-layouts  12 us (6%)
  other arithmetic  3.71 us (2%)
    ppermute x1, waiting for transfers between devices, shards(): right = lax.ppermute(edge(0), 'dev', down)  47.7 us
    pallas_call x1, Pallas kernels, project_and_attend(): pl.pallas_call(body, grid=(HEADS + 1,), out_shape=jax.ShapeDtypeStruct((r...  32.2 us
    all_to_all x1, waiting for transfers between devices, shards(): lax.all_to_all(send_score, 'dev', split_axis=0, concat_axis=0, tiled=True)  29.2 us
    pallas_call x1, Pallas kernels, conv_scores(): pl.pallas_call(body, grid=(height // step,), out_shape=jax.ShapeDtypeStru...  22.9 us
    all_to_all x1, starting transfers between devices, shards(): recv = lax.all_to_all(sent, 'dev', split_axis=0, concat_axis=0, tiled=True)  7.78 us
    pallas_call x1, Pallas kernels, hold_and_norm(): pl.pallas_call(body, out_shape=jax.ShapeDtypeStruct((rows, width), BF), i...  6.5 us
    all_to_all x1, starting transfers between devices, shards(): lax.all_to_all(send_score, 'dev', split_axis=0, concat_axis=0, tiled=True)  6.23 us
    pallas_call x1, Pallas kernels, send_order(): pl.pallas_call(body, out_shape=jax.ShapeDtypeStruct(tokens.shape, tokens....  5.69 us
  transfers between devices with their start and end apart: 9, of which 3 were waited for; matrix products, arithmetic and copies ran while one was open for 6% of the time, Pallas kernels for 17%

profile of v3, /device:TPU:97, one launch (start us, length us, event | category | flops | bytes accessed | tf_op | source)
XLA Modules:
  0.0 207.4 jit_solution(5919415389378365430)
XLA Ops:
  7.2 0.0 copy-start
  7.2 0.0 all-gather.2.cloned.1.call-start
  7.2 1.7 pack_rows.1
  8.9 0.0 all-gather.2.cloned.1.call-update
  8.9 5.7 %send_order.1 = bf16[32,24,3200]{2,1,0:T(8,128)(2,1)} custom-call(s32[32]{0:T(128)} %bitcast.74, s32[32]{0:T(128)} %bitcast.76, s32[1]{0:T(128)} %bitcast.12.own_ref, bf16[32,24,3200]{2,1,0:T(8,128)(2,1)} %tok_ref.1), custom_call_target="tpu_custom_call" | custom-call | tf_op jit(solution)/shard_map/send_order/pallas_call | solution.py:48
  14.6 0.0 copy-start.7
  14.7 0.0 copy-start.8
  14.7 0.0 copy-start.9
  14.7 0.0 copy-start.6
  14.7 0.0 copy-start.3
  14.7 0.0 copy-start.4
  14.7 0.0 copy-start.5
  14.7 7.8 %all-to-all-start = ((bf16[32,24,3200]{2,1,0:T(8,128)(2,1)}), bf16[32,24,3200]{2,1,0:T(8,128)(2,1)}, u32[]{:S(2)}, u32[]{:S(2)}) async-start(bf16[32,24,3200]{2,1,0:T(8,128)(2,1)} %send_order.1), calls=%async_computation | async-start | bytes 9830400 | tf_op jit(solution)/shard_map/all_to_all | solution.py:319
  22.5 0.9 fusion.8
  23.4 3.1 %collective-permute-start = (bf16[1,128,256]{2,1,0:T(8,128)(2,1)S(1)}, bf16[1,128,256]{2,1,0:T(8,128)(2,1)S(1)}, u32[]{:S(2)}, u32[]{:S(2)}) collective-permute-start(bf16[1,128,256]{2,1,0:T(8,128)(2,1)S(1)} %get-tuple-element.11), channel_id=1, source_target_pairs={{0,32},{32,64},{64,96},{1,33},{33,65},{65,97},{2,34},{34,66},{66,9... | collective-permute-start | bytes 196616 | tf_op jit(solution)/shard_map/ppermute | solution.py:324
  26.5 1.3 collective-permute-start.1
  27.8 1.1 fusion.7
  29.0 0.6 reshape.189.gain_ref
  29.6 0.6 fusion
  30.3 0.1 select_reduce_fusion
  30.4 0.7 fusion.5
  31.1 0.7 gather_fusion
  31.8 0.1 select_reduce_fusion.1
  31.9 0.2 select_reduce_fusion.3
  32.1 0.1 broadcast_add_fusion
  32.1 0.2 convert_reduce_fusion
  32.4 0.5 slice_bitcast_fusion.4.src_ref
  32.9 0.0 collective-permute-done.top_ref
  32.9 0.0 collective-permute-done.1.bottom_ref
  33.0 2.6 %collective-permute-start.3 = (bf16[66,256]{1,0:T(8,128)(2,1)S(1)}, bf16[66,256]{1,0:T(8,128)(2,1)S(1)}, u32[]{:S(2)}, u32[]{:S(2)}) collective-permute-start(bf16[66,256]{1,0:T(8,128)(2,1)S(1)} %pad_maximum_fusion.3), channel_id=1, source_target_pairs={{1,0},{2,1},{3,2},{4,3},{5,4},{6,5},{7,6},{8,7},{9,8},{10,9},{11,1... | collective-permute-start | bytes 101384 | tf_op jit(solution)/shard_map/ppermute | solution.py:332
  35.6 5.1 %collective-permute-start.2 = (bf16[66,256]{1,0:T(8,128)(2,1)S(1)}, bf16[66,256]{1,0:T(8,128)(2,1)S(1)}, u32[]{:S(2)}, u32[]{:S(2)}) collective-permute-start(bf16[66,256]{1,0:T(8,128)(2,1)S(1)} %pad_maximum_fusion.2), channel_id=1, source_target_pairs={{0,1},{1,2},{2,3},{3,4},{4,5},{5,6},{6,7},{7,8},{8,9},{9,10},{10,1... | collective-permute-start | bytes 101384 | tf_op jit(solution)/shard_map/ppermute | solution.py:331
  40.7 47.7 %collective-permute-done.3 = bf16[66,256]{1,0:T(8,128)(2,1)S(1)} collective-permute-done((bf16[66,256]{1,0:T(8,128)(2,1)S(1)}, bf16[66,256]{1,0:T(8,128)(2,1)S(1)}, u32[]{:S(2)}, u32[]{:S(2)}) %collective-permute-start.3) | collective-permute-done | bytes 33824 | tf_op jit(solution)/shard_map/ppermute | solution.py:332
  88.4 0.0 collective-permute-done.2
  88.5 0.0 copy-start.2
  88.5 2.3 %copy-done.2 = bf16[64,128,256]{2,1,0:T(8,128)(2,1)S(1)} copy-done((bf16[64,128,256]{2,1,0:T(8,128)(2,1)S(1)}, bf16[64,128,256]{2,1,0:T(8,128)(2,1)}, u32[]{:S(2)}) %copy-start.2) | copy-done | bytes 4194328
  90.8 22.9 %conv_scores.1 = f32[8,8,128]{2,1,0:T(8,128)} custom-call(bf16[64,128,256]{2,1,0:T(8,128)(2,1)S(1)} %copy-done.2, bf16[1,128,256]{2,1,0:T(8,128)(2,1)S(1)} %collective-permute-done.top_ref, bf16[1,128,256]{2,1,0:T(8,128)(2,1)S(1)} %collective-permute-done.1.bottom_ref, bf16[64,768]{1,0:T(8,128)(2,1)S(1)} %get-tuple-element.26.left_ref, ...), custom_call_target="tpu_custom_call" | custom-call | tf_op jit(solution)/shard_map/conv_scores/pallas_call | solution.py:170
  113.7 1.5 gather_fusion.1
  115.2 0.6 fusion.11
  115.8 0.1 fusion.12
  115.9 0.7 maximum_bitcast_fusion
  116.6 0.7 maximum_bitcast_fusion.1
  117.3 0.0 all-to-all-done.recv_ref
  117.3 6.5 %hold_and_norm.1.xh = bf16[192,3200]{1,0:T(8,128)(2,1)} custom-call(s32[8]{0:T(128)} %slice_bitcast_fusion.4.src_ref, bf16[32,24,3200]{2,1,0:T(8,128)(2,1)} %all-to-all-done.recv_ref, f32[1,3200]{1,0:T(1,128)} %reshape.189.gain_ref, s32[25,128]{1,0:T(8,128)} %constant.71.clone.table_ref), custom_call_target="tpu_custom_call" | custom-call | tf_op jit(solution)/shard_map/hold_and_norm/pallas_call | solution.py:99
  123.8 2.1 %collective-permute-start.4 = (bf16[192,3200]{1,0:T(8,128)(2,1)}, bf16[192,3200]{1,0:T(8,128)(2,1)S(1)}, u32[]{:S(2)}, u32[]{:S(2)}) collective-permute-start(bf16[192,3200]{1,0:T(8,128)(2,1)} %hold_and_norm.1.xh), channel_id=1, source_target_pairs={{0,1},{1,2},{2,3},{3,4},{4,5},{5,6},{6,7},{7,8},{8,9},{9,10},{10,1... | collective-permute-start | bytes 3686408 | tf_op jit(solution)/shard_map/ppermute | solution.py:355
  125.9 2.3 %collective-permute-start.5 = (bf16[192,3200]{1,0:T(8,128)(2,1)}, bf16[192,3200]{1,0:T(8,128)(2,1)S(1)}, u32[]{:S(2)}, u32[]{:S(2)}) collective-permute-start(bf16[192,3200]{1,0:T(8,128)(2,1)} %hold_and_norm.1.xh), channel_id=1, source_target_pairs={{1,0},{2,1},{3,2},{4,3},{5,4},{6,5},{7,6},{8,7},{9,8},{10,9},{11,1... | collective-permute-start | bytes 3686408 | tf_op jit(solution)/shard_map/ppermute | solution.py:356
  128.2 0.7 gather_fusion.2
  128.9 0.1 slice.85
  129.0 0.7 copy.34
  129.7 6.2 %all-to-all-start.1 = ((bf16[32,1,3]{2,1,0:T(2,128)(2,1)}), bf16[32,1,3]{2,1,0:T(2,128)(2,1)S(1)}, u32[]{:S(2)}, u32[]{:S(2)}) async-start(bf16[32,1,3]{2,1,0:T(2,128)(2,1)} %copy.34), calls=%async_computation.1 | async-start | bytes 32768 | tf_op jit(solution)/shard_map/all_to_all | solution.py:343
  135.9 0.1 broadcast_in_dim.109
  136.0 0.1 broadcast_in_dim.112.refs_10_
  136.1 0.1 broadcast_in_dim.111
  136.2 0.1 broadcast_in_dim_reshape.7.refs_11_
  136.3 29.2 %all-to-all-done.1 = bf16[32,1,3]{2,1,0:T(2,128)(2,1)S(1)} async-done(((bf16[32,1,3]{2,1,0:T(2,128)(2,1)}), bf16[32,1,3]{2,1,0:T(2,128)(2,1)S(1)}, u32[]{:S(2)}, u32[]{:S(2)}) %all-to-all-start.1) | async-done | bytes 224 | tf_op jit(solution)/shard_map/all_to_all | solution.py:343
  165.5 0.1 copy.35
  165.6 0.2 select_reduce_fusion.2
  165.8 0.1 reshape.190
  165.9 0.1 broadcast_in_dim.107
  166.0 0.2 broadcast_in_dim_reshape.8.refs_9_
  166.1 0.0 collective-permute-done.4.xb
  166.1 0.0 collective-permute-done.5.xa
  166.1 0.9 all-gather.2.cloned.1.call-done.ext.refs_0_.refs_1_.refs_2_.refs_3_.refs_4_.refs_5_.refs_6_.refs_7_.refs_8_
  167.1 1.3 copy-done.1
  168.4 32.2 %project_and_attend.1 = bf16[192,1664]{1,0:T(8,128)(2,1)} custom-call(bf16[192,3200]{1,0:T(8,128)(2,1)S(1)} %collective-permute-done.4.xb, bf16[192,3200]{1,0:T(8,128)(2,1)S(1)} %copy-done.1, bf16[192,3200]{1,0:T(8,128)(2,1)S(1)} %collective-permute-done.5.xa, ...), custom_call_target="tpu_custom_call" | custom-call | tf_op jit(solution)/shard_map/project_and_attend/pallas_call | solution.py:275
  (31 shorter events, 0.2 us)
Async XLA Ops:
  7.2 121.0 %copy-start = (s32[1,256]{1,0:T(1,128)S(1)}, s32[1,256]{1,0:T(1,128)}, u32[]{:S(2)}) copy-start(s32[1,256]{1,0:T(1,128)} %param.20) | copy-start | bytes 3076
  7.2 159.9 %all-gather.2.cloned.1.call-start = ((), (), s32[]{:S(2)}) async-start(), calls=%async_computation.2 | async-start | bytes 32231424 | tf_op jit(solution)/shard_map/all_gather | solution.py:321
  14.6 14.4 %copy-start.7 = (f32[3200]{0:T(1024)S(1)}, f32[3200]{0:T(1024)}, u32[]{:S(2)}) copy-start(f32[3200]{0:T(1024)} %param.21) | copy-start | bytes 38404
  14.7 15.0 %copy-start.8 = (s32[1,32]{1,0:T(1,128)S(1)}, s32[1,32]{1,0:T(1,128)}, u32[]{:S(2)}) copy-start(s32[1,32]{1,0:T(1,128)} %param.18) | copy-start | bytes 388
  14.7 15.6 %copy-start.9 = (s32[1,32]{1,0:T(1,128)S(1)}, s32[1,32]{1,0:T(1,128)}, u32[]{:S(2)}) copy-start(s32[1,32]{1,0:T(1,128)} %param.19) | copy-start | bytes 388
  14.7 16.4 %copy-start.6 = (s32[1,32]{1,0:T(1,128)S(1)}, s32[1,32]{1,0:T(1,128)}, u32[]{:S(2)}) copy-start(s32[1,32]{1,0:T(1,128)} %param.17) | copy-start | bytes 388
  14.7 73.8 %copy-start.3 = (bf16[2304,256]{1,0:T(8,128)(2,1)S(1)}, bf16[2304,256]{1,0:T(8,128)(2,1)}, u32[]{:S(2)}) copy-start(bf16[2304,256]{1,0:T(8,128)(2,1)} %w_ref.2) | copy-start | bytes 3538948
  14.7 73.8 %copy-start.4 = (f32[256]{0:T(256)S(1)}, f32[256]{0:T(256)}, u32[]{:S(2)}) copy-start(f32[256]{0:T(256)} %param.14) | copy-start | bytes 3076
  14.7 73.8 %copy-start.5 = (f32[256]{0:T(256)S(1)}, f32[256]{0:T(256)}, u32[]{:S(2)}) copy-start(f32[256]{0:T(256)} %param.15) | copy-start | bytes 3076
  14.7 102.6 %all-to-all-start = ((bf16[32,24,3200]{2,1,0:T(8,128)(2,1)}), bf16[32,24,3200]{2,1,0:T(8,128)(2,1)}, u32[]{:S(2)}, u32[]{:S(2)}) async-start(bf16[32,24,3200]{2,1,0:T(8,128)(2,1)} %send_order.1), calls=%async_computation | async-start | bytes 9830400 | tf_op jit(solution)/shard_map/all_to_all | solution.py:319
  23.4 9.5 %collective-permute-start = (bf16[1,128,256]{2,1,0:T(8,128)(2,1)S(1)}, bf16[1,128,256]{2,1,0:T(8,128)(2,1)S(1)}, u32[]{:S(2)}, u32[]{:S(2)}) collective-permute-start(bf16[1,128,256]{2,1,0:T(8,128)(2,1)S(1)} %get-tuple-element.11), channel_id=1, source_target_pairs={{0,32},{32,64},{64,96},{1,33},{33,65},{65,97},{2,34},{34,66},{66,9... | collective-permute-start | bytes 196616 | tf_op jit(solution)/shard_map/ppermute | solution.py:324
  26.5 6.4 %collective-permute-start.1 = (bf16[1,128,256]{2,1,0:T(8,128)(2,1)S(1)}, bf16[1,128,256]{2,1,0:T(8,128)(2,1)S(1)}, u32[]{:S(2)}, u32[]{:S(2)}) collective-permute-start(bf16[1,128,256]{2,1,0:T(8,128)(2,1)S(1)} %get-tuple-element.10), channel_id=1, source_target_pairs={{32,0},{64,32},{96,64},{33,1},{65,33},{97,65},{34,2},{66,34},{98,6... | collective-permute-start | bytes 196616 | tf_op jit(solution)/shard_map/ppermute | solution.py:325
  33.0 55.4 %collective-permute-start.3 = (bf16[66,256]{1,0:T(8,128)(2,1)S(1)}, bf16[66,256]{1,0:T(8,128)(2,1)S(1)}, u32[]{:S(2)}, u32[]{:S(2)}) collective-permute-start(bf16[66,256]{1,0:T(8,128)(2,1)S(1)} %pad_maximum_fusion.3), channel_id=1, source_target_pairs={{1,0},{2,1},{3,2},{4,3},{5,4},{6,5},{7,6},{8,7},{9,8},{10,9},{11,1... | collective-permute-start | bytes 101384 | tf_op jit(solution)/shard_map/ppermute | solution.py:332
  35.6 52.8 %collective-permute-start.2 = (bf16[66,256]{1,0:T(8,128)(2,1)S(1)}, bf16[66,256]{1,0:T(8,128)(2,1)S(1)}, u32[]{:S(2)}, u32[]{:S(2)}) collective-permute-start(bf16[66,256]{1,0:T(8,128)(2,1)S(1)} %pad_maximum_fusion.2), channel_id=1, source_target_pairs={{0,1},{1,2},{2,3},{3,4},{4,5},{5,6},{6,7},{7,8},{8,9},{9,10},{10,1... | collective-permute-start | bytes 101384 | tf_op jit(solution)/shard_map/ppermute | solution.py:331
  88.5 2.3 %copy-start.2 = (bf16[64,128,256]{2,1,0:T(8,128)(2,1)S(1)}, bf16[64,128,256]{2,1,0:T(8,128)(2,1)}, u32[]{:S(2)}) copy-start(bf16[64,128,256]{2,1,0:T(8,128)(2,1)} %canvas_ref.1) | copy-start | bytes 12582916
  123.8 42.3 %collective-permute-start.4 = (bf16[192,3200]{1,0:T(8,128)(2,1)}, bf16[192,3200]{1,0:T(8,128)(2,1)S(1)}, u32[]{:S(2)}, u32[]{:S(2)}) collective-permute-start(bf16[192,3200]{1,0:T(8,128)(2,1)} %hold_and_norm.1.xh), channel_id=1, source_target_pairs={{0,1},{1,2},{2,3},{3,4},{4,5},{5,6},{6,7},{7,8},{8,9},{9,10},{10,1... | collective-permute-start | bytes 3686408 | tf_op jit(solution)/shard_map/ppermute | solution.py:355
  125.9 40.2 %collective-permute-start.5 = (bf16[192,3200]{1,0:T(8,128)(2,1)}, bf16[192,3200]{1,0:T(8,128)(2,1)S(1)}, u32[]{:S(2)}, u32[]{:S(2)}) collective-permute-start(bf16[192,3200]{1,0:T(8,128)(2,1)} %hold_and_norm.1.xh), channel_id=1, source_target_pairs={{1,0},{2,1},{3,2},{4,3},{5,4},{6,5},{7,6},{8,7},{9,8},{10,9},{11,1... | collective-permute-start | bytes 3686408 | tf_op jit(solution)/shard_map/ppermute | solution.py:356
  129.7 35.8 %all-to-all-start.1 = ((bf16[32,1,3]{2,1,0:T(2,128)(2,1)}), bf16[32,1,3]{2,1,0:T(2,128)(2,1)S(1)}, u32[]{:S(2)}, u32[]{:S(2)}) async-start(bf16[32,1,3]{2,1,0:T(2,128)(2,1)} %copy.34), calls=%async_computation.1 | async-start | bytes 32768 | tf_op jit(solution)/shard_map/all_to_all | solution.py:343
  167.1 1.3 copy-start.1
Sparse Core Ops, SparseCore 0:
  11.5 155.4 all-gather.1

commit v4 on v3

--- a/solution.py
+++ b/solution.py
@@ -221,10 +221,10 @@
     scale = 1.0 / math.sqrt(HD)
 
     def body(xb, xh, xa, ext, *refs):
-        w_refs = refs[:9]
-        sharp_ref, own_ref, key_ref, out_ref, x, bias, wide, lasts, q_buf, k_buf, v_buf = refs[9:]
+        w_refs = (refs[:9], refs[9:18])
+        sharp_ref, own_ref, key_ref, out_ref, x, bias, wide, lasts, q_buf, k_buf, v_buf = refs[18:]
         n = pl.program_id(0)
-        head = jnp.minimum(n, HEADS - 1)
+        heads = [jnp.minimum(2 * n + slot, HEADS - 1) for slot in range(2)]
 
         @pl.when(n == 0)
         def _():
@@ -237,61 +237,64 @@
             for j in range(spare):
                 for s in range(8):
                     lasts[8 * j + s] = wide[j, pl.ds(s, parts, stride=8), :].astype(BF)
-            q_buf[1] = jnp.zeros((rows, HD), BF)
-            k_buf[1] = jnp.zeros((near, HD), BF)
-            v_buf[1] = jnp.zeros((near, HD), BF)
-
-        done = (n + 1) % 2
-        logits = lax.dot_general(
-            q_buf[done], k_buf[done], (((1,), (1,)), ((), ())), preferred_element_type=F32
+            q_buf[1] = jnp.zeros((2, rows, HD), BF)
+            k_buf[1] = jnp.zeros((2, near, HD), BF)
+            v_buf[1] = jnp.zeros((2, near, HD), BF)
+
+        done, new = (n + 1) % 2, n % 2
+        for slot in range(2):
+            logits = lax.dot_general(
+                q_buf[done, slot], k_buf[done, slot], (((1,), (1,)), ((), ())), preferred_element_type=F32
+            )
+            logits = logits * scale + bias[...]
+            peak = jnp.max(logits, axis=1, keepdims=True)
+            weights = jnp.exp(logits - peak)
+            total = jnp.sum(weights, axis=1, keepdims=True)
+            result = jnp.dot(weights.astype(BF), v_buf[done, slot], preferred_element_type=F32)
+            out_ref[:, slot * HD : (slot + 1) * HD] = (result / total).astype(BF)
+
+        at = eights * deep
+        q = jnp.dot(
+            xh[:, at:], jnp.concatenate([lasts[h] for h in heads], axis=1), preferred_element_type=F32
         )
-        logits = logits * scale + bias[...]
-        peak = jnp.max(logits, axis=1, keepdims=True)
-        weights = jnp.exp(logits - peak)
-        total = jnp.sum(weights, axis=1, keepdims=True)
-        result = jnp.dot(weights.astype(BF), v_buf[done], preferred_element_type=F32)
-        out_ref[...] = (result / total).astype(BF)
-
-        q = jnp.zeros((rows, HD), F32)
-        kv = jnp.zeros((near, 2 * HD), F32)
         for b in range(eights):
-            at = b * deep
-            q = q + jnp.dot(xh[:, at : at + deep], w_refs[b][...], preferred_element_type=F32)
-            both = jnp.concatenate([w_refs[3 + b][...], w_refs[6 + b][...]], axis=1)
-            kv = kv + jnp.dot(x[:, at : at + deep], both, preferred_element_type=F32)
-        at = eights * deep
-        q = q + jnp.dot(xh[:, at:], lasts[head], preferred_element_type=F32)
-        both = jnp.concatenate([lasts[head + HEADS], lasts[head + 2 * HEADS]], axis=1)
-        kv = kv + jnp.dot(x[:, at:], both, preferred_element_type=F32)
-        new = n % 2
-        q_buf[new] = q.astype(BF)
-        k_buf[new] = (kv[:, :HD] * sharp_ref[...]).astype(BF)
-        v_buf[new] = kv[:, HD:].astype(BF)
-
-    def w_spec(b, kind):
+            both = jnp.concatenate([w_refs[0][b][...], w_refs[1][b][...]], axis=1)
+            q = q + jnp.dot(xh[:, b * deep : (b + 1) * deep], both, preferred_element_type=F32)
+        for slot in range(2):
+            q_buf[new, slot] = q[:, slot * HD : (slot + 1) * HD].astype(BF)
+            h = heads[slot]
+            both = jnp.concatenate([lasts[h + HEADS], lasts[h + 2 * HEADS]], axis=1)
+            kv = jnp.dot(x[:, at:], both, preferred_element_type=F32)
+            for b in range(eights):
+                both = jnp.concatenate([w_refs[slot][3 + b][...], w_refs[slot][6 + b][...]], axis=1)
+                kv = kv + jnp.dot(x[:, b * deep : (b + 1) * deep], both, preferred_element_type=F32)
+            k_buf[new, slot] = (kv[:, :HD] * sharp_ref[...]).astype(BF)
+            v_buf[new, slot] = kv[:, HD:].astype(BF)
+
+    def w_spec(b, kind, slot):
         first = spare + b * 3 * HEADS + kind * HEADS
-        return pl.BlockSpec((deep, HD), lambda n: (0, first + jnp.minimum(n, HEADS - 1)))
+        return pl.BlockSpec((deep, HD), lambda n: (0, first + jnp.minimum(2 * n + slot, HEADS - 1)))
 
     return pl.pallas_call(
         body,
-        grid=(HEADS + 1,),
+        grid=(-(-HEADS // 2) + 1,),
         out_shape=jax.ShapeDtypeStruct((rows, HW), BF),
         in_specs=[VMEM, VMEM, VMEM, pl.BlockSpec((deep, spare * 128), lambda n: (0, 0))]
-        + [w_spec(b, kind) for kind in range(3) for b in range(3)]
+        + [w_spec(b, kind, slot) for slot in range(2) for kind in range(3) for b in range(3)]
         + [VMEM, VMEM, VMEM],
-        out_specs=pl.BlockSpec((rows, HD), lambda n: (0, jnp.maximum(n - 1, 0))),
+        out_specs=pl.BlockSpec((rows, 2 * HD), lambda n: (0, jnp.maximum(n - 1, 0))),
         scratch_shapes=[
             pltpu.VMEM((near, width), BF),
             pltpu.VMEM((rows, near), F32),
             pltpu.VMEM((spare, deep, 128), F32),
             pltpu.VMEM((8 * spare, parts, HD), BF),
-            pltpu.VMEM((2, rows, HD), BF),
-            pltpu.VMEM((2, near, HD), BF),
-            pltpu.VMEM((2, near, HD), BF),
+            pltpu.VMEM((2, 2, rows, HD), BF),
+            pltpu.VMEM((2, 2, near, HD), BF),
+            pltpu.VMEM((2, 2, near, HD), BF),
         ],
         compiler_params=pltpu.CompilerParams(vmem_limit_bytes=48 << 20),
         name="project_and_attend",
-    )(before, here, after, *([packed] * 10), sharp, own_ids, key_ids)
+    )(before, here, after, *([packed] * 19), sharp, own_ids, key_ids)
 
 
 def shards(
@@ -339,7 +342,7 @@
     cells = jnp.take(tile_cell[0], slot_for)
     send_score = jnp.take(score_map.reshape(-1), cells).astype(BF)
     send_score = jnp.stack([jnp.roll(send_score, 1), send_score, jnp.roll(send_score, -1)], axis=1)
-    recv, send_score = lax.optimization_barrier((recv, send_score))
+    _, send_score = lax.optimization_barrier((recv, send_score))
     recv_score = lax.all_to_all(send_score, "dev", split_axis=0, concat_axis=0, tiled=True)
 
     near_holders = jnp.clip(own + jnp.arange(-1, 2, dtype=jnp.int32), 0, holders - 1)

time: 211 us -> 212 us (level)
  no operation moved by 1% of the time
where the time goes in v4:
time: 212 us; the launch traced here: 208 us
  waiting for transfers between devices  77.8 us (37%)
  Pallas kernels  70.1 us (33%)
  starting transfers between devices  30.5 us (14%)
  between operations  14.4 us (7%)
  local copies, waits for them, and re-layouts  11.9 us (6%)
  other arithmetic  3.57 us (2%)
    ppermute x1, waiting for transfers between devices, shards(): right = lax.ppermute(edge(0), 'dev', down)  46.9 us
    pallas_call x1, Pallas kernels, project_and_attend(): pl.pallas_call(body, grid=(-(-HEADS // 2) + 1,), out_shape=jax.ShapeDtype...  33.4 us
    all_to_all x1, waiting for transfers between devices, shards(): lax.all_to_all(send_score, 'dev', split_axis=0, concat_axis=0, tiled=True)  29.8 us
    pallas_call x1, Pallas kernels, conv_scores(): pl.pallas_call(body, grid=(height // step,), out_shape=jax.ShapeDtypeStru...  22.9 us
    all_to_all x1, starting transfers between devices, shards(): recv = lax.all_to_all(sent, 'dev', split_axis=0, concat_axis=0, tiled=True)  7.78 us
    pallas_call x1, Pallas kernels, hold_and_norm(): pl.pallas_call(body, out_shape=jax.ShapeDtypeStruct((rows, width), BF), i...  6.52 us
    all_to_all x1, starting transfers between devices, shards(): lax.all_to_all(send_score, 'dev', split_axis=0, concat_axis=0, tiled=True)  6.29 us
    pallas_call x1, Pallas kernels, send_order(): pl.pallas_call(body, out_shape=jax.ShapeDtypeStruct(tokens.shape, tokens....  5.69 us
  transfers between devices with their start and end apart: 9, of which 3 were waited for; matrix products, arithmetic and copies ran while one was open for 6% of the time, Pallas kernels for 17%

profile of v4, /device:TPU:97, one launch (start us, length us, event | category | flops | bytes accessed | tf_op | source)
XLA Modules:
  0.0 208.4 jit_solution(2125944146729044244)
XLA Ops:
  7.2 0.0 copy-start
  7.2 0.0 all-gather.2.cloned.1.call-start
  7.2 1.7 pack_rows.1
  8.9 0.0 all-gather.2.cloned.1.call-update
  8.9 5.7 %send_order.1 = bf16[32,24,3200]{2,1,0:T(8,128)(2,1)} custom-call(s32[32]{0:T(128)} %bitcast.74, s32[32]{0:T(128)} %bitcast.76, s32[1]{0:T(128)} %bitcast.12.own_ref, bf16[32,24,3200]{2,1,0:T(8,128)(2,1)} %tok_ref.1), custom_call_target="tpu_custom_call" | custom-call | tf_op jit(solution)/shard_map/send_order/pallas_call | solution.py:48
  14.6 0.0 copy-start.7
  14.7 0.0 copy-start.8
  14.7 0.0 copy-start.9
  14.7 0.0 copy-start.6
  14.7 0.0 copy-start.3
  14.7 0.0 copy-start.4
  14.7 0.0 copy-start.5
  14.7 7.8 %all-to-all-start = ((bf16[32,24,3200]{2,1,0:T(8,128)(2,1)}), bf16[32,24,3200]{2,1,0:T(8,128)(2,1)}, u32[]{:S(2)}, u32[]{:S(2)}) async-start(bf16[32,24,3200]{2,1,0:T(8,128)(2,1)} %send_order.1), calls=%async_computation | async-start | bytes 9830400 | tf_op jit(solution)/shard_map/all_to_all | solution.py:322
  22.5 0.9 fusion.8
  23.4 3.1 %collective-permute-start = (bf16[1,128,256]{2,1,0:T(8,128)(2,1)S(1)}, bf16[1,128,256]{2,1,0:T(8,128)(2,1)S(1)}, u32[]{:S(2)}, u32[]{:S(2)}) collective-permute-start(bf16[1,128,256]{2,1,0:T(8,128)(2,1)S(1)} %get-tuple-element.9), channel_id=1, source_target_pairs={{0,32},{32,64},{64,96},{1,33},{33,65},{65,97},{2,34},{34,66},{66,9... | collective-permute-start | bytes 196616 | tf_op jit(solution)/shard_map/ppermute | solution.py:327
  26.5 1.3 collective-permute-start.1
  27.8 1.1 fusion.7
  29.0 0.6 reshape.189.gain_ref
  29.7 0.7 gather_fusion.2
  30.4 0.1 slice.85
  30.5 0.6 fusion
  31.1 0.1 select_reduce_fusion
  31.2 0.6 fusion.5
  31.8 0.7 gather_fusion
  32.5 0.1 select_reduce_fusion.1
  32.6 0.2 select_reduce_fusion.3
  32.8 0.1 broadcast_add_fusion
  32.9 0.2 convert_reduce_fusion
  33.1 0.5 slice_bitcast_fusion.4.src_ref
  33.7 0.0 collective-permute-done.top_ref
  33.7 0.0 collective-permute-done.1.bottom_ref
  33.7 2.6 %collective-permute-start.3 = (bf16[66,256]{1,0:T(8,128)(2,1)S(1)}, bf16[66,256]{1,0:T(8,128)(2,1)S(1)}, u32[]{:S(2)}, u32[]{:S(2)}) collective-permute-start(bf16[66,256]{1,0:T(8,128)(2,1)S(1)} %pad_maximum_fusion.3), channel_id=1, source_target_pairs={{1,0},{2,1},{3,2},{4,3},{5,4},{6,5},{7,6},{8,7},{9,8},{10,9},{11,1... | collective-permute-start | bytes 101384 | tf_op jit(solution)/shard_map/ppermute | solution.py:335
  36.3 5.1 %collective-permute-start.2 = (bf16[66,256]{1,0:T(8,128)(2,1)S(1)}, bf16[66,256]{1,0:T(8,128)(2,1)S(1)}, u32[]{:S(2)}, u32[]{:S(2)}) collective-permute-start(bf16[66,256]{1,0:T(8,128)(2,1)S(1)} %pad_maximum_fusion.2), channel_id=1, source_target_pairs={{0,1},{1,2},{2,3},{3,4},{4,5},{5,6},{6,7},{7,8},{8,9},{9,10},{10,1... | collective-permute-start | bytes 101384 | tf_op jit(solution)/shard_map/ppermute | solution.py:334
  41.4 46.9 %collective-permute-done.3 = bf16[66,256]{1,0:T(8,128)(2,1)S(1)} collective-permute-done((bf16[66,256]{1,0:T(8,128)(2,1)S(1)}, bf16[66,256]{1,0:T(8,128)(2,1)S(1)}, u32[]{:S(2)}, u32[]{:S(2)}) %collective-permute-start.3) | collective-permute-done | bytes 33824 | tf_op jit(solution)/shard_map/ppermute | solution.py:335
  88.4 0.0 collective-permute-done.2
  88.5 0.0 copy-start.2
  88.5 2.3 %copy-done.2 = bf16[64,128,256]{2,1,0:T(8,128)(2,1)S(1)} copy-done((bf16[64,128,256]{2,1,0:T(8,128)(2,1)S(1)}, bf16[64,128,256]{2,1,0:T(8,128)(2,1)}, u32[]{:S(2)}) %copy-start.2) | copy-done | bytes 4194328
  90.8 22.9 %conv_scores.1 = f32[8,8,128]{2,1,0:T(8,128)} custom-call(bf16[64,128,256]{2,1,0:T(8,128)(2,1)S(1)} %copy-done.2, bf16[1,128,256]{2,1,0:T(8,128)(2,1)S(1)} %collective-permute-done.top_ref, bf16[1,128,256]{2,1,0:T(8,128)(2,1)S(1)} %collective-permute-done.1.bottom_ref, bf16[64,768]{1,0:T(8,128)(2,1)S(1)} %get-tuple-element.24.left_ref, ...), custom_call_target="tpu_custom_call" | custom-call | tf_op jit(solution)/shard_map/conv_scores/pallas_call | solution.py:170
  113.7 1.5 gather_fusion.1
  115.2 0.0 all-to-all-done.recv_ref
  115.2 6.5 %hold_and_norm.1.xh = bf16[192,3200]{1,0:T(8,128)(2,1)} custom-call(s32[8]{0:T(128)} %slice_bitcast_fusion.4.src_ref, bf16[32,24,3200]{2,1,0:T(8,128)(2,1)} %all-to-all-done.recv_ref, f32[1,3200]{1,0:T(1,128)} %reshape.189.gain_ref, s32[25,128]{1,0:T(8,128)} %constant.71.clone.table_ref), custom_call_target="tpu_custom_call" | custom-call | tf_op jit(solution)/shard_map/hold_and_norm/pallas_call | solution.py:99
  121.7 2.1 %collective-permute-start.4 = (bf16[192,3200]{1,0:T(8,128)(2,1)}, bf16[192,3200]{1,0:T(8,128)(2,1)S(1)}, u32[]{:S(2)}, u32[]{:S(2)}) collective-permute-start(bf16[192,3200]{1,0:T(8,128)(2,1)} %hold_and_norm.1.xh), channel_id=1, source_target_pairs={{0,1},{1,2},{2,3},{3,4},{4,5},{5,6},{6,7},{7,8},{8,9},{9,10},{10,1... | collective-permute-start | bytes 3686408 | tf_op jit(solution)/shard_map/ppermute | solution.py:358
  123.8 2.2 %collective-permute-start.5 = (bf16[192,3200]{1,0:T(8,128)(2,1)}, bf16[192,3200]{1,0:T(8,128)(2,1)S(1)}, u32[]{:S(2)}, u32[]{:S(2)}) collective-permute-start(bf16[192,3200]{1,0:T(8,128)(2,1)} %hold_and_norm.1.xh), channel_id=1, source_target_pairs={{1,0},{2,1},{3,2},{4,3},{5,4},{6,5},{7,6},{8,7},{9,8},{10,9},{11,1... | collective-permute-start | bytes 3686408 | tf_op jit(solution)/shard_map/ppermute | solution.py:359
  126.0 0.6 fusion.11
  126.6 0.1 fusion.12
  126.7 0.7 maximum_bitcast_fusion
  127.4 0.6 maximum_bitcast_fusion.1
  128.1 0.7 copy.34
  128.8 6.3 %all-to-all-start.1 = ((bf16[32,1,3]{2,1,0:T(2,128)(2,1)}), bf16[32,1,3]{2,1,0:T(2,128)(2,1)S(1)}, u32[]{:S(2)}, u32[]{:S(2)}) async-start(bf16[32,1,3]{2,1,0:T(2,128)(2,1)} %copy.34), calls=%async_computation.1 | async-start | bytes 32768 | tf_op jit(solution)/shard_map/all_to_all | solution.py:346
  135.1 0.1 broadcast_in_dim.109
  135.2 0.1 broadcast_in_dim.112.refs_19_
  135.3 0.1 broadcast_in_dim.111
  135.3 0.1 broadcast_in_dim_reshape.7.refs_20_
  135.4 29.8 %all-to-all-done.1 = bf16[32,1,3]{2,1,0:T(2,128)(2,1)S(1)} async-done(((bf16[32,1,3]{2,1,0:T(2,128)(2,1)}), bf16[32,1,3]{2,1,0:T(2,128)(2,1)S(1)}, u32[]{:S(2)}, u32[]{:S(2)}) %all-to-all-start.1) | async-done | bytes 224 | tf_op jit(solution)/shard_map/all_to_all | solution.py:346
  165.3 0.1 copy.35
  165.4 0.2 select_reduce_fusion.2
  165.5 0.1 reshape.190
  165.6 0.1 broadcast_in_dim.107
  165.7 0.2 broadcast_in_dim_reshape.8.refs_18_
  165.9 0.0 collective-permute-done.4.xb
  165.9 0.0 collective-permute-done.5.xa
  165.9 1.0 all-gather.2.cloned.1.call-done.ext.refs_0_.refs_1_.refs_2_.refs_3_.refs_4_.refs_5_.refs_6_.refs_7_.refs_8_.refs_9_.refs_10_.refs_11_.refs_12_.refs_13_.refs_14_.refs_15_.refs_16_.refs_17_
  166.9 1.3 copy-done.1
  168.2 33.4 %project_and_attend.1 = bf16[192,1664]{1,0:T(8,128)(2,1)} custom-call(bf16[192,3200]{1,0:T(8,128)(2,1)S(1)} %collective-permute-done.4.xb, bf16[192,3200]{1,0:T(8,128)(2,1)S(1)} %copy-done.1, bf16[192,3200]{1,0:T(8,128)(2,1)S(1)} %collective-permute-done.5.xa, ...), custom_call_target="tpu_custom_call" | custom-call | tf_op jit(solution)/shard_map/project_and_attend/pallas_call | solution.py:278
  (31 shorter events, 0.2 us)
Async XLA Ops:
  7.2 22.5 %copy-start = (s32[1,256]{1,0:T(1,128)S(1)}, s32[1,256]{1,0:T(1,128)}, u32[]{:S(2)}) copy-start(s32[1,256]{1,0:T(1,128)} %param.20) | copy-start | bytes 3076
  7.2 159.7 %all-gather.2.cloned.1.call-start = ((), (), s32[]{:S(2)}) async-start(), calls=%async_computation.2 | async-start | bytes 32231424 | tf_op jit(solution)/shard_map/all_gather | solution.py:324
  14.6 14.4 %copy-start.7 = (f32[3200]{0:T(1024)S(1)}, f32[3200]{0:T(1024)}, u32[]{:S(2)}) copy-start(f32[3200]{0:T(1024)} %param.21) | copy-start | bytes 38404
  14.7 15.8 %copy-start.8 = (s32[1,32]{1,0:T(1,128)S(1)}, s32[1,32]{1,0:T(1,128)}, u32[]{:S(2)}) copy-start(s32[1,32]{1,0:T(1,128)} %param.18) | copy-start | bytes 388
  14.7 16.4 %copy-start.9 = (s32[1,32]{1,0:T(1,128)S(1)}, s32[1,32]{1,0:T(1,128)}, u32[]{:S(2)}) copy-start(s32[1,32]{1,0:T(1,128)} %param.19) | copy-start | bytes 388
  14.7 17.1 %copy-start.6 = (s32[1,32]{1,0:T(1,128)S(1)}, s32[1,32]{1,0:T(1,128)}, u32[]{:S(2)}) copy-start(s32[1,32]{1,0:T(1,128)} %param.17) | copy-start | bytes 388
  14.7 73.8 %copy-start.3 = (bf16[2304,256]{1,0:T(8,128)(2,1)S(1)}, bf16[2304,256]{1,0:T(8,128)(2,1)}, u32[]{:S(2)}) copy-start(bf16[2304,256]{1,0:T(8,128)(2,1)} %w_ref.2) | copy-start | bytes 3538948
  14.7 73.8 %copy-start.4 = (f32[256]{0:T(256)S(1)}, f32[256]{0:T(256)}, u32[]{:S(2)}) copy-start(f32[256]{0:T(256)} %param.14) | copy-start | bytes 3076
  14.7 73.8 %copy-start.5 = (f32[256]{0:T(256)S(1)}, f32[256]{0:T(256)}, u32[]{:S(2)}) copy-start(f32[256]{0:T(256)} %param.15) | copy-start | bytes 3076
  14.7 100.5 %all-to-all-start = ((bf16[32,24,3200]{2,1,0:T(8,128)(2,1)}), bf16[32,24,3200]{2,1,0:T(8,128)(2,1)}, u32[]{:S(2)}, u32[]{:S(2)}) async-start(bf16[32,24,3200]{2,1,0:T(8,128)(2,1)} %send_order.1), calls=%async_computation | async-start | bytes 9830400 | tf_op jit(solution)/shard_map/all_to_all | solution.py:322
  23.4 10.3 %collective-permute-start = (bf16[1,128,256]{2,1,0:T(8,128)(2,1)S(1)}, bf16[1,128,256]{2,1,0:T(8,128)(2,1)S(1)}, u32[]{:S(2)}, u32[]{:S(2)}) collective-permute-start(bf16[1,128,256]{2,1,0:T(8,128)(2,1)S(1)} %get-tuple-element.9), channel_id=1, source_target_pairs={{0,32},{32,64},{64,96},{1,33},{33,65},{65,97},{2,34},{34,66},{66,9... | collective-permute-start | bytes 196616 | tf_op jit(solution)/shard_map/ppermute | solution.py:327
  26.5 7.2 %collective-permute-start.1 = (bf16[1,128,256]{2,1,0:T(8,128)(2,1)S(1)}, bf16[1,128,256]{2,1,0:T(8,128)(2,1)S(1)}, u32[]{:S(2)}, u32[]{:S(2)}) collective-permute-start(bf16[1,128,256]{2,1,0:T(8,128)(2,1)S(1)} %get-tuple-element.8), channel_id=1, source_target_pairs={{32,0},{64,32},{96,64},{33,1},{65,33},{97,65},{34,2},{66,34},{98,6... | collective-permute-start | bytes 196616 | tf_op jit(solution)/shard_map/ppermute | solution.py:328
  33.7 54.6 %collective-permute-start.3 = (bf16[66,256]{1,0:T(8,128)(2,1)S(1)}, bf16[66,256]{1,0:T(8,128)(2,1)S(1)}, u32[]{:S(2)}, u32[]{:S(2)}) collective-permute-start(bf16[66,256]{1,0:T(8,128)(2,1)S(1)} %pad_maximum_fusion.3), channel_id=1, source_target_pairs={{1,0},{2,1},{3,2},{4,3},{5,4},{6,5},{7,6},{8,7},{9,8},{10,9},{11,1... | collective-permute-start | bytes 101384 | tf_op jit(solution)/shard_map/ppermute | solution.py:335
  36.3 52.0 %collective-permute-start.2 = (bf16[66,256]{1,0:T(8,128)(2,1)S(1)}, bf16[66,256]{1,0:T(8,128)(2,1)S(1)}, u32[]{:S(2)}, u32[]{:S(2)}) collective-permute-start(bf16[66,256]{1,0:T(8,128)(2,1)S(1)} %pad_maximum_fusion.2), channel_id=1, source_target_pairs={{0,1},{1,2},{2,3},{3,4},{4,5},{5,6},{6,7},{7,8},{8,9},{9,10},{10,1... | collective-permute-start | bytes 101384 | tf_op jit(solution)/shard_map/ppermute | solution.py:334
  88.5 2.3 %copy-start.2 = (bf16[64,128,256]{2,1,0:T(8,128)(2,1)S(1)}, bf16[64,128,256]{2,1,0:T(8,128)(2,1)}, u32[]{:S(2)}) copy-start(bf16[64,128,256]{2,1,0:T(8,128)(2,1)} %canvas_ref.1) | copy-start | bytes 12582916
  121.7 44.2 %collective-permute-start.4 = (bf16[192,3200]{1,0:T(8,128)(2,1)}, bf16[192,3200]{1,0:T(8,128)(2,1)S(1)}, u32[]{:S(2)}, u32[]{:S(2)}) collective-permute-start(bf16[192,3200]{1,0:T(8,128)(2,1)} %hold_and_norm.1.xh), channel_id=1, source_target_pairs={{0,1},{1,2},{2,3},{3,4},{4,5},{5,6},{6,7},{7,8},{8,9},{9,10},{10,1... | collective-permute-start | bytes 3686408 | tf_op jit(solution)/shard_map/ppermute | solution.py:358
  123.8 42.1 %collective-permute-start.5 = (bf16[192,3200]{1,0:T(8,128)(2,1)}, bf16[192,3200]{1,0:T(8,128)(2,1)S(1)}, u32[]{:S(2)}, u32[]{:S(2)}) collective-permute-start(bf16[192,3200]{1,0:T(8,128)(2,1)} %hold_and_norm.1.xh), channel_id=1, source_target_pairs={{1,0},{2,1},{3,2},{4,3},{5,4},{6,5},{7,6},{8,7},{9,8},{10,9},{11,1... | collective-permute-start | bytes 3686408 | tf_op jit(solution)/shard_map/ppermute | solution.py:359
  128.8 36.5 %all-to-all-start.1 = ((bf16[32,1,3]{2,1,0:T(2,128)(2,1)}), bf16[32,1,3]{2,1,0:T(2,128)(2,1)S(1)}, u32[]{:S(2)}, u32[]{:S(2)}) async-start(bf16[32,1,3]{2,1,0:T(2,128)(2,1)} %copy.34), calls=%async_computation.1 | async-start | bytes 32768 | tf_op jit(solution)/shard_map/all_to_all | solution.py:346
  166.9 1.3 copy-start.1
Sparse Core Ops, SparseCore 0:
  11.5 155.3 all-gather.1

commit v5 on v3

--- a/solution.py
+++ b/solution.py
@@ -212,26 +212,22 @@
     )(weight)
 
 
-def project_and_attend(before, here, after, packed, sharp, own_ids, key_ids):
-    rows, width = here.shape
+def project_and_attend(near_tokens, bias, packed, sharp):
+    near, width = near_tokens.shape
+    rows = near // 3
     deep = packed.shape[0]
     eights, parts = width // deep, deep // 8
-    near = 3 * rows
     spare = -(-3 * HEADS // 8)
     scale = 1.0 / math.sqrt(HD)
 
-    def body(xb, xh, xa, ext, *refs):
+    def body(x, bias, ext, *refs):
         w_refs = refs[:9]
-        sharp_ref, own_ref, key_ref, out_ref, x, bias, wide, lasts, q_buf, k_buf, v_buf = refs[9:]
+        sharp_ref, out_ref, wide, lasts, q_buf, k_buf, v_buf = refs[9:]
         n = pl.program_id(0)
         head = jnp.minimum(n, HEADS - 1)
 
         @pl.when(n == 0)
         def _():
-            x[0:rows] = xb[...]
-            x[rows : 2 * rows] = xh[...]
-            x[2 * rows :] = xa[...]
-            bias[...] = jnp.where(own_ref[...] == key_ref[...], 0.0, -1e30)
             for j in range(spare):
                 wide[j] = ext[:, j * 128 : (j + 1) * 128].astype(F32)
             for j in range(spare):
@@ -256,11 +252,11 @@
         kv = jnp.zeros((near, 2 * HD), F32)
         for b in range(eights):
             at = b * deep
-            q = q + jnp.dot(xh[:, at : at + deep], w_refs[b][...], preferred_element_type=F32)
+            q = q + jnp.dot(x[rows : 2 * rows, at : at + deep], w_refs[b][...], preferred_element_type=F32)
             both = jnp.concatenate([w_refs[3 + b][...], w_refs[6 + b][...]], axis=1)
             kv = kv + jnp.dot(x[:, at : at + deep], both, preferred_element_type=F32)
         at = eights * deep
-        q = q + jnp.dot(xh[:, at:], lasts[head], preferred_element_type=F32)
+        q = q + jnp.dot(x[rows : 2 * rows, at:], lasts[head], preferred_element_type=F32)
         both = jnp.concatenate([lasts[head + HEADS], lasts[head + 2 * HEADS]], axis=1)
         kv = kv + jnp.dot(x[:, at:], both, preferred_element_type=F32)
         new = n % 2
@@ -276,13 +272,11 @@
         body,
         grid=(HEADS + 1,),
         out_shape=jax.ShapeDtypeStruct((rows, HW), BF),
-        in_specs=[VMEM, VMEM, VMEM, pl.BlockSpec((deep, spare * 128), lambda n: (0, 0))]
+        in_specs=[VMEM, VMEM, pl.BlockSpec((deep, spare * 128), lambda n: (0, 0))]
         + [w_spec(b, kind) for kind in range(3) for b in range(3)]
-        + [VMEM, VMEM, VMEM],
+        + [VMEM],
         out_specs=pl.BlockSpec((rows, HD), lambda n: (0, jnp.maximum(n - 1, 0))),
         scratch_shapes=[
-            pltpu.VMEM((near, width), BF),
-            pltpu.VMEM((rows, near), F32),
             pltpu.VMEM((spare, deep, 128), F32),
             pltpu.VMEM((8 * spare, parts, HD), BF),
             pltpu.VMEM((2, rows, HD), BF),
@@ -291,7 +285,7 @@
         ],
         compiler_params=pltpu.CompilerParams(vmem_limit_bytes=48 << 20),
         name="project_and_attend",
-    )(before, here, after, *([packed] * 10), sharp, own_ids, key_ids)
+    )(near_tokens, bias, *([packed] * 10), sharp)
 
 
 def shards(
@@ -339,7 +333,7 @@
     cells = jnp.take(tile_cell[0], slot_for)
     send_score = jnp.take(score_map.reshape(-1), cells).astype(BF)
     send_score = jnp.stack([jnp.roll(send_score, 1), send_score, jnp.roll(send_score, -1)], axis=1)
-    recv, send_score = lax.optimization_barrier((recv, send_score))
+    _, send_score = lax.optimization_barrier((recv, send_score))
     recv_score = lax.all_to_all(send_score, "dev", split_axis=0, concat_axis=0, tiled=True)
 
     near_holders = jnp.clip(own + jnp.arange(-1, 2, dtype=jnp.int32), 0, holders - 1)
@@ -361,7 +355,9 @@
     near_ids = jnp.where(inside, jnp.take(all_ids, jnp.clip(places, 0, all_ids.shape[0] - 1)), -1)
     key_ids = jnp.repeat(near_ids, tile_len)
     own_ids = key_ids[held_rows : 2 * held_rows]
-    attended = project_and_attend(before, here, after, packed, sharp, own_ids[:, None], key_ids[None, :])
+    near_tokens = jnp.concatenate([before, here, after], axis=0)
+    bias = jnp.where(own_ids[:, None] == key_ids[None, :], 0.0, -1e30)
+    attended = project_and_attend(near_tokens, bias, packed, sharp)
     return (score_map, attended)
 
 

time: 211 us -> 215 us (1.019)
  the two profiles are of different devices: /device:TPU:97 before, /device:TPU:1 now
where the time goes in v5:
time: 215 us
  waiting for transfers between devices  76.5 us (36%)
  Pallas kernels  68.9 us (32%)
  starting transfers between devices  35.1 us (16%)
  between operations  14.4 us (7%)
  local copies, waits for them, and re-layouts  12.6 us (6%)
  other arithmetic  6.97 us (3%)
    ppermute x1, waiting for transfers between devices, shards(): right = lax.ppermute(edge(0), 'dev', down)  42.6 us
    all_to_all x1, waiting for transfers between devices, shards(): lax.all_to_all(send_score, 'dev', split_axis=0, concat_axis=0, tiled=True)  32.4 us
    pallas_call x1, Pallas kernels, project_and_attend(): pl.pallas_call(body, grid=(HEADS + 1,), out_shape=jax.ShapeDtypeStruct((r...  32.1 us
    pallas_call x1, Pallas kernels, conv_scores(): pl.pallas_call(body, grid=(height // step,), out_shape=jax.ShapeDtypeStru...  22.9 us
    all_to_all x1, starting transfers between devices, shards(): recv = lax.all_to_all(sent, 'dev', split_axis=0, concat_axis=0, tiled=True)  9.77 us
    all_to_all x1, starting transfers between devices, shards(): lax.all_to_all(send_score, 'dev', split_axis=0, concat_axis=0, tiled=True)  8.88 us
    pallas_call x1, Pallas kernels, hold_and_norm(): pl.pallas_call(body, out_shape=jax.ShapeDtypeStruct((rows, width), BF), i...  6.48 us
    pallas_call x1, Pallas kernels, send_order(): pl.pallas_call(body, out_shape=jax.ShapeDtypeStruct(tokens.shape, tokens....  5.71 us
  transfers between devices with their start and end apart: 9, of which 3 were waited for; matrix products, arithmetic and copies ran while one was open for 7% of the time, Pallas kernels for 16%

profile of v5, /device:TPU:1, one launch (start us, length us, event | category | flops | bytes accessed | tf_op | source)
XLA Modules:
  0.0 214.5 jit_solution(7782697313431498023)
XLA Ops:
  7.2 0.0 copy-start
  7.2 0.0 all-gather.2.cloned.1.call-start
  7.2 1.7 pack_rows.1
  8.9 0.0 all-gather.2.cloned.1.call-update
  8.9 5.7 %send_order.1 = bf16[32,24,3200]{2,1,0:T(8,128)(2,1)} custom-call(s32[32]{0:T(128)} %bitcast.74, s32[32]{0:T(128)} %bitcast.76, s32[1]{0:T(128)} %bitcast.12.own_ref, bf16[32,24,3200]{2,1,0:T(8,128)(2,1)} %tok_ref.1), custom_call_target="tpu_custom_call" | custom-call | tf_op jit(solution)/shard_map/send_order/pallas_call | solution.py:48
  14.7 0.0 copy-start.7
  14.7 0.0 copy-start.8
  14.7 0.0 copy-start.9
  14.7 0.0 copy-start.6
  14.7 0.0 copy-start.3
  14.7 0.0 copy-start.4
  14.7 0.0 copy-start.5
  14.7 9.8 %all-to-all-start = ((bf16[32,24,3200]{2,1,0:T(8,128)(2,1)}), bf16[32,24,3200]{2,1,0:T(8,128)(2,1)}, u32[]{:S(2)}, u32[]{:S(2)}) async-start(bf16[32,24,3200]{2,1,0:T(8,128)(2,1)} %send_order.1), calls=%async_computation | async-start | bytes 9830400 | tf_op jit(solution)/shard_map/all_to_all | solution.py:313
  24.5 0.9 fusion.8
  25.4 3.1 %collective-permute-start = (bf16[1,128,256]{2,1,0:T(8,128)(2,1)S(1)}, bf16[1,128,256]{2,1,0:T(8,128)(2,1)S(1)}, u32[]{:S(2)}, u32[]{:S(2)}) collective-permute-start(bf16[1,128,256]{2,1,0:T(8,128)(2,1)S(1)} %get-tuple-element.9), channel_id=1, source_target_pairs={{0,32},{32,64},{64,96},{1,33},{33,65},{65,97},{2,34},{34,66},{66,9... | collective-permute-start | bytes 196616 | tf_op jit(solution)/shard_map/ppermute | solution.py:318
  28.5 1.3 collective-permute-start.1
  29.8 1.1 fusion.7
  31.0 0.6 reshape.191.gain_ref
  31.7 0.7 gather_fusion
  32.4 0.1 slice.81
  32.5 0.1 broadcast_in_dim.107
  32.5 0.1 eq.62
  32.6 0.1 broadcast_in_dim.106
  32.7 0.1 eq.60
  32.8 0.6 fusion
  33.4 0.1 select_reduce_fusion
  33.5 0.6 fusion.5
  34.1 0.7 gather_fusion.1
  34.9 0.1 select_reduce_fusion.1
  35.0 0.2 select_reduce_fusion.3
  35.2 0.1 broadcast_add_fusion
  35.2 0.2 convert_reduce_fusion
  35.5 0.5 slice_bitcast_fusion.4.src_ref
  36.0 0.0 collective-permute-done.top_ref
  36.1 2.5 %collective-permute-start.3 = (bf16[66,256]{1,0:T(8,128)(2,1)S(1)}, bf16[66,256]{1,0:T(8,128)(2,1)S(1)}, u32[]{:S(2)}, u32[]{:S(2)}) collective-permute-start(bf16[66,256]{1,0:T(8,128)(2,1)S(1)} %pad_maximum_fusion.4), channel_id=1, source_target_pairs={{1,0},{2,1},{3,2},{4,3},{5,4},{6,5},{7,6},{8,7},{9,8},{10,9},{11,1... | collective-permute-start | bytes 101384 | tf_op jit(solution)/shard_map/ppermute | solution.py:326
  38.6 3.3 %collective-permute-start.2 = (bf16[66,256]{1,0:T(8,128)(2,1)S(1)}, bf16[66,256]{1,0:T(8,128)(2,1)S(1)}, u32[]{:S(2)}, u32[]{:S(2)}) collective-permute-start(bf16[66,256]{1,0:T(8,128)(2,1)S(1)} %pad_maximum_fusion.3), channel_id=1, source_target_pairs={{0,1},{1,2},{2,3},{3,4},{4,5},{5,6},{6,7},{7,8},{8,9},{9,10},{10,1... | collective-permute-start | bytes 101384 | tf_op jit(solution)/shard_map/ppermute | solution.py:325
  41.8 42.6 %collective-permute-done.3 = bf16[66,256]{1,0:T(8,128)(2,1)S(1)} collective-permute-done((bf16[66,256]{1,0:T(8,128)(2,1)S(1)}, bf16[66,256]{1,0:T(8,128)(2,1)S(1)}, u32[]{:S(2)}, u32[]{:S(2)}) %collective-permute-start.3) | collective-permute-done | bytes 33824 | tf_op jit(solution)/shard_map/ppermute | solution.py:326
  84.5 1.4 collective-permute-done.2
  86.0 0.0 copy-start.2
  86.0 2.3 %copy-done.2 = bf16[64,128,256]{2,1,0:T(8,128)(2,1)S(1)} copy-done((bf16[64,128,256]{2,1,0:T(8,128)(2,1)S(1)}, bf16[64,128,256]{2,1,0:T(8,128)(2,1)}, u32[]{:S(2)}) %copy-start.2) | copy-done | bytes 4194328
  88.2 22.9 %conv_scores.1 = f32[8,8,128]{2,1,0:T(8,128)} custom-call(bf16[64,128,256]{2,1,0:T(8,128)(2,1)S(1)} %copy-done.2, bf16[1,128,256]{2,1,0:T(8,128)(2,1)S(1)} %collective-permute-done.top_ref, bf16[1,128,256]{2,1,0:T(8,128)(2,1)S(1)} %collective-permute-done.1.bottom_ref, bf16[64,768]{1,0:T(8,128)(2,1)S(1)} %get-tuple-element.24.left_ref, ...), custom_call_target="tpu_custom_call" | custom-call | tf_op jit(solution)/shard_map/conv_scores/pallas_call | solution.py:170
  111.1 1.5 gather_fusion.2
  112.6 0.1 fusion.12
  112.7 0.0 all-to-all-done.recv_ref
  112.7 6.5 %hold_and_norm.1 = bf16[192,3200]{1,0:T(8,128)(2,1)} custom-call(s32[8]{0:T(128)} %slice_bitcast_fusion.4.src_ref, bf16[32,24,3200]{2,1,0:T(8,128)(2,1)} %all-to-all-done.recv_ref, f32[1,3200]{1,0:T(1,128)} %reshape.191.gain_ref, s32[25,128]{1,0:T(8,128)} %constant.73.clone.table_ref), custom_call_target="tpu_custom_call" | custom-call | tf_op jit(solution)/shard_map/hold_and_norm/pallas_call | solution.py:99
  119.2 4.4 %collective-permute-start.4 = (bf16[192,3200]{1,0:T(8,128)(2,1)}, bf16[192,3200]{1,0:T(8,128)(2,1)S(1)}, u32[]{:S(2)}, u32[]{:S(2)}) collective-permute-start(bf16[192,3200]{1,0:T(8,128)(2,1)} %hold_and_norm.1), channel_id=1, source_target_pairs={{0,1},{1,2},{2,3},{3,4},{4,5},{5,6},{6,7},{7,8},{8,9},{9,10},{10,1... | collective-permute-start | bytes 3686408 | tf_op jit(solution)/shard_map/ppermute | solution.py:349
  123.6 1.9 collective-permute-start.5
  125.5 0.6 fusion.11
  126.1 0.7 maximum_bitcast_fusion
  126.8 0.7 maximum_bitcast_fusion.1
  127.5 0.7 copy.31
  128.2 8.9 %all-to-all-start.1 = ((bf16[32,1,3]{2,1,0:T(2,128)(2,1)}), bf16[32,1,3]{2,1,0:T(2,128)(2,1)S(1)}, u32[]{:S(2)}, u32[]{:S(2)}) async-start(bf16[32,1,3]{2,1,0:T(2,128)(2,1)} %copy.31), calls=%async_computation.1 | async-start | bytes 32768 | tf_op jit(solution)/shard_map/all_to_all | solution.py:337
  137.1 0.1 compare_select_fusion.bias
  137.2 32.4 %all-to-all-done.1 = bf16[32,1,3]{2,1,0:T(2,128)(2,1)S(1)} async-done(((bf16[32,1,3]{2,1,0:T(2,128)(2,1)}), bf16[32,1,3]{2,1,0:T(2,128)(2,1)S(1)}, u32[]{:S(2)}, u32[]{:S(2)}) %all-to-all-start.1) | async-done | bytes 224 | tf_op jit(solution)/shard_map/all_to_all | solution.py:337
  169.6 0.1 copy.32
  169.7 0.2 select_reduce_fusion.2
  169.9 0.1 reshape.192
  170.0 0.1 broadcast_in_dim.118
  170.0 0.2 broadcast_in_dim_reshape.5.refs_9_
  170.2 0.0 collective-permute-done.4
  170.2 0.0 collective-permute-done.5
  170.2 3.3 %pad_maximum_fusion.x = bf16[576,3200]{1,0:T(8,128)(2,1)} fusion(bf16[192,3200]{1,0:T(8,128)(2,1)S(1)} %collective-permute-done.5, bf16[192,3200]{1,0:T(8,128)(2,1)} %hold_and_norm.1, bf16[192,3200]{1,0:T(8,128)(2,1)S(1)} %collective-permute-done.4), kind=kLoop, calls=%fused_computation.3 | loop fusion | flops 11059200 | bytes 7372800 | tf_op jit(solution)/shard_map/concatenate | solution.py:358
  173.5 2.0 copy-done.1
  175.6 32.1 %project_and_attend.1 = bf16[192,1664]{1,0:T(8,128)(2,1)} custom-call(bf16[576,3200]{1,0:T(8,128)(2,1)S(1)} %copy-done.1, f32[192,576]{1,0:T(8,128)S(1)} %compare_select_fusion.bias, bf16[1024,15616]{1,0:T(8,128)(2,1)} %all-gather.2.cloned.1.call-done.ext.refs_0_.refs_1_.refs_2_.refs_3_.refs_4_.refs_5_.refs_6_.refs_7_.refs_8_, ...), custom_call_target="tpu_custom_call" | custom-call | tf_op jit(solution)/shard_map/project_and_attend/pallas_call | solution.py:271
  (33 shorter events, 0.2 us)
Async XLA Ops:
  7.2 24.5 %copy-start = (s32[1,256]{1,0:T(1,128)S(1)}, s32[1,256]{1,0:T(1,128)}, u32[]{:S(2)}) copy-start(s32[1,256]{1,0:T(1,128)} %param.20) | copy-start | bytes 3076
  7.2 166.4 %all-gather.2.cloned.1.call-start = ((), (), s32[]{:S(2)}) async-start(), calls=%async_computation.2 | async-start | bytes 32231424 | tf_op jit(solution)/shard_map/all_gather | solution.py:315
  14.7 16.4 %copy-start.7 = (f32[3200]{0:T(1024)S(1)}, f32[3200]{0:T(1024)}, u32[]{:S(2)}) copy-start(f32[3200]{0:T(1024)} %param.21) | copy-start | bytes 38404
  14.7 18.1 %copy-start.8 = (s32[1,32]{1,0:T(1,128)S(1)}, s32[1,32]{1,0:T(1,128)}, u32[]{:S(2)}) copy-start(s32[1,32]{1,0:T(1,128)} %param.18) | copy-start | bytes 388
  14.7 18.7 %copy-start.9 = (s32[1,32]{1,0:T(1,128)S(1)}, s32[1,32]{1,0:T(1,128)}, u32[]{:S(2)}) copy-start(s32[1,32]{1,0:T(1,128)} %param.19) | copy-start | bytes 388
  14.7 19.4 %copy-start.6 = (s32[1,32]{1,0:T(1,128)S(1)}, s32[1,32]{1,0:T(1,128)}, u32[]{:S(2)}) copy-start(s32[1,32]{1,0:T(1,128)} %param.17) | copy-start | bytes 388
  14.7 71.2 %copy-start.3 = (bf16[2304,256]{1,0:T(8,128)(2,1)S(1)}, bf16[2304,256]{1,0:T(8,128)(2,1)}, u32[]{:S(2)}) copy-start(bf16[2304,256]{1,0:T(8,128)(2,1)} %w_ref.2) | copy-start | bytes 3538948
  14.7 71.2 %copy-start.4 = (f32[256]{0:T(256)S(1)}, f32[256]{0:T(256)}, u32[]{:S(2)}) copy-start(f32[256]{0:T(256)} %param.14) | copy-start | bytes 3076
  14.7 71.2 %copy-start.5 = (f32[256]{0:T(256)S(1)}, f32[256]{0:T(256)}, u32[]{:S(2)}) copy-start(f32[256]{0:T(256)} %param.15) | copy-start | bytes 3076
  14.7 98.0 %all-to-all-start = ((bf16[32,24,3200]{2,1,0:T(8,128)(2,1)}), bf16[32,24,3200]{2,1,0:T(8,128)(2,1)}, u32[]{:S(2)}, u32[]{:S(2)}) async-start(bf16[32,24,3200]{2,1,0:T(8,128)(2,1)} %send_order.1), calls=%async_computation | async-start | bytes 9830400 | tf_op jit(solution)/shard_map/all_to_all | solution.py:313
  25.4 10.6 %collective-permute-start = (bf16[1,128,256]{2,1,0:T(8,128)(2,1)S(1)}, bf16[1,128,256]{2,1,0:T(8,128)(2,1)S(1)}, u32[]{:S(2)}, u32[]{:S(2)}) collective-permute-start(bf16[1,128,256]{2,1,0:T(8,128)(2,1)S(1)} %get-tuple-element.9), channel_id=1, source_target_pairs={{0,32},{32,64},{64,96},{1,33},{33,65},{65,97},{2,34},{34,66},{66,9... | collective-permute-start | bytes 196616 | tf_op jit(solution)/shard_map/ppermute | solution.py:318
  28.5 7.5 %collective-permute-start.1 = (bf16[1,128,256]{2,1,0:T(8,128)(2,1)S(1)}, bf16[1,128,256]{2,1,0:T(8,128)(2,1)S(1)}, u32[]{:S(2)}, u32[]{:S(2)}) collective-permute-start(bf16[1,128,256]{2,1,0:T(8,128)(2,1)S(1)} %get-tuple-element.8), channel_id=1, source_target_pairs={{32,0},{64,32},{96,64},{33,1},{65,33},{97,65},{34,2},{66,34},{98,6... | collective-permute-start | bytes 196616 | tf_op jit(solution)/shard_map/ppermute | solution.py:319
  36.1 48.4 %collective-permute-start.3 = (bf16[66,256]{1,0:T(8,128)(2,1)S(1)}, bf16[66,256]{1,0:T(8,128)(2,1)S(1)}, u32[]{:S(2)}, u32[]{:S(2)}) collective-permute-start(bf16[66,256]{1,0:T(8,128)(2,1)S(1)} %pad_maximum_fusion.4), channel_id=1, source_target_pairs={{1,0},{2,1},{3,2},{4,3},{5,4},{6,5},{7,6},{8,7},{9,8},{10,9},{11,1... | collective-permute-start | bytes 101384 | tf_op jit(solution)/shard_map/ppermute | solution.py:326
  38.6 47.3 %collective-permute-start.2 = (bf16[66,256]{1,0:T(8,128)(2,1)S(1)}, bf16[66,256]{1,0:T(8,128)(2,1)S(1)}, u32[]{:S(2)}, u32[]{:S(2)}) collective-permute-start(bf16[66,256]{1,0:T(8,128)(2,1)S(1)} %pad_maximum_fusion.3), channel_id=1, source_target_pairs={{0,1},{1,2},{2,3},{3,4},{4,5},{5,6},{6,7},{7,8},{8,9},{9,10},{10,1... | collective-permute-start | bytes 101384 | tf_op jit(solution)/shard_map/ppermute | solution.py:325
  86.0 2.3 %copy-start.2 = (bf16[64,128,256]{2,1,0:T(8,128)(2,1)S(1)}, bf16[64,128,256]{2,1,0:T(8,128)(2,1)}, u32[]{:S(2)}) copy-start(bf16[64,128,256]{2,1,0:T(8,128)(2,1)} %canvas_ref.1) | copy-start | bytes 12582916
  119.2 51.0 %collective-permute-start.4 = (bf16[192,3200]{1,0:T(8,128)(2,1)}, bf16[192,3200]{1,0:T(8,128)(2,1)S(1)}, u32[]{:S(2)}, u32[]{:S(2)}) collective-permute-start(bf16[192,3200]{1,0:T(8,128)(2,1)} %hold_and_norm.1), channel_id=1, source_target_pairs={{0,1},{1,2},{2,3},{3,4},{4,5},{5,6},{6,7},{7,8},{8,9},{9,10},{10,1... | collective-permute-start | bytes 3686408 | tf_op jit(solution)/shard_map/ppermute | solution.py:349
  123.6 46.6 %collective-permute-start.5 = (bf16[192,3200]{1,0:T(8,128)(2,1)}, bf16[192,3200]{1,0:T(8,128)(2,1)S(1)}, u32[]{:S(2)}, u32[]{:S(2)}) collective-permute-start(bf16[192,3200]{1,0:T(8,128)(2,1)} %hold_and_norm.1), channel_id=1, source_target_pairs={{1,0},{2,1},{3,2},{4,3},{5,4},{6,5},{7,6},{8,7},{9,8},{10,9},{11,1... | collective-permute-start | bytes 3686408 | tf_op jit(solution)/shard_map/ppermute | solution.py:350
  128.2 41.4 %all-to-all-start.1 = ((bf16[32,1,3]{2,1,0:T(2,128)(2,1)}), bf16[32,1,3]{2,1,0:T(2,128)(2,1)S(1)}, u32[]{:S(2)}, u32[]{:S(2)}) async-start(bf16[32,1,3]{2,1,0:T(2,128)(2,1)} %copy.31), calls=%async_computation.1 | async-start | bytes 32768 | tf_op jit(solution)/shard_map/all_to_all | solution.py:337
  173.5 2.0 copy-start.1
Sparse Core Ops, SparseCore 0:
  11.5 156.8 all-gather.1

commit v6 on v5

--- a/solution.py
+++ b/solution.py
@@ -189,6 +189,7 @@
     rows, cols = weight.shape
     eights, tiles = rows // 8, cols // 128
     spare = -(-tiles // 8)
+    ahead = eights * tiles
 
     def body(w_ref, out_ref):
         w = w_ref[...].astype(F32)
@@ -198,10 +199,12 @@
                 w[rows - 1 : rows, t * 128 : (t + 1) * 128] if t < tiles else zero
                 for t in range(8 * j, 8 * j + 8)
             ]
-            out_ref[:, j * 128 : (j + 1) * 128] = jnp.concatenate(pieces, axis=0).astype(BF)
-        for b in range(eights):
-            at = spare * 128 + b * cols
-            out_ref[:, at : at + cols] = w[8 * b : 8 * b + 8].astype(BF)
+            out_ref[:, (ahead + j) * 128 : (ahead + j + 1) * 128] = jnp.concatenate(pieces, axis=0).astype(BF)
+        for h in range(HEADS):
+            for b in range(eights):
+                for kind in range(3):
+                    at, low = (3 * (eights * h + b) + kind) * 128, (kind * HEADS + h) * 128
+                    out_ref[:, at : at + 128] = w[8 * b : 8 * b + 8, low : low + 128].astype(BF)
 
     return pl.pallas_call(
         body,
@@ -220,16 +223,16 @@
     spare = -(-3 * HEADS // 8)
     scale = 1.0 / math.sqrt(HD)
 
-    def body(x, bias, ext, *refs):
-        w_refs = refs[:9]
-        sharp_ref, out_ref, wide, lasts, q_buf, k_buf, v_buf = refs[9:]
+    def body(x, bias, w_ref, *refs):
+        ext = refs[:spare]
+        sharp_ref, out_ref, wide, lasts, q_buf, k_buf, v_buf = refs[spare:]
         n = pl.program_id(0)
         head = jnp.minimum(n, HEADS - 1)
 
         @pl.when(n == 0)
         def _():
             for j in range(spare):
-                wide[j] = ext[:, j * 128 : (j + 1) * 128].astype(F32)
+                wide[j] = ext[j][...].astype(F32)
             for j in range(spare):
                 for s in range(8):
                     lasts[8 * j + s] = wide[j, pl.ds(s, parts, stride=8), :].astype(BF)
@@ -252,8 +255,10 @@
         kv = jnp.zeros((near, 2 * HD), F32)
         for b in range(eights):
             at = b * deep
-            q = q + jnp.dot(x[rows : 2 * rows, at : at + deep], w_refs[b][...], preferred_element_type=F32)
-            both = jnp.concatenate([w_refs[3 + b][...], w_refs[6 + b][...]], axis=1)
+            q = q + jnp.dot(
+                x[rows : 2 * rows, at : at + deep], w_ref[:, 3 * b * HD : (3 * b + 1) * HD], preferred_element_type=F32
+            )
+            both = w_ref[:, (3 * b + 1) * HD : (3 * b + 3) * HD]
             kv = kv + jnp.dot(x[:, at : at + deep], both, preferred_element_type=F32)
         at = eights * deep
         q = q + jnp.dot(x[rows : 2 * rows, at:], lasts[head], preferred_element_type=F32)
@@ -264,16 +269,15 @@
         k_buf[new] = (kv[:, :HD] * sharp_ref[...]).astype(BF)
         v_buf[new] = kv[:, HD:].astype(BF)
 
-    def w_spec(b, kind):
-        first = spare + b * 3 * HEADS + kind * HEADS
-        return pl.BlockSpec((deep, HD), lambda n: (0, first + jnp.minimum(n, HEADS - 1)))
+    def ext_spec(j):
+        return pl.BlockSpec((deep, 128), lambda n: (0, 3 * eights * HEADS + j))
 
     return pl.pallas_call(
         body,
         grid=(HEADS + 1,),
         out_shape=jax.ShapeDtypeStruct((rows, HW), BF),
-        in_specs=[VMEM, VMEM, pl.BlockSpec((deep, spare * 128), lambda n: (0, 0))]
-        + [w_spec(b, kind) for kind in range(3) for b in range(3)]
+        in_specs=[VMEM, VMEM, pl.BlockSpec((deep, 3 * eights * HD), lambda n: (0, jnp.minimum(n, HEADS - 1)))]
+        + [ext_spec(j) for j in range(spare)]
         + [VMEM],
         out_specs=pl.BlockSpec((rows, HD), lambda n: (0, jnp.maximum(n - 1, 0))),
         scratch_shapes=[
@@ -285,7 +289,7 @@
         ],
         compiler_params=pltpu.CompilerParams(vmem_limit_bytes=48 << 20),
         name="project_and_attend",
-    )(near_tokens, bias, *([packed] * 10), sharp)
+    )(near_tokens, bias, *([packed] * (1 + spare)), sharp)
 
 
 def shards(

time: 215 us -> 213 us (level)
  no operation moved by 1% of the time
where the time goes in v6:
time: 213 us
  waiting for transfers between devices  76.3 us (36%)
  Pallas kernels  67.2 us (32%)
  starting transfers between devices  35.3 us (17%)
  between operations  14.4 us (7%)
  local copies, waits for them, and re-layouts  12.6 us (6%)
  other arithmetic  6.97 us (3%)
    ppermute x1, waiting for transfers between devices, shards(): right = lax.ppermute(edge(0), 'dev', down)  42.7 us
    all_to_all x1, waiting for transfers between devices, shards(): lax.all_to_all(send_score, 'dev', split_axis=0, concat_axis=0, tiled=True)  32.2 us
    pallas_call x1, Pallas kernels, project_and_attend(): pl.pallas_call(body, grid=(HEADS + 1,), out_shape=jax.ShapeDtypeStruct((r...  30.4 us
    pallas_call x1, Pallas kernels, conv_scores(): pl.pallas_call(body, grid=(height // step,), out_shape=jax.ShapeDtypeStru...  22.9 us
    all_to_all x1, starting transfers between devices, shards(): recv = lax.all_to_all(sent, 'dev', split_axis=0, concat_axis=0, tiled=True)  9.77 us
    all_to_all x1, starting transfers between devices, shards(): lax.all_to_all(send_score, 'dev', split_axis=0, concat_axis=0, tiled=True)  8.96 us
    pallas_call x1, Pallas kernels, hold_and_norm(): pl.pallas_call(body, out_shape=jax.ShapeDtypeStruct((rows, width), BF), i...  6.48 us
    pallas_call x1, Pallas kernels, send_order(): pl.pallas_call(body, out_shape=jax.ShapeDtypeStruct(tokens.shape, tokens....  5.71 us
  transfers between devices with their start and end apart: 9, of which 3 were waited for; matrix products, arithmetic and copies ran while one was open for 7% of the time, Pallas kernels for 16%

profile of v6, /device:TPU:1, one launch (start us, length us, event | category | flops | bytes accessed | tf_op | source)
XLA Modules:
  0.0 212.7 jit_solution(6500057000491625421)
XLA Ops:
  7.2 0.0 copy-start
  7.2 0.0 all-gather.2.cloned.1.call-start
  7.2 1.7 pack_rows.1
  8.9 0.0 all-gather.2.cloned.1.call-update
  9.0 5.7 %send_order.1 = bf16[32,24,3200]{2,1,0:T(8,128)(2,1)} custom-call(s32[32]{0:T(128)} %bitcast.74, s32[32]{0:T(128)} %bitcast.76, s32[1]{0:T(128)} %bitcast.12.own_ref, bf16[32,24,3200]{2,1,0:T(8,128)(2,1)} %tok_ref.1), custom_call_target="tpu_custom_call" | custom-call | tf_op jit(solution)/shard_map/send_order/pallas_call | solution.py:48
  14.7 0.0 copy-start.7
  14.7 0.0 copy-start.8
  14.7 0.0 copy-start.9
  14.7 0.0 copy-start.6
  14.7 0.0 copy-start.3
  14.7 0.0 copy-start.4
  14.8 0.0 copy-start.5
  14.8 9.8 %all-to-all-start = ((bf16[32,24,3200]{2,1,0:T(8,128)(2,1)}), bf16[32,24,3200]{2,1,0:T(8,128)(2,1)}, u32[]{:S(2)}, u32[]{:S(2)}) async-start(bf16[32,24,3200]{2,1,0:T(8,128)(2,1)} %send_order.1), calls=%async_computation | async-start | bytes 9830400 | tf_op jit(solution)/shard_map/all_to_all | solution.py:317
  24.5 0.9 fusion.8
  25.4 3.1 %collective-permute-start = (bf16[1,128,256]{2,1,0:T(8,128)(2,1)S(1)}, bf16[1,128,256]{2,1,0:T(8,128)(2,1)S(1)}, u32[]{:S(2)}, u32[]{:S(2)}) collective-permute-start(bf16[1,128,256]{2,1,0:T(8,128)(2,1)S(1)} %get-tuple-element.9), channel_id=1, source_target_pairs={{0,32},{32,64},{64,96},{1,33},{33,65},{65,97},{2,34},{34,66},{66,9... | collective-permute-start | bytes 196616 | tf_op jit(solution)/shard_map/ppermute | solution.py:322
  28.6 1.3 collective-permute-start.1
  29.9 1.1 fusion.7
  31.0 0.6 reshape.191.gain_ref
  31.7 0.7 gather_fusion
  32.4 0.1 slice.81
  32.5 0.1 broadcast_in_dim.107
  32.6 0.1 eq.62
  32.6 0.1 broadcast_in_dim.106
  32.7 0.1 eq.60
  32.8 0.6 fusion
  33.4 0.1 select_reduce_fusion
  33.6 0.6 fusion.5
  34.2 0.7 gather_fusion.1
  34.9 0.1 select_reduce_fusion.1
  35.0 0.2 select_reduce_fusion.3
  35.2 0.1 broadcast_add_fusion
  35.2 0.2 convert_reduce_fusion
  35.5 0.5 slice_bitcast_fusion.4.src_ref
  36.0 0.0 collective-permute-done.top_ref
  36.0 0.0 collective-permute-done.1.bottom_ref
  36.1 2.5 %collective-permute-start.3 = (bf16[66,256]{1,0:T(8,128)(2,1)S(1)}, bf16[66,256]{1,0:T(8,128)(2,1)S(1)}, u32[]{:S(2)}, u32[]{:S(2)}) collective-permute-start(bf16[66,256]{1,0:T(8,128)(2,1)S(1)} %pad_maximum_fusion.4), channel_id=1, source_target_pairs={{1,0},{2,1},{3,2},{4,3},{5,4},{6,5},{7,6},{8,7},{9,8},{10,9},{11,1... | collective-permute-start | bytes 101384 | tf_op jit(solution)/shard_map/ppermute | solution.py:330
  38.6 3.3 %collective-permute-start.2 = (bf16[66,256]{1,0:T(8,128)(2,1)S(1)}, bf16[66,256]{1,0:T(8,128)(2,1)S(1)}, u32[]{:S(2)}, u32[]{:S(2)}) collective-permute-start(bf16[66,256]{1,0:T(8,128)(2,1)S(1)} %pad_maximum_fusion.3), channel_id=1, source_target_pairs={{0,1},{1,2},{2,3},{3,4},{4,5},{5,6},{6,7},{7,8},{8,9},{9,10},{10,1... | collective-permute-start | bytes 101384 | tf_op jit(solution)/shard_map/ppermute | solution.py:329
  41.9 42.7 %collective-permute-done.3 = bf16[66,256]{1,0:T(8,128)(2,1)S(1)} collective-permute-done((bf16[66,256]{1,0:T(8,128)(2,1)S(1)}, bf16[66,256]{1,0:T(8,128)(2,1)S(1)}, u32[]{:S(2)}, u32[]{:S(2)}) %collective-permute-start.3) | collective-permute-done | bytes 33824 | tf_op jit(solution)/shard_map/ppermute | solution.py:330
  84.5 1.4 collective-permute-done.2
  86.0 0.0 copy-start.2
  86.0 2.3 %copy-done.2 = bf16[64,128,256]{2,1,0:T(8,128)(2,1)S(1)} copy-done((bf16[64,128,256]{2,1,0:T(8,128)(2,1)S(1)}, bf16[64,128,256]{2,1,0:T(8,128)(2,1)}, u32[]{:S(2)}) %copy-start.2) | copy-done | bytes 4194328
  88.3 22.9 %conv_scores.1 = f32[8,8,128]{2,1,0:T(8,128)} custom-call(bf16[64,128,256]{2,1,0:T(8,128)(2,1)S(1)} %copy-done.2, bf16[1,128,256]{2,1,0:T(8,128)(2,1)S(1)} %collective-permute-done.top_ref, bf16[1,128,256]{2,1,0:T(8,128)(2,1)S(1)} %collective-permute-done.1.bottom_ref, bf16[64,768]{1,0:T(8,128)(2,1)S(1)} %get-tuple-element.24.left_ref, ...), custom_call_target="tpu_custom_call" | custom-call | tf_op jit(solution)/shard_map/conv_scores/pallas_call | solution.py:170
  111.2 1.5 gather_fusion.2
  112.6 0.1 fusion.12
  112.7 0.0 all-to-all-done.recv_ref
  112.7 6.5 %hold_and_norm.1 = bf16[192,3200]{1,0:T(8,128)(2,1)} custom-call(s32[8]{0:T(128)} %slice_bitcast_fusion.4.src_ref, bf16[32,24,3200]{2,1,0:T(8,128)(2,1)} %all-to-all-done.recv_ref, f32[1,3200]{1,0:T(1,128)} %reshape.191.gain_ref, s32[25,128]{1,0:T(8,128)} %constant.73.clone.table_ref), custom_call_target="tpu_custom_call" | custom-call | tf_op jit(solution)/shard_map/hold_and_norm/pallas_call | solution.py:99
  119.2 4.4 %collective-permute-start.4 = (bf16[192,3200]{1,0:T(8,128)(2,1)}, bf16[192,3200]{1,0:T(8,128)(2,1)S(1)}, u32[]{:S(2)}, u32[]{:S(2)}) collective-permute-start(bf16[192,3200]{1,0:T(8,128)(2,1)} %hold_and_norm.1), channel_id=1, source_target_pairs={{0,1},{1,2},{2,3},{3,4},{4,5},{5,6},{6,7},{7,8},{8,9},{9,10},{10,1... | collective-permute-start | bytes 3686408 | tf_op jit(solution)/shard_map/ppermute | solution.py:353
  123.6 1.9 collective-permute-start.5
  125.6 0.6 fusion.11
  126.2 0.7 maximum_bitcast_fusion
  126.9 0.6 maximum_bitcast_fusion.1
  127.5 0.7 copy.31
  128.2 9.0 %all-to-all-start.1 = ((bf16[32,1,3]{2,1,0:T(2,128)(2,1)}), bf16[32,1,3]{2,1,0:T(2,128)(2,1)S(1)}, u32[]{:S(2)}, u32[]{:S(2)}) async-start(bf16[32,1,3]{2,1,0:T(2,128)(2,1)} %copy.31), calls=%async_computation.1 | async-start | bytes 32768 | tf_op jit(solution)/shard_map/all_to_all | solution.py:341
  137.2 0.1 compare_select_fusion.bias
  137.3 32.2 %all-to-all-done.1 = bf16[32,1,3]{2,1,0:T(2,128)(2,1)S(1)} async-done(((bf16[32,1,3]{2,1,0:T(2,128)(2,1)}), bf16[32,1,3]{2,1,0:T(2,128)(2,1)S(1)}, u32[]{:S(2)}, u32[]{:S(2)}) %all-to-all-start.1) | async-done | bytes 224 | tf_op jit(solution)/shard_map/all_to_all | solution.py:341
  169.5 0.1 copy.32
  169.6 0.2 select_reduce_fusion.2
  169.8 0.1 reshape.192
  169.9 0.1 broadcast_in_dim.118
  170.0 0.2 broadcast_in_dim_reshape.5.refs_5_
  170.1 0.0 collective-permute-done.5
  170.1 3.3 %pad_maximum_fusion.x = bf16[576,3200]{1,0:T(8,128)(2,1)} fusion(bf16[192,3200]{1,0:T(8,128)(2,1)S(1)} %collective-permute-done.5, bf16[192,3200]{1,0:T(8,128)(2,1)} %hold_and_norm.1, bf16[192,3200]{1,0:T(8,128)(2,1)S(1)} %collective-permute-done.4), kind=kLoop, calls=%fused_computation.3 | loop fusion | flops 11059200 | bytes 7372800 | tf_op jit(solution)/shard_map/concatenate | solution.py:362
  173.4 2.0 copy-done.1
  175.5 30.4 %project_and_attend.1 = bf16[192,1664]{1,0:T(8,128)(2,1)} custom-call(bf16[576,3200]{1,0:T(8,128)(2,1)S(1)} %copy-done.1, f32[192,576]{1,0:T(8,128)S(1)} %compare_select_fusion.bias, bf16[1024,15616]{1,0:T(8,128)(2,1)} %all-gather.2.cloned.1.call-done.w_ref.refs_0_.refs_1_.refs_2_.refs_3_.refs_4_, ...), custom_call_target="tpu_custom_call" | custom-call | tf_op jit(solution)/shard_map/project_and_attend/pallas_call | solution.py:275
  (33 shorter events, 0.2 us)
Async XLA Ops:
  7.2 24.5 %copy-start = (s32[1,256]{1,0:T(1,128)S(1)}, s32[1,256]{1,0:T(1,128)}, u32[]{:S(2)}) copy-start(s32[1,256]{1,0:T(1,128)} %param.20) | copy-start | bytes 3076
  7.2 166.3 %all-gather.2.cloned.1.call-start = ((), (), s32[]{:S(2)}) async-start(), calls=%async_computation.2 | async-start | bytes 32231424 | tf_op jit(solution)/shard_map/all_gather | solution.py:319
  14.7 16.4 %copy-start.7 = (f32[3200]{0:T(1024)S(1)}, f32[3200]{0:T(1024)}, u32[]{:S(2)}) copy-start(f32[3200]{0:T(1024)} %param.21) | copy-start | bytes 38404
  14.7 18.1 %copy-start.8 = (s32[1,32]{1,0:T(1,128)S(1)}, s32[1,32]{1,0:T(1,128)}, u32[]{:S(2)}) copy-start(s32[1,32]{1,0:T(1,128)} %param.18) | copy-start | bytes 388
  14.7 18.7 %copy-start.9 = (s32[1,32]{1,0:T(1,128)S(1)}, s32[1,32]{1,0:T(1,128)}, u32[]{:S(2)}) copy-start(s32[1,32]{1,0:T(1,128)} %param.19) | copy-start | bytes 388
  14.7 19.4 %copy-start.6 = (s32[1,32]{1,0:T(1,128)S(1)}, s32[1,32]{1,0:T(1,128)}, u32[]{:S(2)}) copy-start(s32[1,32]{1,0:T(1,128)} %param.17) | copy-start | bytes 388
  14.7 71.2 %copy-start.3 = (bf16[2304,256]{1,0:T(8,128)(2,1)S(1)}, bf16[2304,256]{1,0:T(8,128)(2,1)}, u32[]{:S(2)}) copy-start(bf16[2304,256]{1,0:T(8,128)(2,1)} %w_ref.2) | copy-start | bytes 3538948
  14.7 71.2 %copy-start.4 = (f32[256]{0:T(256)S(1)}, f32[256]{0:T(256)}, u32[]{:S(2)}) copy-start(f32[256]{0:T(256)} %param.14) | copy-start | bytes 3076
  14.8 71.2 %copy-start.5 = (f32[256]{0:T(256)S(1)}, f32[256]{0:T(256)}, u32[]{:S(2)}) copy-start(f32[256]{0:T(256)} %param.15) | copy-start | bytes 3076
  14.8 98.0 %all-to-all-start = ((bf16[32,24,3200]{2,1,0:T(8,128)(2,1)}), bf16[32,24,3200]{2,1,0:T(8,128)(2,1)}, u32[]{:S(2)}, u32[]{:S(2)}) async-start(bf16[32,24,3200]{2,1,0:T(8,128)(2,1)} %send_order.1), calls=%async_computation | async-start | bytes 9830400 | tf_op jit(solution)/shard_map/all_to_all | solution.py:317
  25.4 10.6 %collective-permute-start = (bf16[1,128,256]{2,1,0:T(8,128)(2,1)S(1)}, bf16[1,128,256]{2,1,0:T(8,128)(2,1)S(1)}, u32[]{:S(2)}, u32[]{:S(2)}) collective-permute-start(bf16[1,128,256]{2,1,0:T(8,128)(2,1)S(1)} %get-tuple-element.9), channel_id=1, source_target_pairs={{0,32},{32,64},{64,96},{1,33},{33,65},{65,97},{2,34},{34,66},{66,9... | collective-permute-start | bytes 196616 | tf_op jit(solution)/shard_map/ppermute | solution.py:322
  28.6 7.5 %collective-permute-start.1 = (bf16[1,128,256]{2,1,0:T(8,128)(2,1)S(1)}, bf16[1,128,256]{2,1,0:T(8,128)(2,1)S(1)}, u32[]{:S(2)}, u32[]{:S(2)}) collective-permute-start(bf16[1,128,256]{2,1,0:T(8,128)(2,1)S(1)} %get-tuple-element.8), channel_id=1, source_target_pairs={{32,0},{64,32},{96,64},{33,1},{65,33},{97,65},{34,2},{66,34},{98,6... | collective-permute-start | bytes 196616 | tf_op jit(solution)/shard_map/ppermute | solution.py:323
  36.1 48.4 %collective-permute-start.3 = (bf16[66,256]{1,0:T(8,128)(2,1)S(1)}, bf16[66,256]{1,0:T(8,128)(2,1)S(1)}, u32[]{:S(2)}, u32[]{:S(2)}) collective-permute-start(bf16[66,256]{1,0:T(8,128)(2,1)S(1)} %pad_maximum_fusion.4), channel_id=1, source_target_pairs={{1,0},{2,1},{3,2},{4,3},{5,4},{6,5},{7,6},{8,7},{9,8},{10,9},{11,1... | collective-permute-start | bytes 101384 | tf_op jit(solution)/shard_map/ppermute | solution.py:330
  38.6 47.3 %collective-permute-start.2 = (bf16[66,256]{1,0:T(8,128)(2,1)S(1)}, bf16[66,256]{1,0:T(8,128)(2,1)S(1)}, u32[]{:S(2)}, u32[]{:S(2)}) collective-permute-start(bf16[66,256]{1,0:T(8,128)(2,1)S(1)} %pad_maximum_fusion.3), channel_id=1, source_target_pairs={{0,1},{1,2},{2,3},{3,4},{4,5},{5,6},{6,7},{7,8},{8,9},{9,10},{10,1... | collective-permute-start | bytes 101384 | tf_op jit(solution)/shard_map/ppermute | solution.py:329
  86.0 2.3 %copy-start.2 = (bf16[64,128,256]{2,1,0:T(8,128)(2,1)S(1)}, bf16[64,128,256]{2,1,0:T(8,128)(2,1)}, u32[]{:S(2)}) copy-start(bf16[64,128,256]{2,1,0:T(8,128)(2,1)} %canvas_ref.1) | copy-start | bytes 12582916
  119.2 50.9 %collective-permute-start.4 = (bf16[192,3200]{1,0:T(8,128)(2,1)}, bf16[192,3200]{1,0:T(8,128)(2,1)S(1)}, u32[]{:S(2)}, u32[]{:S(2)}) collective-permute-start(bf16[192,3200]{1,0:T(8,128)(2,1)} %hold_and_norm.1), channel_id=1, source_target_pairs={{0,1},{1,2},{2,3},{3,4},{4,5},{5,6},{6,7},{7,8},{8,9},{9,10},{10,1... | collective-permute-start | bytes 3686408 | tf_op jit(solution)/shard_map/ppermute | solution.py:353
  123.6 46.5 %collective-permute-start.5 = (bf16[192,3200]{1,0:T(8,128)(2,1)}, bf16[192,3200]{1,0:T(8,128)(2,1)S(1)}, u32[]{:S(2)}, u32[]{:S(2)}) collective-permute-start(bf16[192,3200]{1,0:T(8,128)(2,1)} %hold_and_norm.1), channel_id=1, source_target_pairs={{1,0},{2,1},{3,2},{4,3},{5,4},{6,5},{7,6},{8,7},{9,8},{10,9},{11,1... | collective-permute-start | bytes 3686408 | tf_op jit(solution)/shard_map/ppermute | solution.py:354
  128.2 41.3 %all-to-all-start.1 = ((bf16[32,1,3]{2,1,0:T(2,128)(2,1)}), bf16[32,1,3]{2,1,0:T(2,128)(2,1)S(1)}, u32[]{:S(2)}, u32[]{:S(2)}) async-start(bf16[32,1,3]{2,1,0:T(2,128)(2,1)} %copy.31), calls=%async_computation.1 | async-start | bytes 32768 | tf_op jit(solution)/shard_map/all_to_all | solution.py:341
  173.4 2.0 copy-start.1
Sparse Core Ops, SparseCore 0:
  11.5 156.6 all-gather.1

commit v7 on v6

--- a/solution.py
+++ b/solution.py
@@ -215,22 +215,25 @@
     )(weight)
 
 
-def project_and_attend(near_tokens, bias, packed, sharp):
-    near, width = near_tokens.shape
-    rows = near // 3
+def project_and_attend(before, here, after, bias, packed, sharp):
+    rows, width = here.shape
+    near = 3 * rows
     deep = packed.shape[0]
     eights, parts = width // deep, deep // 8
     spare = -(-3 * HEADS // 8)
     scale = 1.0 / math.sqrt(HD)
 
-    def body(x, bias, w_ref, *refs):
+    def body(xb, xh, xa, bias, w_ref, *refs):
         ext = refs[:spare]
-        sharp_ref, out_ref, wide, lasts, q_buf, k_buf, v_buf = refs[spare:]
+        sharp_ref, out_ref, x, wide, lasts, q_buf, k_buf, v_buf = refs[spare:]
         n = pl.program_id(0)
         head = jnp.minimum(n, HEADS - 1)
 
         @pl.when(n == 0)
         def _():
+            x[0:rows] = xb[...]
+            x[rows : 2 * rows] = xh[...]
+            x[2 * rows :] = xa[...]
             for j in range(spare):
                 wide[j] = ext[j][...].astype(F32)
             for j in range(spare):
@@ -276,11 +279,12 @@
         body,
         grid=(HEADS + 1,),
         out_shape=jax.ShapeDtypeStruct((rows, HW), BF),
-        in_specs=[VMEM, VMEM, pl.BlockSpec((deep, 3 * eights * HD), lambda n: (0, jnp.minimum(n, HEADS - 1)))]
+        in_specs=[VMEM, VMEM, VMEM, VMEM, pl.BlockSpec((deep, 3 * eights * HD), lambda n: (0, jnp.minimum(n, HEADS - 1)))]
         + [ext_spec(j) for j in range(spare)]
         + [VMEM],
         out_specs=pl.BlockSpec((rows, HD), lambda n: (0, jnp.maximum(n - 1, 0))),
         scratch_shapes=[
+            pltpu.VMEM((near, width), BF),
             pltpu.VMEM((spare, deep, 128), F32),
             pltpu.VMEM((8 * spare, parts, HD), BF),
             pltpu.VMEM((2, rows, HD), BF),
@@ -289,7 +293,7 @@
         ],
         compiler_params=pltpu.CompilerParams(vmem_limit_bytes=48 << 20),
         name="project_and_attend",
-    )(near_tokens, bias, *([packed] * (1 + spare)), sharp)
+    )(before, here, after, bias, *([packed] * (1 + spare)), sharp)
 
 
 def shards(
@@ -359,9 +363,8 @@
     near_ids = jnp.where(inside, jnp.take(all_ids, jnp.clip(places, 0, all_ids.shape[0] - 1)), -1)
     key_ids = jnp.repeat(near_ids, tile_len)
     own_ids = key_ids[held_rows : 2 * held_rows]
-    near_tokens = jnp.concatenate([before, here, after], axis=0)
     bias = jnp.where(own_ids[:, None] == key_ids[None, :], 0.0, -1e30)
-    attended = project_and_attend(near_tokens, bias, packed, sharp)
+    attended = project_and_attend(before, here, after, bias, packed, sharp)
     return (score_map, attended)
 
 

time: 213 us -> 209 us (0.981)
  the two profiles are of different devices: /device:TPU:1 before, /device:TPU:97 now
where the time goes in v7:
time: 209 us; the launch traced here: 205 us
  waiting for transfers between devices  77.6 us (37%)
  Pallas kernels  67.1 us (32%)
  starting transfers between devices  30.5 us (15%)
  between operations  14.4 us (7%)
  local copies, waits for them, and re-layouts  11.9 us (6%)
  other arithmetic  3.67 us (2%)
    ppermute x1, waiting for transfers between devices, shards(): right = lax.ppermute(edge(0), 'dev', down)  46.6 us
    pallas_call x1, Pallas kernels, project_and_attend(): pl.pallas_call(body, grid=(HEADS + 1,), out_shape=jax.ShapeDtypeStruct((r...  30.3 us
    all_to_all x1, waiting for transfers between devices, shards(): lax.all_to_all(send_score, 'dev', split_axis=0, concat_axis=0, tiled=True)  30 us
    pallas_call x1, Pallas kernels, conv_scores(): pl.pallas_call(body, grid=(height // step,), out_shape=jax.ShapeDtypeStru...  22.9 us
    all_to_all x1, starting transfers between devices, shards(): recv = lax.all_to_all(sent, 'dev', split_axis=0, concat_axis=0, tiled=True)  7.78 us
    pallas_call x1, Pallas kernels, hold_and_norm(): pl.pallas_call(body, out_shape=jax.ShapeDtypeStruct((rows, width), BF), i...  6.49 us
    all_to_all x1, starting transfers between devices, shards(): lax.all_to_all(send_score, 'dev', split_axis=0, concat_axis=0, tiled=True)  6.32 us
    pallas_call x1, Pallas kernels, send_order(): pl.pallas_call(body, out_shape=jax.ShapeDtypeStruct(tokens.shape, tokens....  5.69 us
  transfers between devices with their start and end apart: 9, of which 3 were waited for; matrix products, arithmetic and copies ran while one was open for 6% of the time, Pallas kernels for 17%

profile of v7, /device:TPU:97, one launch (start us, length us, event | category | flops | bytes accessed | tf_op | source)
XLA Modules:
  0.0 205.3 jit_solution(5212918173086325507)
XLA Ops:
  7.2 0.0 copy-start
  7.2 0.0 all-gather.2.cloned.1.call-start
  7.2 1.7 pack_rows.1
  8.9 0.0 all-gather.2.cloned.1.call-update
  9.0 5.7 %send_order.1 = bf16[32,24,3200]{2,1,0:T(8,128)(2,1)} custom-call(s32[32]{0:T(128)} %bitcast.74, s32[32]{0:T(128)} %bitcast.76, s32[1]{0:T(128)} %bitcast.12.own_ref, bf16[32,24,3200]{2,1,0:T(8,128)(2,1)} %tok_ref.1), custom_call_target="tpu_custom_call" | custom-call | tf_op jit(solution)/shard_map/send_order/pallas_call | solution.py:48
  14.7 0.0 copy-start.7
  14.7 0.0 copy-start.8
  14.7 0.0 copy-start.9
  14.7 0.0 copy-start.6
  14.7 0.0 copy-start.3
  14.7 0.0 copy-start.4
  14.7 0.0 copy-start.5
  14.7 7.8 %all-to-all-start = ((bf16[32,24,3200]{2,1,0:T(8,128)(2,1)}), bf16[32,24,3200]{2,1,0:T(8,128)(2,1)}, u32[]{:S(2)}, u32[]{:S(2)}) async-start(bf16[32,24,3200]{2,1,0:T(8,128)(2,1)} %send_order.1), calls=%async_computation | async-start | bytes 9830400 | tf_op jit(solution)/shard_map/all_to_all | solution.py:321
  22.5 0.9 fusion.8
  23.4 3.1 %collective-permute-start = (bf16[1,128,256]{2,1,0:T(8,128)(2,1)S(1)}, bf16[1,128,256]{2,1,0:T(8,128)(2,1)S(1)}, u32[]{:S(2)}, u32[]{:S(2)}) collective-permute-start(bf16[1,128,256]{2,1,0:T(8,128)(2,1)S(1)} %get-tuple-element.9), channel_id=1, source_target_pairs={{0,32},{32,64},{64,96},{1,33},{33,65},{65,97},{2,34},{34,66},{66,9... | collective-permute-start | bytes 196616 | tf_op jit(solution)/shard_map/ppermute | solution.py:326
  26.6 1.3 collective-permute-start.1
  27.9 1.1 fusion.7
  29.1 0.7 gather_fusion
  29.8 0.1 slice.81
  29.9 0.1 broadcast_in_dim.107
  29.9 0.1 eq.62
  30.0 0.1 broadcast_in_dim.106
  30.1 0.1 eq.60
  30.2 0.6 reshape.191.gain_ref
  30.8 0.6 fusion
  31.4 0.1 select_reduce_fusion
  31.6 0.6 fusion.5
  32.2 0.7 gather_fusion.1
  32.9 0.1 select_reduce_fusion.1
  33.0 0.2 select_reduce_fusion.3
  33.2 0.1 broadcast_add_fusion
  33.3 0.2 convert_reduce_fusion
  33.5 0.5 slice_bitcast_fusion.4.src_ref
  34.0 0.0 collective-permute-done.top_ref
  34.0 0.0 collective-permute-done.1.bottom_ref
  34.1 2.6 %collective-permute-start.3 = (bf16[66,256]{1,0:T(8,128)(2,1)S(1)}, bf16[66,256]{1,0:T(8,128)(2,1)S(1)}, u32[]{:S(2)}, u32[]{:S(2)}) collective-permute-start(bf16[66,256]{1,0:T(8,128)(2,1)S(1)} %pad_maximum_fusion.3), channel_id=1, source_target_pairs={{1,0},{2,1},{3,2},{4,3},{5,4},{6,5},{7,6},{8,7},{9,8},{10,9},{11,1... | collective-permute-start | bytes 101384 | tf_op jit(solution)/shard_map/ppermute | solution.py:334
  36.7 5.1 %collective-permute-start.2 = (bf16[66,256]{1,0:T(8,128)(2,1)S(1)}, bf16[66,256]{1,0:T(8,128)(2,1)S(1)}, u32[]{:S(2)}, u32[]{:S(2)}) collective-permute-start(bf16[66,256]{1,0:T(8,128)(2,1)S(1)} %pad_maximum_fusion.2), channel_id=1, source_target_pairs={{0,1},{1,2},{2,3},{3,4},{4,5},{5,6},{6,7},{7,8},{8,9},{9,10},{10,1... | collective-permute-start | bytes 101384 | tf_op jit(solution)/shard_map/ppermute | solution.py:333
  41.8 46.6 %collective-permute-done.3 = bf16[66,256]{1,0:T(8,128)(2,1)S(1)} collective-permute-done((bf16[66,256]{1,0:T(8,128)(2,1)S(1)}, bf16[66,256]{1,0:T(8,128)(2,1)S(1)}, u32[]{:S(2)}, u32[]{:S(2)}) %collective-permute-start.3) | collective-permute-done | bytes 33824 | tf_op jit(solution)/shard_map/ppermute | solution.py:334
  88.4 0.0 collective-permute-done.2
  88.5 0.0 copy-start.2
  88.5 2.3 %copy-done.2 = bf16[64,128,256]{2,1,0:T(8,128)(2,1)S(1)} copy-done((bf16[64,128,256]{2,1,0:T(8,128)(2,1)S(1)}, bf16[64,128,256]{2,1,0:T(8,128)(2,1)}, u32[]{:S(2)}) %copy-start.2) | copy-done | bytes 4194328
  90.8 22.9 %conv_scores.1 = f32[8,8,128]{2,1,0:T(8,128)} custom-call(bf16[64,128,256]{2,1,0:T(8,128)(2,1)S(1)} %copy-done.2, bf16[1,128,256]{2,1,0:T(8,128)(2,1)S(1)} %collective-permute-done.top_ref, bf16[1,128,256]{2,1,0:T(8,128)(2,1)S(1)} %collective-permute-done.1.bottom_ref, bf16[64,768]{1,0:T(8,128)(2,1)S(1)} %get-tuple-element.24.left_ref, ...), custom_call_target="tpu_custom_call" | custom-call | tf_op jit(solution)/shard_map/conv_scores/pallas_call | solution.py:170
  113.7 1.5 gather_fusion.2
  115.2 0.1 fusion.12
  115.3 0.0 all-to-all-done.recv_ref
  115.3 6.5 %hold_and_norm.1.xh = bf16[192,3200]{1,0:T(8,128)(2,1)} custom-call(s32[8]{0:T(128)} %slice_bitcast_fusion.4.src_ref, bf16[32,24,3200]{2,1,0:T(8,128)(2,1)} %all-to-all-done.recv_ref, f32[1,3200]{1,0:T(1,128)} %reshape.191.gain_ref, s32[25,128]{1,0:T(8,128)} %constant.73.clone.table_ref), custom_call_target="tpu_custom_call" | custom-call | tf_op jit(solution)/shard_map/hold_and_norm/pallas_call | solution.py:99
  121.8 2.1 %collective-permute-start.4 = (bf16[192,3200]{1,0:T(8,128)(2,1)}, bf16[192,3200]{1,0:T(8,128)(2,1)S(1)}, u32[]{:S(2)}, u32[]{:S(2)}) collective-permute-start(bf16[192,3200]{1,0:T(8,128)(2,1)} %hold_and_norm.1.xh), channel_id=1, source_target_pairs={{0,1},{1,2},{2,3},{3,4},{4,5},{5,6},{6,7},{7,8},{8,9},{9,10},{10,1... | collective-permute-start | bytes 3686408 | tf_op jit(solution)/shard_map/ppermute | solution.py:357
  123.9 2.2 %collective-permute-start.5 = (bf16[192,3200]{1,0:T(8,128)(2,1)}, bf16[192,3200]{1,0:T(8,128)(2,1)S(1)}, u32[]{:S(2)}, u32[]{:S(2)}) collective-permute-start(bf16[192,3200]{1,0:T(8,128)(2,1)} %hold_and_norm.1.xh), channel_id=1, source_target_pairs={{1,0},{2,1},{3,2},{4,3},{5,4},{6,5},{7,6},{8,7},{9,8},{10,9},{11,1... | collective-permute-start | bytes 3686408 | tf_op jit(solution)/shard_map/ppermute | solution.py:358
  126.1 0.6 fusion.11
  126.7 0.7 maximum_bitcast_fusion
  127.4 0.6 maximum_bitcast_fusion.1
  128.1 0.7 copy.31
  128.8 6.3 %all-to-all-start.1 = ((bf16[32,1,3]{2,1,0:T(2,128)(2,1)}), bf16[32,1,3]{2,1,0:T(2,128)(2,1)S(1)}, u32[]{:S(2)}, u32[]{:S(2)}) async-start(bf16[32,1,3]{2,1,0:T(2,128)(2,1)} %copy.31), calls=%async_computation.1 | async-start | bytes 32768 | tf_op jit(solution)/shard_map/all_to_all | solution.py:345
  135.1 0.1 compare_select_fusion.bias
  135.2 30.0 %all-to-all-done.1 = bf16[32,1,3]{2,1,0:T(2,128)(2,1)S(1)} async-done(((bf16[32,1,3]{2,1,0:T(2,128)(2,1)}), bf16[32,1,3]{2,1,0:T(2,128)(2,1)S(1)}, u32[]{:S(2)}, u32[]{:S(2)}) %all-to-all-start.1) | async-done | bytes 224 | tf_op jit(solution)/shard_map/all_to_all | solution.py:345
  165.3 0.1 copy.32
  165.4 0.2 select_reduce_fusion.2
  165.5 0.1 reshape.192
  165.6 0.1 broadcast_in_dim.118
  165.7 0.2 broadcast_in_dim_reshape.5.refs_5_
  165.9 0.0 collective-permute-done.4.xb
  165.9 0.9 all-gather.2.cloned.1.call-done.w_ref.refs_0_.refs_1_.refs_2_.refs_3_.refs_4_
  166.8 1.3 copy-done.1
  168.1 30.3 %project_and_attend.1 = bf16[192,1664]{1,0:T(8,128)(2,1)} custom-call(bf16[192,3200]{1,0:T(8,128)(2,1)S(1)} %collective-permute-done.4.xb, bf16[192,3200]{1,0:T(8,128)(2,1)S(1)} %copy-done.1, bf16[192,3200]{1,0:T(8,128)(2,1)S(1)} %collective-permute-done.5.xa, f32[192,576]{1,0:T(8,128)S(1)} %compare_select_fusion.bias, ...), custom_call_target="tpu_custom_call" | custom-call | tf_op jit(solution)/shard_map/project_and_attend/pallas_call | solution.py:278
  (32 shorter events, 0.2 us)
Async XLA Ops:
  7.2 21.9 %copy-start = (s32[1,256]{1,0:T(1,128)S(1)}, s32[1,256]{1,0:T(1,128)}, u32[]{:S(2)}) copy-start(s32[1,256]{1,0:T(1,128)} %param.20) | copy-start | bytes 3076
  7.2 159.7 %all-gather.2.cloned.1.call-start = ((), (), s32[]{:S(2)}) async-start(), calls=%async_computation.2 | async-start | bytes 32231424 | tf_op jit(solution)/shard_map/all_gather | solution.py:323
  14.7 15.5 %copy-start.7 = (f32[3200]{0:T(1024)S(1)}, f32[3200]{0:T(1024)}, u32[]{:S(2)}) copy-start(f32[3200]{0:T(1024)} %param.21) | copy-start | bytes 38404
  14.7 16.1 %copy-start.8 = (s32[1,32]{1,0:T(1,128)S(1)}, s32[1,32]{1,0:T(1,128)}, u32[]{:S(2)}) copy-start(s32[1,32]{1,0:T(1,128)} %param.18) | copy-start | bytes 388
  14.7 16.8 %copy-start.9 = (s32[1,32]{1,0:T(1,128)S(1)}, s32[1,32]{1,0:T(1,128)}, u32[]{:S(2)}) copy-start(s32[1,32]{1,0:T(1,128)} %param.19) | copy-start | bytes 388
  14.7 17.5 %copy-start.6 = (s32[1,32]{1,0:T(1,128)S(1)}, s32[1,32]{1,0:T(1,128)}, u32[]{:S(2)}) copy-start(s32[1,32]{1,0:T(1,128)} %param.17) | copy-start | bytes 388
  14.7 73.8 %copy-start.3 = (bf16[2304,256]{1,0:T(8,128)(2,1)S(1)}, bf16[2304,256]{1,0:T(8,128)(2,1)}, u32[]{:S(2)}) copy-start(bf16[2304,256]{1,0:T(8,128)(2,1)} %w_ref.2) | copy-start | bytes 3538948
  14.7 73.8 %copy-start.4 = (f32[256]{0:T(256)S(1)}, f32[256]{0:T(256)}, u32[]{:S(2)}) copy-start(f32[256]{0:T(256)} %param.14) | copy-start | bytes 3076
  14.7 73.8 %copy-start.5 = (f32[256]{0:T(256)S(1)}, f32[256]{0:T(256)}, u32[]{:S(2)}) copy-start(f32[256]{0:T(256)} %param.15) | copy-start | bytes 3076
  14.7 100.5 %all-to-all-start = ((bf16[32,24,3200]{2,1,0:T(8,128)(2,1)}), bf16[32,24,3200]{2,1,0:T(8,128)(2,1)}, u32[]{:S(2)}, u32[]{:S(2)}) async-start(bf16[32,24,3200]{2,1,0:T(8,128)(2,1)} %send_order.1), calls=%async_computation | async-start | bytes 9830400 | tf_op jit(solution)/shard_map/all_to_all | solution.py:321
  23.4 10.6 %collective-permute-start = (bf16[1,128,256]{2,1,0:T(8,128)(2,1)S(1)}, bf16[1,128,256]{2,1,0:T(8,128)(2,1)S(1)}, u32[]{:S(2)}, u32[]{:S(2)}) collective-permute-start(bf16[1,128,256]{2,1,0:T(8,128)(2,1)S(1)} %get-tuple-element.9), channel_id=1, source_target_pairs={{0,32},{32,64},{64,96},{1,33},{33,65},{65,97},{2,34},{34,66},{66,9... | collective-permute-start | bytes 196616 | tf_op jit(solution)/shard_map/ppermute | solution.py:326
  26.6 7.5 %collective-permute-start.1 = (bf16[1,128,256]{2,1,0:T(8,128)(2,1)S(1)}, bf16[1,128,256]{2,1,0:T(8,128)(2,1)S(1)}, u32[]{:S(2)}, u32[]{:S(2)}) collective-permute-start(bf16[1,128,256]{2,1,0:T(8,128)(2,1)S(1)} %get-tuple-element.8), channel_id=1, source_target_pairs={{32,0},{64,32},{96,64},{33,1},{65,33},{97,65},{34,2},{66,34},{98,6... | collective-permute-start | bytes 196616 | tf_op jit(solution)/shard_map/ppermute | solution.py:327
  34.1 54.3 %collective-permute-start.3 = (bf16[66,256]{1,0:T(8,128)(2,1)S(1)}, bf16[66,256]{1,0:T(8,128)(2,1)S(1)}, u32[]{:S(2)}, u32[]{:S(2)}) collective-permute-start(bf16[66,256]{1,0:T(8,128)(2,1)S(1)} %pad_maximum_fusion.3), channel_id=1, source_target_pairs={{1,0},{2,1},{3,2},{4,3},{5,4},{6,5},{7,6},{8,7},{9,8},{10,9},{11,1... | collective-permute-start | bytes 101384 | tf_op jit(solution)/shard_map/ppermute | solution.py:334
  36.7 51.7 %collective-permute-start.2 = (bf16[66,256]{1,0:T(8,128)(2,1)S(1)}, bf16[66,256]{1,0:T(8,128)(2,1)S(1)}, u32[]{:S(2)}, u32[]{:S(2)}) collective-permute-start(bf16[66,256]{1,0:T(8,128)(2,1)S(1)} %pad_maximum_fusion.2), channel_id=1, source_target_pairs={{0,1},{1,2},{2,3},{3,4},{4,5},{5,6},{6,7},{7,8},{8,9},{9,10},{10,1... | collective-permute-start | bytes 101384 | tf_op jit(solution)/shard_map/ppermute | solution.py:333
  88.5 2.3 %copy-start.2 = (bf16[64,128,256]{2,1,0:T(8,128)(2,1)S(1)}, bf16[64,128,256]{2,1,0:T(8,128)(2,1)}, u32[]{:S(2)}) copy-start(bf16[64,128,256]{2,1,0:T(8,128)(2,1)} %canvas_ref.1) | copy-start | bytes 12582916
  121.8 44.1 %collective-permute-start.4 = (bf16[192,3200]{1,0:T(8,128)(2,1)}, bf16[192,3200]{1,0:T(8,128)(2,1)S(1)}, u32[]{:S(2)}, u32[]{:S(2)}) collective-permute-start(bf16[192,3200]{1,0:T(8,128)(2,1)} %hold_and_norm.1.xh), channel_id=1, source_target_pairs={{0,1},{1,2},{2,3},{3,4},{4,5},{5,6},{6,7},{7,8},{8,9},{9,10},{10,1... | collective-permute-start | bytes 3686408 | tf_op jit(solution)/shard_map/ppermute | solution.py:357
  123.9 42.0 %collective-permute-start.5 = (bf16[192,3200]{1,0:T(8,128)(2,1)}, bf16[192,3200]{1,0:T(8,128)(2,1)S(1)}, u32[]{:S(2)}, u32[]{:S(2)}) collective-permute-start(bf16[192,3200]{1,0:T(8,128)(2,1)} %hold_and_norm.1.xh), channel_id=1, source_target_pairs={{1,0},{2,1},{3,2},{4,3},{5,4},{6,5},{7,6},{8,7},{9,8},{10,9},{11,1... | collective-permute-start | bytes 3686408 | tf_op jit(solution)/shard_map/ppermute | solution.py:358
  128.8 36.5 %all-to-all-start.1 = ((bf16[32,1,3]{2,1,0:T(2,128)(2,1)}), bf16[32,1,3]{2,1,0:T(2,128)(2,1)S(1)}, u32[]{:S(2)}, u32[]{:S(2)}) async-start(bf16[32,1,3]{2,1,0:T(2,128)(2,1)} %copy.31), calls=%async_computation.1 | async-start | bytes 32768 | tf_op jit(solution)/shard_map/all_to_all | solution.py:345
  166.8 1.3 copy-start.1
Sparse Core Ops, SparseCore 0:
  11.5 155.2 all-gather.1
